TPU v7x, 32 devices: a whole 2x2x4 slice. The times are simulated.
32 devices in a mesh: snap: 8 (over z, core), space: 4 (over y, x).
Axes of the slice: x: 2, y: 2, z: 4, core: 2. Of those that a mesh axis runs over, the one named last changes fastest.
Arguments:
- snapshots: bfloat16 [16384, 1024], P('space', 'snap'), may hold values from -36 to 36
Outputs:
- gram_band: float32 [1024, 640], P(('snap', 'space'))
- mean_field: float32 [16384], P('space')
All inputs are finite; a program needn't handle non-finite values.
Results may differ from a plain program's by a relative error of at most 0.00036.
Values may be sent and summed in bfloat16 or wider, within the bound.
No kernel may reach another device: no remote copies, remote signals or barrier semaphores. Data moves between devices by JAX's collectives and lax.ppermute only.
A program may use at most 64 MiB of HBM per device.

v0:
```python
import jax
import jax.numpy as jnp
from jax import lax
from jax.sharding import PartitionSpec as P


def passed_along(x, axis, by):
    count = lax.axis_size(axis)
    return lax.ppermute(x, axis, [(i, (i + by) % count) for i in range(count)])


def cross_tiles(left_block, right_block):
    return lax.dot_general(
        left_block, right_block, (((0,), (0,)), ((), ())), preferred_element_type=jnp.float32
    )


def per_device(snapshots):
    snap_count = lax.axis_size("snap")
    space_count = lax.axis_size("space")
    row_count, block_width = snapshots.shape
    totals = jnp.sum(snapshots.astype(jnp.float32), axis=1)
    mean_field = lax.psum(totals, "snap") / (block_width * snap_count)
    fluctuation = (snapshots.astype(jnp.float32) - mean_field[:, None]).astype(jnp.bfloat16)
    half_count = snap_count // 2
    pieces = [cross_tiles(fluctuation, fluctuation)]

    def advance(current, ignored):
        current = passed_along(current, "snap", -1)
        return (current, cross_tiles(fluctuation, current))

    ignored, tile_stack = lax.scan(advance, fluctuation, None, length=half_count)
    kept_rows = tile_stack.shape[1]
    pieces.append(jnp.transpose(tile_stack, (1, 0, 2)).reshape(kept_rows, half_count * block_width))
    gram_band = jnp.concatenate(pieces, axis=1)
    gram_band = lax.psum_scatter(gram_band, "space", scatter_dimension=0, tiled=True)
    return (gram_band * (1.0 / (row_count * space_count)), mean_field)


def solution(mesh):
    return jax.shard_map(
        per_device,
        mesh=mesh,
        in_specs=(P("space", "snap"),),
        out_specs=(P(("snap", "space"), None), P("space")),
        check_vma=False,
    )
```

profile of v0, /device:TPU:0, one launch (start us, length us, event | category | flops | bytes accessed | tf_op | source)
XLA Modules:
  0.0 138.7 jit_solution(4167629784102174336)
XLA Ops:
  7.2 0.0 copy-start
  7.2 0.0 reduce-scatter.2.cloned.1.call-start
  7.2 1.7 %convert_reduce_fusion = f32[4096]{0:T(1024)S(1)} fusion(bf16[4096,128]{1,0:T(8,128)(2,1)} %param.3), kind=kLoop, calls=%fused_computation.3 | loop fusion | flops 1044480 | bytes 1064960 | tf_op jit(solution)/shard_map/reduce_sum | solution.py:22
  8.9 30.4 %psum.7 = f32[4096]{0:T(1024)S(1)} all-reduce(f32[4096]{0:T(1024)S(1)} %convert_reduce_fusion), channel_id=1, replica_groups=mesh['snap'=8,'space'=4] {'snap'}, use_global_device_ids=true, to_apply=%region_1.0 | all-reduce | flops 4096 | bytes 32768 | tf_op jit(solution)/shard_map/psum | solution.py:23
  39.3 0.0 copy-done
  39.3 0.0 copy-start.1
  39.3 0.7 fusion.1
  40.0 0.0 copy-done.1
  40.0 0.1 copy.10
  40.1 0.5 fusion.2
  40.6 62.9 %while.12 = (s32[]{:T(128)}, bf16[4096,128]{1,0:T(8,128)(2,1)S(1)}, f32[4,128,128]{2,1,0:T(8,128)S(1)}, bf16[4096,128]{1,0:T(8,128)(2,1)S(1)}, s32[]{:T(128)}) while((s32[]{:T(128)}, bf16[4096,128]{1,0:T(8,128)(2,1)S(1)}, f32[4,128,128]{2,1,0:T(8,128)S(1)}, bf16[4096,128]{1,0:T(8,128)(2,1)S(1)}, s32[]{:T(128)}) %tuple.22), condition=%wide.region_3.4_spmd, body=%wide.region_2.3_spmd.sunk | while | flops 134217728 | bytes 8454257 | solution.py:32
  40.6 0.1 collective-permute-start
  40.6 12.3 %collective-permute-done = bf16[4096,128]{1,0:T(8,128)(2,1)S(1)} collective-permute-done((bf16[4096,128]{1,0:T(8,128)(2,1)S(1)}, bf16[4096,128]{1,0:T(8,128)(2,1)S(1)}, u32[]{:S(2)}, u32[]{:S(2)}) %collective-permute-start) | collective-permute-done | bytes 1048608 | tf_op jit(solution)/shard_map/while/body/eval_jaxpr/ppermute | solution.py:9
  53.0 0.1 copy.16
  53.0 0.5 fusion.13
  53.5 3.8 %collective-permute-start = (bf16[4096,128]{1,0:T(8,128)(2,1)S(1)}, bf16[4096,128]{1,0:T(8,128)(2,1)S(1)}, u32[]{:S(2)}, u32[]{:S(2)}) collective-permute-start(bf16[4096,128]{1,0:T(8,128)(2,1)S(1)} %get-tuple-element.64), channel_id=1, source_target_pairs={{0,28},{4,0},{8,4},{12,8},{16,12},{20,16},{24,20},{28,24},{1,29},{... | collective-permute-start | bytes 3145736 | tf_op jit(solution)/shard_map/while/body/eval_jaxpr/ppermute | solution.py:9
  57.3 12.3 %collective-permute-done = bf16[4096,128]{1,0:T(8,128)(2,1)S(1)} collective-permute-done((bf16[4096,128]{1,0:T(8,128)(2,1)S(1)}, bf16[4096,128]{1,0:T(8,128)(2,1)S(1)}, u32[]{:S(2)}, u32[]{:S(2)}) %collective-permute-start) | collective-permute-done | bytes 1048608 | tf_op jit(solution)/shard_map/while/body/eval_jaxpr/ppermute | solution.py:9
  69.6 0.1 copy.16
  69.7 0.5 fusion.13
  70.2 3.8 %collective-permute-start = (bf16[4096,128]{1,0:T(8,128)(2,1)S(1)}, bf16[4096,128]{1,0:T(8,128)(2,1)S(1)}, u32[]{:S(2)}, u32[]{:S(2)}) collective-permute-start(bf16[4096,128]{1,0:T(8,128)(2,1)S(1)} %get-tuple-element.64), channel_id=1, source_target_pairs={{0,28},{4,0},{8,4},{12,8},{16,12},{20,16},{24,20},{28,24},{1,29},{... | collective-permute-start | bytes 3145736 | tf_op jit(solution)/shard_map/while/body/eval_jaxpr/ppermute | solution.py:9
  73.9 12.3 %collective-permute-done = bf16[4096,128]{1,0:T(8,128)(2,1)S(1)} collective-permute-done((bf16[4096,128]{1,0:T(8,128)(2,1)S(1)}, bf16[4096,128]{1,0:T(8,128)(2,1)S(1)}, u32[]{:S(2)}, u32[]{:S(2)}) %collective-permute-start) | collective-permute-done | bytes 1048608 | tf_op jit(solution)/shard_map/while/body/eval_jaxpr/ppermute | solution.py:9
  86.2 0.1 copy.16
  86.3 0.5 fusion.13
  86.8 3.8 %collective-permute-start = (bf16[4096,128]{1,0:T(8,128)(2,1)S(1)}, bf16[4096,128]{1,0:T(8,128)(2,1)S(1)}, u32[]{:S(2)}, u32[]{:S(2)}) collective-permute-start(bf16[4096,128]{1,0:T(8,128)(2,1)S(1)} %get-tuple-element.64), channel_id=1, source_target_pairs={{0,28},{4,0},{8,4},{12,8},{16,12},{20,16},{24,20},{28,24},{1,29},{... | collective-permute-start | bytes 3145736 | tf_op jit(solution)/shard_map/while/body/eval_jaxpr/ppermute | solution.py:9
  90.6 12.3 %collective-permute-done = bf16[4096,128]{1,0:T(8,128)(2,1)S(1)} collective-permute-done((bf16[4096,128]{1,0:T(8,128)(2,1)S(1)}, bf16[4096,128]{1,0:T(8,128)(2,1)S(1)}, u32[]{:S(2)}, u32[]{:S(2)}) %collective-permute-start) | collective-permute-done | bytes 1048608 | tf_op jit(solution)/shard_map/while/body/eval_jaxpr/ppermute | solution.py:9
  102.9 0.1 copy.16
  103.0 0.5 fusion.13
  103.5 0.7 pad_maximum_fusion
  104.2 0.0 reduce-scatter.2.cloned.1.call-update
  104.2 26.1 %reduce-scatter.2.cloned.1.call-done = f32[32,640]{1,0:T(8,128)} async-done(((f32[128,640]{1,0:T(8,128)}), f32[32,640]{1,0:T(8,128)}) %reduce-scatter.2.cloned.1.call-update) | async-done | bytes 81936 | tf_op jit(solution)/shard_map/reduce_scatter | solution.py:36
  130.3 1.5 %broadcast_multiply_fusion = f32[32,640]{1,0:T(8,128)} fusion(f32[32,640]{1,0:T(8,128)} %reduce-scatter.2.cloned.1.call-done), kind=kLoop, calls=%fused_computation.7 | loop fusion | flops 20480 | bytes 163840 | tf_op jit(solution)/shard_map/mul | solution.py:37
  (3 shorter events, 0.0 us)
Async XLA Ops:
  7.2 32.1 %copy-start = (bf16[4096,128]{1,0:T(8,128)(2,1)S(1)}, bf16[4096,128]{1,0:T(8,128)(2,1)}, u32[]{:S(2)}) copy-start(bf16[4096,128]{1,0:T(8,128)(2,1)} %param.3) | copy-start | bytes 3145732
  7.2 123.1 %reduce-scatter.2.cloned.1.call-start = ((), (), s32[]{:S(2)}) async-start(), calls=%async_computation.1 | async-start | bytes 409600 | tf_op jit(solution)/shard_map/reduce_scatter | solution.py:36
  39.3 0.7 copy-start.1
  40.6 12.4 %collective-permute-start = (bf16[4096,128]{1,0:T(8,128)(2,1)S(1)}, bf16[4096,128]{1,0:T(8,128)(2,1)S(1)}, u32[]{:S(2)}, u32[]{:S(2)}) collective-permute-start(bf16[4096,128]{1,0:T(8,128)(2,1)S(1)} %get-tuple-element.64), channel_id=1, source_target_pairs={{0,28},{4,0},{8,4},{12,8},{16,12},{20,16},{24,20},{28,24},{1,29},{... | collective-permute-start | bytes 3145736 | tf_op jit(solution)/shard_map/while/body/eval_jaxpr/ppermute | solution.py:9
  53.5 16.1 %collective-permute-start = (bf16[4096,128]{1,0:T(8,128)(2,1)S(1)}, bf16[4096,128]{1,0:T(8,128)(2,1)S(1)}, u32[]{:S(2)}, u32[]{:S(2)}) collective-permute-start(bf16[4096,128]{1,0:T(8,128)(2,1)S(1)} %get-tuple-element.64), channel_id=1, source_target_pairs={{0,28},{4,0},{8,4},{12,8},{16,12},{20,16},{24,20},{28,24},{1,29},{... | collective-permute-start | bytes 3145736 | tf_op jit(solution)/shard_map/while/body/eval_jaxpr/ppermute | solution.py:9
  70.2 16.1 %collective-permute-start = (bf16[4096,128]{1,0:T(8,128)(2,1)S(1)}, bf16[4096,128]{1,0:T(8,128)(2,1)S(1)}, u32[]{:S(2)}, u32[]{:S(2)}) collective-permute-start(bf16[4096,128]{1,0:T(8,128)(2,1)S(1)} %get-tuple-element.64), channel_id=1, source_target_pairs={{0,28},{4,0},{8,4},{12,8},{16,12},{20,16},{24,20},{28,24},{1,29},{... | collective-permute-start | bytes 3145736 | tf_op jit(solution)/shard_map/while/body/eval_jaxpr/ppermute | solution.py:9
  86.8 16.1 %collective-permute-start = (bf16[4096,128]{1,0:T(8,128)(2,1)S(1)}, bf16[4096,128]{1,0:T(8,128)(2,1)S(1)}, u32[]{:S(2)}, u32[]{:S(2)}) collective-permute-start(bf16[4096,128]{1,0:T(8,128)(2,1)S(1)} %get-tuple-element.64), channel_id=1, source_target_pairs={{0,28},{4,0},{8,4},{12,8},{16,12},{20,16},{24,20},{28,24},{1,29},{... | collective-permute-start | bytes 3145736 | tf_op jit(solution)/shard_map/while/body/eval_jaxpr/ppermute | solution.py:9
Sparse Core Ops, SparseCore 0:
  104.4 25.8 reduce-scatter.1
where the time goes:
time: 139 us
  waiting for transfers between devices  75.3 us (54%)
  blocking collectives  30.4 us (22%)
  between operations  14.1 us (10%)
  starting transfers between devices  11.4 us (8%)
  other arithmetic  4.63 us (3%)
  matrix products  2.39 us (2%)
    ppermute x4, waiting for transfers between devices, passed_along(): return lax.ppermute(x, axis, [(i, (i + by) % count) for i in range(count)])  49.3 us
    psum x1, blocking collectives, per_device(): mean_field = lax.psum(totals, 'snap') / (block_width * snap_count)  30.4 us
    reduce_scatter x1, waiting for transfers between devices, per_device(): lax.psum_scatter(gram_band, 'space', scatter_dimension=0, tiled=True)  26.1 us
    ppermute x4, starting transfers between devices, passed_along(): return lax.ppermute(x, axis, [(i, (i + by) % count) for i in range(count)])  11.3 us
  transfers between devices with their start and end apart: 5, of which 5 were waited for; matrix products, arithmetic and copies ran while one was open for 0% of the time, Pallas kernels for 0%

commit v1 on v0

v1 whole, which is shorter than its diff:
```python
import functools

import jax
import jax.numpy as jnp
import numpy as np
from jax import lax
from jax.experimental import pallas as pl
from jax.experimental.pallas import tpu as pltpu
from jax.sharding import PartitionSpec as P


LANES = 128


def bits_of(count):
    return [1 << n for n in range(count.bit_length() - 1)]


def part_masks(space_count, core):
    bits = bits_of(space_count)
    taken = [bits[(step + core) % len(bits)] for step in range(len(bits))]
    masks = []
    for position in range(space_count):
        mask = 0
        for step, bit in enumerate(taken):
            if position >> (len(bits) - 1 - step) & 1:
                mask |= bit
        masks.append(mask)
    return masks


def tile_tables(snap_count, late):
    early_rows, late_rows = [], []
    for me in range(snap_count):
        parts = ([], [])
        for offset in range(snap_count // 2):
            block = ((me // 2) ^ offset) * 2 + me % 2
            for k in range(snap_count // 2 + 1):
                other = (((block + k) % snap_count) ^ me) // 2
                parts[int(late in (offset, other))].append((offset, k))
        early_rows.append(parts[0])
        late_rows.append(parts[1])

    def even(rows):
        longest = max(len(row) for row in rows)
        return np.array([row + [row[-1]] * (longest - len(row)) for row in rows], np.int32)

    return even(early_rows), even(late_rows)


def place_tiles(sizes, place_ref, table_ref, tiles_ref, keep_ref, send_ref):
    space_count, part_rows = sizes
    space, core = place_ref[1], place_ref[0] % 2
    masks = [part_masks(space_count, c) for c in (0, 1)]
    half = space_count // 2

    def one(slot, carry):
        offset, k = table_ref[0, slot], table_ref[1, slot]
        lanes = pl.ds(pl.multiple_of(k * LANES, LANES), LANES)
        for position in range(space_count):
            part = space ^ jnp.where(core == 0, masks[0][position], masks[1][position])
            rows = pl.ds(pl.multiple_of(part * part_rows, part_rows), part_rows)
            target = keep_ref if position < half else send_ref
            target[position % half, slot] = tiles_ref[offset, rows, lanes]
        return carry

    lax.fori_loop(0, table_ref.shape[1], one, 0)


def fluctuations(totals_ref, first_row, total_columns, tile):
    row = pl.ds(first_row // LANES + tile, 1)
    mean = totals_ref[row, :] * (1.0 / total_columns)
    return jnp.transpose(jnp.broadcast_to(mean, (LANES, LANES)))


def early_kernel(sizes, early, place_ref, table_ref, totals_ref, *refs):
    snap_count, space_count, rows, width = sizes
    blocks = refs[: 2 * len(early)]
    fluct_ref, keep_ref, send_ref, tiles_ref = refs[2 * len(early) :]
    me = place_ref[0]
    first_row = place_ref[2]
    band = snap_count // 2 + 1

    def one_tile(tile, carry):
        mean = fluctuations(totals_ref, first_row, width * snap_count, tile)
        target = pl.ds(pl.multiple_of(tile * LANES, LANES), LANES)
        for n, offset in enumerate(early):
            for other in (0, 1):
                ref = blocks[2 * n + other]
                base = first_row if offset == 0 else 0
                source = pl.ds(pl.multiple_of(base + tile * LANES, LANES), LANES)
                value = (ref[source, :].astype(jnp.float32) - mean).astype(jnp.bfloat16)
                slot = me ^ (2 * offset + other)
                fluct_ref[target, pl.ds(pl.multiple_of(slot * width, width), width)] = value

                @pl.when(slot < band - 1)
                def _():
                    again = pl.multiple_of((slot + snap_count) * width, width)
                    fluct_ref[target, pl.ds(again, width)] = value

        return carry

    lax.fori_loop(0, rows // LANES, one_tile, 0)
    for offset in early:
        block = ((me // 2) ^ offset) * 2 + me % 2
        first = pl.multiple_of(block * width, width)
        tiles_ref[offset] = lax.dot_general(
            fluct_ref[:, pl.ds(first, width)],
            fluct_ref[:, pl.ds(first, band * width)],
            (((0,), (0,)), ((), ())),
            preferred_element_type=jnp.float32,
        )
    place_tiles((space_count, width // space_count), place_ref, table_ref, tiles_ref, keep_ref, send_ref)


def late_kernel(sizes, late, place_ref, table_ref, totals_ref, same_ref, other_ref, early_ref, *refs):
    snap_count, space_count, rows, width = sizes
    keep_ref, send_ref, fluct_ref, tiles_ref = refs
    me = place_ref[0]
    first_row = place_ref[2]
    band = snap_count // 2 + 1
    core = me % 2

    def one_tile(tile, carry):
        mean = fluctuations(totals_ref, first_row, width * snap_count, tile)
        target = pl.ds(pl.multiple_of(tile * LANES, LANES), LANES)
        for ref, column in ((same_ref, core), (other_ref, 1 - core)):
            value = (ref[target, :].astype(jnp.float32) - mean).astype(jnp.bfloat16)
            fluct_ref[target, pl.ds(pl.multiple_of(column * width, width), width)] = value
        return carry

    lax.fori_loop(0, rows // LANES, one_tile, 0)

    def product(left, right):
        return lax.dot_general(left, right, (((0,), (0,)), ((), ())), preferred_element_type=jnp.float32)

    late_first = ((me // 2) ^ late) * 2
    for offset in range(snap_count // 2):
        block = ((me // 2) ^ offset) * 2 + core
        first = pl.multiple_of(block * width, width)
        if offset == late:
            left = fluct_ref[:, pl.ds(pl.multiple_of(core * width, width), width)]
            tiles_ref[offset] = product(left, early_ref[:, pl.ds(first, band * width)])
        else:
            left = early_ref[:, pl.ds(first, width)]
        pair = product(left, fluct_ref[...])
        for n in (0, 1):
            k = (late_first + n - block + snap_count) % snap_count

            @pl.when(k < band)
            def _():
                lanes = pl.ds(pl.multiple_of(k * width, width), width)
                tiles_ref[offset, :, lanes] = pair[:, n * width : (n + 1) * width]

    place_tiles((space_count, width // space_count), place_ref, table_ref, tiles_ref, keep_ref, send_ref)


def joined_kernel(width, early_table, late_table, *refs):
    first_keep, first_recv, second_keep, second_recv, out_ref = refs
    for table, keep, recv in ((early_table, first_keep, first_recv), (late_table, second_keep, second_recv)):

        def one(slot, carry, table=table, keep=keep, recv=recv):
            offset, k = table[0, slot], table[1, slot]
            lanes = pl.ds(pl.multiple_of(k * width, width), width)
            out_ref[offset, :, lanes] = keep[0, slot] + recv[0, slot]
            return carry

        lax.fori_loop(0, table.shape[1], one, 0)


def per_device(snapshots):
    snap_count = lax.axis_size("snap")
    space_count = lax.axis_size("space")
    row_count, width = snapshots.shape
    me, space = lax.axis_index("snap"), lax.axis_index("space")
    chip_count = snap_count // 2
    first_chip, hub_chips = chip_count // 4, chip_count // 2
    hubs = list(range(2 * first_chip, 2 * (first_chip + hub_chips)))
    rows = row_count // hub_chips
    band = chip_count + 1
    part_rows = width // space_count
    late = chip_count // 2
    early = [offset for offset in range(chip_count) if offset != late]

    def hub_rows(device):
        return jnp.clip(device // 2 - first_chip, 0, hub_chips - 1) * rows

    def to_hubs(offset):
        piece = lax.dynamic_slice_in_dim(snapshots, hub_rows(me ^ (2 * offset)), rows, 0)
        return lax.ppermute(piece, "snap", [(h ^ (2 * offset), h) for h in hubs])

    def to_other_core(x):
        return lax.ppermute(x, "snap", [(h, h ^ 1) for h in hubs])

    received = {offset: to_hubs(offset) for offset in early[1:] + [late]}
    mate = lax.ppermute(snapshots, "snap", [(i, i ^ 1) for i in range(snap_count)])

    totals = jnp.sum(snapshots.astype(jnp.float32), axis=1)
    for bit in bits_of(snap_count):
        there = lax.ppermute(totals, "snap", [(i, i ^ bit) for i in range(snap_count)])
        totals = totals + there
    mean_field = totals * (1.0 / (width * snap_count))
    lane_totals = totals.reshape(row_count // LANES, LANES)

    passed = {offset: to_other_core(received[offset]) for offset in received}

    place = jnp.stack([me, space, hub_rows(me)]).astype(jnp.int32)
    early_all, late_all = tile_tables(snap_count, late)
    early_table = lax.dynamic_index_in_dim(jnp.asarray(early_all.transpose(0, 2, 1)), me, 0, False)
    late_table = lax.dynamic_index_in_dim(jnp.asarray(late_all.transpose(0, 2, 1)), me, 0, False)
    smem = pl.BlockSpec(memory_space=pltpu.SMEM)
    vmem = pl.BlockSpec(memory_space=pltpu.VMEM)
    sizes = (snap_count, space_count, rows, width)
    columns = (snap_count + band - 1) * width
    product = 2 * width * width * rows

    def halves(slots):
        shape = jax.ShapeDtypeStruct((space_count // 2, slots, part_rows, width), jnp.float32)
        return [shape, shape]

    def grant(*shapes):
        total = sum(int(np.prod(s.shape)) * jnp.dtype(s.dtype).itemsize for s in shapes)
        return total + (8 << 20)

    tiles = jax.ShapeDtypeStruct((chip_count, width, band * width), jnp.float32)
    operands = [snapshots, mate]
    for offset in early[1:]:
        operands += [received[offset], passed[offset]]
    early_out = [jax.ShapeDtypeStruct((rows, columns), jnp.bfloat16)] + halves(early_all.shape[1])
    fluct, first_keep, first_send = pl.pallas_call(
        functools.partial(early_kernel, sizes, early),
        out_shape=early_out,
        in_specs=[smem, smem, vmem] + [vmem] * len(operands),
        out_specs=[vmem] * 3,
        scratch_shapes=[pltpu.VMEM(tiles.shape, jnp.float32)],
        cost_estimate=pl.CostEstimate(flops=product * len(early) * band, bytes_accessed=0, transcendentals=0),
        compiler_params=pltpu.CompilerParams(vmem_limit_bytes=grant(tiles, *operands, *early_out)),
        name="early_tiles",
    )(place, early_table, lane_totals, *operands)

    operands = [received[late], passed[late], fluct]
    late_out = halves(late_all.shape[1])
    late_fluct = jax.ShapeDtypeStruct((rows, 2 * width), jnp.bfloat16)
    second_keep, second_send = pl.pallas_call(
        functools.partial(late_kernel, sizes, late),
        out_shape=late_out,
        in_specs=[smem, smem, vmem] + [vmem] * len(operands),
        out_specs=[vmem] * 2,
        scratch_shapes=[pltpu.VMEM(late_fluct.shape, jnp.bfloat16), pltpu.VMEM(tiles.shape, jnp.float32)],
        cost_estimate=pl.CostEstimate(flops=product * (band + snap_count), bytes_accessed=0, transcendentals=0),
        compiler_params=pltpu.CompilerParams(vmem_limit_bytes=grant(tiles, late_fluct, *operands, *late_out)),
        name="late_tiles",
    )(place, late_table, lane_totals, *operands)

    bits = bits_of(space_count)

    def exchanged(x, step):
        pairs = []
        for h in hubs:
            bit = bits[(step + h % 2) % len(bits)]
            pairs += [(h * space_count + s, h * space_count + (s ^ bit)) for s in range(space_count)]
        return lax.ppermute(x, ("snap", "space"), pairs)

    def over_space(keep, send):
        for step in range(len(bits) - 1):
            both = keep + exchanged(send, step)
            half = both.shape[0] // 2
            keep, send = both[:half], both[half:]
        return keep, exchanged(send, len(bits) - 1)

    sums = (*over_space(first_keep, first_send), *over_space(second_keep, second_send))
    summed = pl.pallas_call(
        functools.partial(joined_kernel, width),
        out_shape=jax.ShapeDtypeStruct((chip_count, part_rows, band * width), jnp.float32),
        in_specs=[smem, smem] + [vmem] * 4,
        out_specs=vmem,
        cost_estimate=pl.CostEstimate(flops=1000, bytes_accessed=0, transcendentals=0),
        compiler_params=pltpu.CompilerParams(vmem_limit_bytes=8 << 20),
        name="joined",
    )(early_table, late_table, *sums)

    is_hub = (me >= hubs[0]) & (me <= hubs[-1])
    gram_band = jnp.where(is_hub, summed[0], 0.0)
    for offset in range(1, chip_count):
        gram_band = gram_band + lax.ppermute(summed[offset], "snap", [(h, h ^ (2 * offset)) for h in hubs])
    return gram_band * (1.0 / (row_count * space_count)), mean_field


def solution(mesh):
    return jax.shard_map(
        per_device,
        mesh=mesh,
        in_specs=(P("space", "snap"),),
        out_specs=(P(("snap", "space"), None), P("space")),
        check_vma=False,
    )
```

time: 139 us -> 91 us (0.65)
  waiting for transfers between devices: 75.3 us -> 34.1 us
  blocking collectives: 30.4 us -> 0 us
  starting transfers between devices: 11.4 us -> 36.3 us
  between operations: 14.1 us -> 0.97 us
  Pallas kernels: 0 us -> 11.1 us
  local copies, waits for them, and re-layouts: 0.37 us -> 4.92 us
  matrix products: 2.39 us -> 0 us
  other arithmetic: 4.63 us -> 3.03 us
    psum x1 -> x0, blocking collectives: 30.4 us -> none  [per_device(): mean_field = lax.psum(totals, 'snap') / (block_width * snap_count)]
    reduce_scatter x1 -> x0, waiting for transfers between devices: 26.1 us -> none  [per_device(): lax.psum_scatter(gram_band, 'space', scatter_dimension=0, tiled=True)]
    ppermute x4 -> x17, starting transfers between devices: 11.3 us -> 36.3 us  [the longest x3 17.8 us: per_device(): lax.ppermute(totals, 'snap', [(i, i ^ bit) for i in range(snap_count)])]
    ppermute x4 -> x17, waiting for transfers between devices: 49.3 us -> 34.1 us  [the longest x3 24.2 us: per_device(): lax.ppermute(summed[offset], 'snap', [(h, h ^ 2 * offset) for h in hubs])]
    pallas_call x0 -> x3, Pallas kernels: none -> 11.1 us  [the longest x1 5.2 us: per_device(): pl.pallas_call(functools.partial(late_kernel, sizes, late), out_shape=lat...]
    dot_general x5 -> x0, matrix products: 2.39 us -> none  [cross_tiles(): lax.dot_general(left_block, right_block, (((0,), (0,)), ((), ())), prefer...]
    dynamic_slice x0 -> x1, local copies, waits for them, and re-layouts: none -> 2.27 us  [to_hubs(): lax.dynamic_slice_in_dim(snapshots, hub_rows(me ^ 2 * offset), rows, 0)]
  transfers between devices with their start and end apart: 5 -> 17, of which waited for: 5 -> 6; matrix products, arithmetic and copies ran while one was open for 0% -> 4% of each run, Pallas kernels for 0% -> 11%
where the time goes in v1:
time: 91 us; the launch traced here: 90.4 us
  starting transfers between devices  36.3 us (40%)
  waiting for transfers between devices  34.1 us (37%)
  Pallas kernels  11.1 us (12%)
  local copies, waits for them, and re-layouts  4.92 us (5%)
  other arithmetic  3.03 us (3%)
  between operations  0.97 us (1%)
    ppermute x3, waiting for transfers between devices, per_device(): lax.ppermute(summed[offset], 'snap', [(h, h ^ 2 * offset) for h in hubs])  24.2 us
    ppermute x3, starting transfers between devices, per_device(): lax.ppermute(totals, 'snap', [(i, i ^ bit) for i in range(snap_count)])  17.8 us
    ppermute x3, starting transfers between devices, to_hubs(): return lax.ppermute(piece, 'snap', [(h ^ 2 * offset, h) for h in hubs])  10.4 us
    ppermute x3, waiting for transfers between devices, to_hubs(): return lax.ppermute(piece, 'snap', [(h ^ 2 * offset, h) for h in hubs])  6.73 us
    pallas_call x1, Pallas kernels, per_device(): pl.pallas_call(functools.partial(late_kernel, sizes, late), out_shape=lat...  5.2 us
    pallas_call x1, Pallas kernels, per_device(): pl.pallas_call(functools.partial(early_kernel, sizes, early), out_shape=e...  5.1 us
    ppermute x3, starting transfers between devices, per_device(): lax.ppermute(summed[offset], 'snap', [(h, h ^ 2 * offset) for h in hubs])  3.25 us
    ppermute x3, waiting for transfers between devices, per_device(): lax.ppermute(totals, 'snap', [(i, i ^ bit) for i in range(snap_count)])  3.15 us
  transfers between devices with their start and end apart: 17, of which 6 were waited for; matrix products, arithmetic and copies ran while one was open for 4% of the time, Pallas kernels for 11%

profile of v1, /device:TPU:0, one launch (start us, length us, event | category | flops | bytes accessed | tf_op | source)
XLA Modules:
  0.0 90.4 jit_solution(12437093016798704149)
XLA Ops:
  0.7 2.3 %constant_dynamic-slice_fusion = (bf16[2048,128]{1,0:T(8,128)(2,1)}, bf16[2048,128]{1,0:T(8,128)(2,1)S(1)}, bf16[2048,128]{1,0:T(8,128)(2,1)S(1)}) fusion(bf16[4096,128]{1,0:T(8,128)(2,1)} %refs_0_.1, s32[]{:T(128)S(6)} %select_n.48, s32[]{:T(128)S(6)} %select_n.46, s32[]{:T(128)S(6)} %select_n.44), kind=kLoop, calls=%fused_computation.12 | loop fusion | bytes 3145740 | tf_op jit(solution)/shard_map/dynamic_slice | solution.py:189
  3.0 5.0 %collective-permute-start.4 = (bf16[2048,128]{1,0:T(8,128)(2,1)S(1)}, bf16[2048,128]{1,0:T(8,128)(2,1)S(1)}, u32[]{:S(2)}, u32[]{:S(2)}) collective-permute-start(bf16[2048,128]{1,0:T(8,128)(2,1)S(1)} %get-tuple-element.14), channel_id=1, source_target_pairs={{0,8},{4,12},{24,16},{28,20},{1,9},{5,13},{25,17},{29,21},{2,10},{... | collective-permute-start | bytes 1572872 | tf_op jit(solution)/shard_map/ppermute | solution.py:190
  8.0 0.7 collective-permute-start.6
  8.8 4.8 %collective-permute-start.10 = (bf16[2048,128]{1,0:T(8,128)(2,1)}, bf16[2048,128]{1,0:T(8,128)(2,1)}, u32[]{:S(2)}, u32[]{:S(2)}) collective-permute-start(bf16[2048,128]{1,0:T(8,128)(2,1)} %get-tuple-element.12), channel_id=1, source_target_pairs={{24,8},{28,12},{0,16},{4,20},{25,9},{29,13},{1,17},{5,21},{26,10},... | collective-permute-start | bytes 1572872 | tf_op jit(solution)/shard_map/ppermute | solution.py:190
  13.5 6.7 %collective-permute-done.4.refs_2_ = bf16[2048,128]{1,0:T(8,128)(2,1)S(1)} collective-permute-done((bf16[2048,128]{1,0:T(8,128)(2,1)S(1)}, bf16[2048,128]{1,0:T(8,128)(2,1)S(1)}, u32[]{:S(2)}, u32[]{:S(2)}) %collective-permute-start.4) | collective-permute-done | bytes 524320 | tf_op jit(solution)/shard_map/ppermute | solution.py:190
  20.2 0.7 collective-permute-start.5
  20.9 0.7 collective-permute-start.7
  21.6 1.6 %convert_reduce_fusion = f32[4096]{0:T(1024)S(1)} fusion(bf16[4096,128]{1,0:T(8,128)(2,1)} %refs_0_.1), kind=kLoop, calls=%fused_computation | loop fusion | flops 1044480 | bytes 1064960 | tf_op jit(solution)/shard_map/reduce_sum | solution.py:198
  23.3 1.2 %collective-permute-done = f32[4096]{0:T(1024)S(1)} collective-permute-done((f32[4096]{0:T(1024)S(1)}, f32[4096]{0:T(1024)S(1)}, u32[]{:S(2)}, u32[]{:S(2)}) %collective-permute-start) | collective-permute-done | bytes 16416 | tf_op jit(solution)/shard_map/ppermute | solution.py:200
  24.5 14.6 %collective-permute-start.1 = (f32[4096]{0:T(1024)S(1)}, f32[4096]{0:T(1024)S(1)}, u32[]{:S(2)}, u32[]{:S(2)}) collective-permute-start(f32[4096]{0:T(1024)S(1)} %add.48), channel_id=1, source_target_pairs={{0,8},{4,12},{8,0},{12,4},{16,24},{20,28},{24,16},{28,20},{1,9},{5... | collective-permute-start | bytes 49160 | tf_op jit(solution)/shard_map/ppermute | solution.py:200
  39.0 0.7 fusion.5.table_ref.early_table
  39.7 1.0 %collective-permute-done.1 = f32[4096]{0:T(1024)S(1)} collective-permute-done((f32[4096]{0:T(1024)S(1)}, f32[4096]{0:T(1024)S(1)}, u32[]{:S(2)}, u32[]{:S(2)}) %collective-permute-start.1) | collective-permute-done | bytes 16416 | tf_op jit(solution)/shard_map/ppermute | solution.py:200
  40.7 3.1 %collective-permute-start.2 = (f32[4096]{0:T(1024)S(1)}, f32[4096]{0:T(1024)S(1)}, u32[]{:S(2)}, u32[]{:S(2)}) collective-permute-start(f32[4096]{0:T(1024)S(1)} %add.49), channel_id=1, source_target_pairs={{0,16},{4,20},{8,24},{12,28},{16,0},{20,4},{24,8},{28,12},{1,17},{... | collective-permute-start | bytes 49160 | tf_op jit(solution)/shard_map/ppermute | solution.py:200
  43.9 0.7 collective-permute-start.11
  44.6 0.1 pad_add_fusion.place_ref
  44.7 0.9 %collective-permute-done.2 = f32[4096]{0:T(1024)S(1)} collective-permute-done((f32[4096]{0:T(1024)S(1)}, f32[4096]{0:T(1024)S(1)}, u32[]{:S(2)}, u32[]{:S(2)}) %collective-permute-start.2) | collective-permute-done | bytes 16416 | tf_op jit(solution)/shard_map/ppermute | solution.py:200
  45.6 0.6 broadcast_multiply_fusion
  46.2 1.2 %copy-done = bf16[4096,128]{1,0:T(8,128)(2,1)S(1)} copy-done((bf16[4096,128]{1,0:T(8,128)(2,1)S(1)}, bf16[4096,128]{1,0:T(8,128)(2,1)}, u32[]{:S(2)}) %copy-start) | copy-done | bytes 1048600
  47.5 5.1 %early_tiles.1 = (bf16[2048,1536]{1,0:T(8,128)(2,1)S(1)}, f32[2,12,32,128]{3,2,1,0:T(8,128)S(1)}, f32[2,12,32,128]{3,2,1,0:T(8,128)S(1)}) custom-call(s32[3]{0:T(128)S(1)} %pad_add_fusion.place_ref, s32[2,12]{1,0:T(2,128)S(1)} %fusion.5.table_ref.early_table, f32[32,128]{1,0:T(8,128)S(1)} %get-tuple-element.23.totals_ref, bf16[4096,128]{1,0:T(8,128)(2,1)S(1)} %copy-done, ...), custom_call_target="tpu_custom_call" | custom-call | flops 1006632960 | tf_op jit(solution)/shard_map/early_tiles/pallas_call | solution.py:230
  52.6 0.7 collective-permute-start.8
  53.3 0.7 fusion.6.table_ref.late_table
  54.0 5.2 %late_tiles.1 = (f32[2,9,32,128]{3,2,1,0:T(8,128)S(1)}, f32[2,9,32,128]{3,2,1,0:T(8,128)S(1)}) custom-call(s32[3]{0:T(128)S(1)} %pad_add_fusion.place_ref, s32[2,9]{1,0:T(2,128)S(1)} %fusion.6.table_ref.late_table, f32[32,128]{1,0:T(8,128)S(1)} %get-tuple-element.23.totals_ref, bf16[2048,128]{1,0:T(8,128)(2,1)} %collective-permute-done.10.same_ref, ...), custom_call_target="tpu_custom_call" | custom-call | flops 872415232 | tf_op jit(solution)/shard_map/late_tiles/pallas_call | solution.py:244
  59.2 0.7 collective-permute-start.12
  60.0 0.7 collective-permute-start.9
  60.7 0.7 collective-permute-start.13
  61.4 0.8 joined.1
  62.2 1.3 %collective-permute-start.14 = (f32[32,640]{1,0:T(8,128)S(1)}, f32[32,640]{1,0:T(8,128)S(1)}, u32[]{:S(2)}, u32[]{:S(2)}) collective-permute-start(f32[32,640]{1,0:T(8,128)S(1)} %get-tuple-element.17), channel_id=1, source_target_pairs={{8,0},{12,4},{16,24},{20,28},{9,1},{13,5},{17,25},{21,29},{10,2},{... | collective-permute-start | bytes 245768 | tf_op jit(solution)/shard_map/ppermute | solution.py:285
  63.5 1.3 %collective-permute-start.15 = (f32[32,640]{1,0:T(8,128)S(1)}, f32[32,640]{1,0:T(8,128)S(1)}, u32[]{:S(2)}, u32[]{:S(2)}) collective-permute-start(f32[32,640]{1,0:T(8,128)S(1)} %get-tuple-element.19), channel_id=1, source_target_pairs={{8,24},{12,28},{16,0},{20,4},{9,25},{13,29},{17,1},{21,5},{10,26},... | collective-permute-start | bytes 245768 | tf_op jit(solution)/shard_map/ppermute | solution.py:285
  64.8 0.7 collective-permute-start.16
  65.5 21.9 %collective-permute-done.14 = f32[32,640]{1,0:T(8,128)S(1)} collective-permute-done((f32[32,640]{1,0:T(8,128)S(1)}, f32[32,640]{1,0:T(8,128)S(1)}, u32[]{:S(2)}, u32[]{:S(2)}) %collective-permute-start.14) | collective-permute-done | bytes 81952 | tf_op jit(solution)/shard_map/ppermute | solution.py:285
  87.4 2.3 %collective-permute-done.15 = f32[32,640]{1,0:T(8,128)S(1)} collective-permute-done((f32[32,640]{1,0:T(8,128)S(1)}, f32[32,640]{1,0:T(8,128)S(1)}, u32[]{:S(2)}, u32[]{:S(2)}) %collective-permute-start.15) | collective-permute-done | bytes 81952 | tf_op jit(solution)/shard_map/ppermute | solution.py:285
  89.7 0.7 fusion.4
  (21 shorter events, 0.4 us)
Async XLA Ops:
  3.0 17.2 %collective-permute-start.4 = (bf16[2048,128]{1,0:T(8,128)(2,1)S(1)}, bf16[2048,128]{1,0:T(8,128)(2,1)S(1)}, u32[]{:S(2)}, u32[]{:S(2)}) collective-permute-start(bf16[2048,128]{1,0:T(8,128)(2,1)S(1)} %get-tuple-element.14), channel_id=1, source_target_pairs={{0,8},{4,12},{24,16},{28,20},{1,9},{5,13},{25,17},{29,21},{2,10},{... | collective-permute-start | bytes 1572872 | tf_op jit(solution)/shard_map/ppermute | solution.py:190
  8.0 13.0 %collective-permute-start.6 = (bf16[2048,128]{1,0:T(8,128)(2,1)S(1)}, bf16[2048,128]{1,0:T(8,128)(2,1)S(1)}, u32[]{:S(2)}, u32[]{:S(2)}) collective-permute-start(bf16[2048,128]{1,0:T(8,128)(2,1)S(1)} %get-tuple-element.13), channel_id=1, source_target_pairs={{16,8},{20,12},{8,16},{12,20},{17,9},{21,13},{9,17},{13,21},{18,10... | collective-permute-start | bytes 1572872 | tf_op jit(solution)/shard_map/ppermute | solution.py:190
  8.7 37.6 %collective-permute-start.3 = (bf16[4096,128]{1,0:T(8,128)(2,1)}, bf16[4096,128]{1,0:T(8,128)(2,1)S(1)}, u32[]{:S(2)}, u32[]{:S(2)}) collective-permute-start(bf16[4096,128]{1,0:T(8,128)(2,1)} %refs_0_.1), channel_id=1, source_target_pairs={{0,4},{4,0},{8,12},{12,8},{16,20},{20,16},{24,28},{28,24},{1,5},{5... | collective-permute-start | bytes 3145736 | tf_op jit(solution)/shard_map/ppermute | solution.py:196
  8.8 35.1 %collective-permute-start.10 = (bf16[2048,128]{1,0:T(8,128)(2,1)}, bf16[2048,128]{1,0:T(8,128)(2,1)}, u32[]{:S(2)}, u32[]{:S(2)}) collective-permute-start(bf16[2048,128]{1,0:T(8,128)(2,1)} %get-tuple-element.12), channel_id=1, source_target_pairs={{24,8},{28,12},{0,16},{4,20},{25,9},{29,13},{1,17},{5,21},{26,10},... | collective-permute-start | bytes 1572872 | tf_op jit(solution)/shard_map/ppermute | solution.py:190
  20.2 26.0 %collective-permute-start.5 = (bf16[2048,128]{1,0:T(8,128)(2,1)S(1)}, bf16[2048,128]{1,0:T(8,128)(2,1)S(1)}, u32[]{:S(2)}, u32[]{:S(2)}) collective-permute-start(bf16[2048,128]{1,0:T(8,128)(2,1)S(1)} %collective-permute-done.4.refs_2_), channel_id=1, source_target_pairs={{8,12},{12,8},{16,20},{20,16},{9,13},{13,9},{17,21},{21,17},{10,14... | collective-permute-start | bytes 1572872 | tf_op jit(solution)/shard_map/ppermute | solution.py:193
  20.9 25.3 %collective-permute-start.7 = (bf16[2048,128]{1,0:T(8,128)(2,1)S(1)}, bf16[2048,128]{1,0:T(8,128)(2,1)S(1)}, u32[]{:S(2)}, u32[]{:S(2)}) collective-permute-start(bf16[2048,128]{1,0:T(8,128)(2,1)S(1)} %collective-permute-done.6.refs_4_), channel_id=1, source_target_pairs={{8,12},{12,8},{16,20},{20,16},{9,13},{13,9},{17,21},{21,17},{10,14... | collective-permute-start | bytes 1572872 | tf_op jit(solution)/shard_map/ppermute | solution.py:193
  23.2 1.2 %collective-permute-start = (f32[4096]{0:T(1024)S(1)}, f32[4096]{0:T(1024)S(1)}, u32[]{:S(2)}, u32[]{:S(2)}) collective-permute-start(f32[4096]{0:T(1024)S(1)} %convert_reduce_fusion), channel_id=1, source_target_pairs={{0,4},{4,0},{8,12},{12,8},{16,20},{20,16},{24,28},{28,24},{1,5},{5... | collective-permute-start | bytes 49160 | tf_op jit(solution)/shard_map/ppermute | solution.py:200
  24.5 16.3 %collective-permute-start.1 = (f32[4096]{0:T(1024)S(1)}, f32[4096]{0:T(1024)S(1)}, u32[]{:S(2)}, u32[]{:S(2)}) collective-permute-start(f32[4096]{0:T(1024)S(1)} %add.48), channel_id=1, source_target_pairs={{0,8},{4,12},{8,0},{12,4},{16,24},{20,28},{24,16},{28,20},{1,9},{5... | collective-permute-start | bytes 49160 | tf_op jit(solution)/shard_map/ppermute | solution.py:200
  40.7 4.9 %collective-permute-start.2 = (f32[4096]{0:T(1024)S(1)}, f32[4096]{0:T(1024)S(1)}, u32[]{:S(2)}, u32[]{:S(2)}) collective-permute-start(f32[4096]{0:T(1024)S(1)} %add.49), channel_id=1, source_target_pairs={{0,16},{4,20},{8,24},{12,28},{16,0},{20,4},{24,8},{28,12},{1,17},{... | collective-permute-start | bytes 49160 | tf_op jit(solution)/shard_map/ppermute | solution.py:200
  43.9 10.1 %collective-permute-start.11 = (bf16[2048,128]{1,0:T(8,128)(2,1)}, bf16[2048,128]{1,0:T(8,128)(2,1)S(1)}, u32[]{:S(2)}, u32[]{:S(2)}) collective-permute-start(bf16[2048,128]{1,0:T(8,128)(2,1)} %collective-permute-done.10.same_ref), channel_id=1, source_target_pairs={{8,12},{12,8},{16,20},{20,16},{9,13},{13,9},{17,21},{21,17},{10,14... | collective-permute-start | bytes 1572872 | tf_op jit(solution)/shard_map/ppermute | solution.py:193
  46.2 1.2 %copy-start = (bf16[4096,128]{1,0:T(8,128)(2,1)S(1)}, bf16[4096,128]{1,0:T(8,128)(2,1)}, u32[]{:S(2)}) copy-start(bf16[4096,128]{1,0:T(8,128)(2,1)} %refs_0_.1) | copy-start | bytes 3145732
  52.6 7.3 %collective-permute-start.8 = (f32[2,12,32,128]{3,2,1,0:T(8,128)S(1)}, f32[2,12,32,128]{3,2,1,0:T(8,128)S(1)}, u32[]{:S(2)}, u32[]{:S(2)}) collective-permute-start(f32[2,12,32,128]{3,2,1,0:T(8,128)S(1)} %get-tuple-element.8), channel_id=1, source_target_pairs={{8,9},{9,8},{10,11},{11,10},{12,14},{13,15},{14,12},{15,13},{16,17... | collective-permute-start | bytes 1179656 | tf_op jit(solution)/shard_map/ppermute | solution.py:262
  59.2 0.7 collective-permute-start.12
  60.0 1.4 %collective-permute-start.9 = (f32[1,12,32,128]{3,2,1,0:T(8,128)S(1)}, f32[1,12,32,128]{3,2,1,0:T(8,128)S(1)}, u32[]{:S(2)}, u32[]{:S(2)}) collective-permute-start(f32[1,12,32,128]{3,2,1,0:T(8,128)S(1)} %get-tuple-element.15), channel_id=1, source_target_pairs={{8,10},{9,11},{10,8},{11,9},{12,13},{13,12},{14,15},{15,14},{16,18... | collective-permute-start | bytes 589832 | tf_op jit(solution)/shard_map/ppermute | solution.py:262
  60.7 0.7 collective-permute-start.13
  62.2 25.2 %collective-permute-start.14 = (f32[32,640]{1,0:T(8,128)S(1)}, f32[32,640]{1,0:T(8,128)S(1)}, u32[]{:S(2)}, u32[]{:S(2)}) collective-permute-start(f32[32,640]{1,0:T(8,128)S(1)} %get-tuple-element.17), channel_id=1, source_target_pairs={{8,0},{12,4},{16,24},{20,28},{9,1},{13,5},{17,25},{21,29},{10,2},{... | collective-permute-start | bytes 245768 | tf_op jit(solution)/shard_map/ppermute | solution.py:285
  63.5 26.2 %collective-permute-start.15 = (f32[32,640]{1,0:T(8,128)S(1)}, f32[32,640]{1,0:T(8,128)S(1)}, u32[]{:S(2)}, u32[]{:S(2)}) collective-permute-start(f32[32,640]{1,0:T(8,128)S(1)} %get-tuple-element.19), channel_id=1, source_target_pairs={{8,24},{12,28},{16,0},{20,4},{9,25},{13,29},{17,1},{21,5},{10,26},... | collective-permute-start | bytes 245768 | tf_op jit(solution)/shard_map/ppermute | solution.py:285
  64.8 24.9 %collective-permute-start.16 = (f32[32,640]{1,0:T(8,128)S(1)}, f32[32,640]{1,0:T(8,128)S(1)}, u32[]{:S(2)}, u32[]{:S(2)}) collective-permute-start(f32[32,640]{1,0:T(8,128)S(1)} %get-tuple-element.18), channel_id=1, source_target_pairs={{8,16},{12,20},{16,8},{20,12},{9,17},{13,21},{17,9},{21,13},{10,18... | collective-permute-start | bytes 245768 | tf_op jit(solution)/shard_map/ppermute | solution.py:285

commit v2 on v0

v2 whole, which is shorter than its diff:
```python
import functools

import jax
import jax.numpy as jnp
import numpy as np
from jax import lax
from jax.experimental import pallas as pl
from jax.experimental.pallas import tpu as pltpu
from jax.sharding import PartitionSpec as P


LANES = 128


def bits_of(count):
    return [1 << n for n in range(count.bit_length() - 1)]


def part_masks(space_count, core):
    bits = bits_of(space_count)
    taken = [bits[(step + core) % len(bits)] for step in range(len(bits))]
    masks = []
    for position in range(space_count):
        mask = 0
        for step, bit in enumerate(taken):
            if position >> (len(bits) - 1 - step) & 1:
                mask |= bit
        masks.append(mask)
    return masks


def tile_tables(snap_count, late, early):
    chip_count = snap_count // 2
    near = 2 * len(early)
    column = {offset: n for n, offset in enumerate(early)}
    early_rows, late_rows = [], []
    for me in range(snap_count):
        parts = ([], [])
        for offset in range(chip_count):
            block = ((me // 2) ^ offset) * 2 + me % 2
            for k in range(chip_count + 1):
                rel = ((block + k) % snap_count) ^ me
                if offset == late:
                    place = near + 1 if rel == 2 * late + 1 else near if rel == 2 * late else 2 * column[rel // 2] + rel % 2
                    parts[1].append((near + place, offset, k))
                elif rel // 2 == late:
                    parts[1].append((2 * column[offset] + rel % 2, offset, k))
                else:
                    parts[0].append((column[offset] * near + 2 * column[rel // 2] + rel % 2, offset, k))
        early_rows.append(parts[0])
        late_rows.append(parts[1])

    def even(rows):
        longest = max(len(row) for row in rows)
        return np.array([row + [row[-1]] * (longest - len(row)) for row in rows], np.int32).reshape(snap_count, -1)

    return even(early_rows), even(late_rows)


def place_tiles(table_ref, tiles_ref, keep_ref, send_ref):
    me, space = lax.axis_index("snap"), lax.axis_index("space")
    half, slots, part_rows, _ = keep_ref.shape
    core = me % 2
    masks = [part_masks(2 * half, c) for c in (0, 1)]

    def one(slot, carry):
        tile = table_ref[me, 3 * slot]
        for position in range(2 * half):
            part = space ^ jnp.where(core == 0, masks[0][position], masks[1][position])
            rows = pl.ds(pl.multiple_of(part * part_rows, part_rows), part_rows)
            target = keep_ref if position < half else send_ref
            target[position % half, slot] = tiles_ref[tile, rows, :]
        return carry

    lax.fori_loop(0, slots, one, 0)


def as_column(row):
    return jnp.transpose(jnp.broadcast_to(row, (LANES, LANES)))


def product(left, right):
    return lax.dot_general(left, right, (((1,), (0,)), ((), ())), preferred_element_type=jnp.float32)


def split_kernel(hub_of, offsets, rows_ref, *refs):
    pieces, sums_ref, sems = refs[:-2], refs[-2], refs[-1]
    me = lax.axis_index("snap")
    copies = []
    for n, offset in enumerate(offsets):
        first = pl.multiple_of(hub_of(me ^ (2 * offset)), pieces[0].shape[0])
        copies.append(pltpu.make_async_copy(rows_ref.at[pl.ds(first, pieces[0].shape[0]), :], pieces[n], sems.at[n]))
    for copy in reversed(copies):
        copy.start()
    copies[-1].wait()
    for tile in range(sums_ref.shape[0]):
        values = pieces[-1][tile * LANES : (tile + 1) * LANES, :].astype(jnp.float32)
        sums_ref[tile : tile + 1, :] = jnp.sum(jnp.transpose(values), axis=0, keepdims=True)
    for copy in copies[:-1]:
        copy.wait()


def early_kernel(total_columns, table_ref, late_same_ref, late_other_ref, *refs):
    near = len(refs) - 6
    blocks = refs[:near]
    turned_ref, mean_ref, keep_ref, send_ref, fluct_ref, tiles_ref = refs[near:]
    rows, width = blocks[0].shape

    def one_tile(tile, carry):
        target = pl.ds(pl.multiple_of(tile * LANES, LANES), LANES)
        held = [ref[target, :].astype(jnp.float32) for ref in blocks]
        near_sum = jnp.sum(functools.reduce(jnp.add, held), axis=1, keepdims=True)
        far_sum = late_same_ref[pl.ds(tile, 1), :] + late_other_ref[pl.ds(tile, 1), :]
        mean = (as_column(far_sum) + near_sum) * (1.0 / total_columns)
        mean_ref[pl.ds(tile, 1), :] = jnp.transpose(mean)[0:1, :]
        for n in range(near):
            value = (held[n] - mean).astype(jnp.bfloat16)
            fluct_ref[target, n * width : (n + 1) * width] = value
            turned_ref[n * width : (n + 1) * width, target] = jnp.transpose(value)
        return carry

    lax.fori_loop(0, rows // LANES, one_tile, 0)
    for n in range(near // 2):
        left = turned_ref[2 * n * width : (2 * n + 1) * width, :]
        for first in range(0, near, 2):
            both = product(left, fluct_ref[:, first * width : (first + 2) * width])
            tiles_ref[n * near + first] = both[:, :width]
            tiles_ref[n * near + first + 1] = both[:, width:]
    place_tiles(table_ref, tiles_ref, keep_ref, send_ref)


def late_kernel(table_ref, mean_ref, same_ref, other_ref, turned_ref, *refs):
    keep_ref, send_ref, fluct_ref, fluct_turned_ref, tiles_ref = refs
    rows, width = same_ref.shape
    near = turned_ref.shape[0] // width

    def one_tile(tile, carry):
        mean = as_column(mean_ref[pl.ds(tile, 1), :])
        target = pl.ds(pl.multiple_of(tile * LANES, LANES), LANES)
        for n, ref in enumerate((same_ref, other_ref)):
            value = (ref[target, :].astype(jnp.float32) - mean).astype(jnp.bfloat16)
            fluct_ref[target, n * width : (n + 1) * width] = value
            fluct_turned_ref[n * width : (n + 1) * width, target] = jnp.transpose(value)
        return carry

    lax.fori_loop(0, rows // LANES, one_tile, 0)
    step = 2 * width
    for first in range(0, near + 2, 2):
        left = turned_ref[first * width : first * width + step, :] if first < near else fluct_turned_ref[...]
        four = product(left, fluct_ref[...])
        tiles_ref[near + first] = jnp.transpose(four[:width, :width])
        tiles_ref[near + first + 1] = jnp.transpose(four[width:, :width])
        if first < near:
            tiles_ref[first] = four[:width, :width]
            tiles_ref[first + 1] = four[:width, width:]
    place_tiles(table_ref, tiles_ref, keep_ref, send_ref)


def joined_kernel(early_ref, late_ref, mean_ref, first_keep, first_recv, second_keep, second_recv, out_ref):
    me = lax.axis_index("snap")
    _, _, part_rows, width = first_keep.shape
    for table, keep, recv in ((early_ref, first_keep, first_recv), (late_ref, second_keep, second_recv)):

        def one(slot, carry, table=table, keep=keep, recv=recv):
            offset, k = table[me, 3 * slot + 1], table[me, 3 * slot + 2]
            lanes = pl.ds(pl.multiple_of(k * width, width), width)
            out_ref[offset, 0:part_rows, lanes] = keep[0, slot] + recv[0, slot]
            return carry

        lax.fori_loop(0, keep.shape[1], one, 0)
    band = out_ref.shape[2] // width
    for offset in range(out_ref.shape[0]):
        for n in range(mean_ref.shape[0]):
            row = part_rows + n // band
            out_ref[offset, row : row + 1, (n % band) * width : (n % band + 1) * width] = mean_ref[n : n + 1, :]


def collected_kernel(first_chip, scale, own_ref, *refs):
    others, (gram_ref, mean_ref) = refs[:-2], refs[-2:]
    chip = lax.axis_index("snap") // 2
    part_rows, columns = gram_ref.shape
    chip_count = len(others) + 1
    hub_chips = chip_count // 2
    is_hub = (chip >= first_chip) & (chip < first_chip + hub_chips)
    total = jnp.where(is_hub, own_ref[0:part_rows, :], 0.0)
    for ref in others:
        total = total + ref[0:part_rows, :]
    gram_ref[...] = total * scale
    slabs = (own_ref, *others)
    mean_rows = mean_ref.shape[0] // hub_chips
    band = columns // LANES
    for offset, ref in enumerate(slabs):
        hub = (chip ^ offset) - first_chip

        @pl.when((hub >= 0) & (hub < hub_chips))
        def _(ref=ref, hub=hub):
            for n in range(mean_rows):
                row = part_rows + n // band
                mean_ref[pl.ds(hub * mean_rows + n, 1), :] = ref[row : row + 1, (n % band) * LANES : (n % band + 1) * LANES]


def per_device(snapshots):
    snap_count = lax.axis_size("snap")
    space_count = lax.axis_size("space")
    row_count, width = snapshots.shape
    chip_count = snap_count // 2
    first_chip, hub_chips = chip_count // 4, chip_count // 2
    hubs = list(range(2 * first_chip, 2 * (first_chip + hub_chips)))
    rows = row_count // hub_chips
    band = chip_count + 1
    part_rows = width // space_count
    late = chip_count // 2
    early = [offset for offset in range(chip_count) if offset != late]
    near = 2 * len(early)
    smem = pl.BlockSpec(memory_space=pltpu.SMEM)
    vmem = pl.BlockSpec(memory_space=pltpu.VMEM)

    def shaped(dtype, *shape):
        return jax.ShapeDtypeStruct(shape, dtype)

    def kernel(body, tables, operands, out_shapes, scratch=(), flops=1000, raw=False):
        sizes = [int(np.prod(s.shape)) * jnp.dtype(s.dtype).itemsize for s in (*operands, *out_shapes)]
        sizes += [int(np.prod(s.shape)) * jnp.dtype(s.dtype).itemsize for s in scratch if hasattr(s, "shape") and s.memory_space == pltpu.VMEM]
        return pl.pallas_call(
            body,
            out_shape=list(out_shapes),
            in_specs=[smem] * len(tables) + [pl.BlockSpec(memory_space=pl.ANY) if raw else vmem] * len(operands),
            out_specs=[vmem] * len(out_shapes),
            scratch_shapes=list(scratch),
            cost_estimate=pl.CostEstimate(flops=flops, bytes_accessed=0, transcendentals=0),
            compiler_params=pltpu.CompilerParams(vmem_limit_bytes=(60 << 20) if raw else sum(sizes) + (6 << 20)),
        )(*tables, *operands)

    def hub_of(device):
        return jnp.clip(device // 2 - first_chip, 0, hub_chips - 1) * rows

    def to_hubs(x, offset):
        return lax.ppermute(x, "snap", [(h ^ (2 * offset), h) for h in hubs])

    def to_other_core(x):
        return lax.ppermute(x, "snap", [(h, h ^ 1) for h in hubs])

    piece = shaped(snapshots.dtype, rows, width)
    sums = shaped(jnp.float32, rows // LANES, LANES)
    offsets = early + [late]
    *pieces, far_sums = kernel(
        functools.partial(split_kernel, hub_of, offsets),
        [],
        [snapshots],
        [piece] * chip_count + [sums],
        [pltpu.SemaphoreType.DMA((chip_count,))],
        raw=True,
    )
    late_same = to_hubs(far_sums, late)
    blocks = {0: pieces[0]}
    for offset, x in zip(offsets[1:], pieces[1:]):
        blocks[offset] = to_hubs(x, offset)
    late_other = to_other_core(late_same)
    passed = {offset: to_other_core(blocks[offset]) for offset in offsets}

    early_all, late_all = tile_tables(snap_count, late, early)
    early_table, late_table = jnp.asarray(early_all), jnp.asarray(late_all)

    def halves(table):
        return [shaped(jnp.float32, space_count // 2, table.shape[1] // 3, part_rows, width)] * 2

    operands = [late_same, late_other]
    for offset in early:
        operands += [blocks[offset], passed[offset]]
    turned, mean_rows, first_keep, first_send = kernel(
        functools.partial(early_kernel, width * snap_count),
        [early_table],
        operands,
        [shaped(jnp.bfloat16, near * width, rows), sums] + halves(early_all),
        [pltpu.VMEM((rows, near * width), jnp.bfloat16), pltpu.VMEM((near * near // 2, width, width), jnp.float32)],
        flops=near * near * width * width * rows,
    )
    second_keep, second_send = kernel(
        late_kernel,
        [late_table],
        [mean_rows, blocks[late], passed[late], turned],
        halves(late_all),
        [
            pltpu.VMEM((rows, 2 * width), jnp.bfloat16),
            pltpu.VMEM((2 * width, rows), jnp.bfloat16),
            pltpu.VMEM((2 * near + 2, width, width), jnp.float32),
        ],
        flops=4 * snap_count * width * width * rows,
    )

    bits = bits_of(space_count)

    def exchanged(x, step):
        pairs = []
        for h in hubs:
            bit = bits[(step + h % 2) % len(bits)]
            pairs += [(h * space_count + s, h * space_count + (s ^ bit)) for s in range(space_count)]
        return lax.ppermute(x, ("snap", "space"), pairs)

    def over_space(keep, send):
        for step in range(len(bits) - 1):
            both = keep + exchanged(send, step)
            half = both.shape[0] // 2
            keep, send = both[:half], both[half:]
        return keep, exchanged(send, len(bits) - 1)

    summed = (*over_space(first_keep, first_send), *over_space(second_keep, second_send))
    mean_space = -(-(-(-(rows // LANES) // band)) // 8) * 8
    slab = shaped(jnp.float32, part_rows + mean_space, band * width)
    (slabs,) = kernel(
        joined_kernel, [early_table, late_table], [mean_rows, *summed], [shaped(jnp.float32, chip_count, *slab.shape)]
    )

    own = [slabs[0]]
    for offset in range(1, chip_count):
        own.append(lax.ppermute(slabs[offset], "snap", [(h, h ^ (2 * offset)) for h in hubs]))
    gram_band, mean_field = kernel(
        functools.partial(collected_kernel, first_chip, 1.0 / (row_count * space_count)),
        [],
        own,
        [shaped(jnp.float32, part_rows, band * width), shaped(jnp.float32, row_count // LANES, LANES)],
    )
    return gram_band, mean_field.reshape(row_count)


def solution(mesh):
    return jax.shard_map(
        per_device,
        mesh=mesh,
        in_specs=(P("space", "snap"),),
        out_specs=(P(("snap", "space"), None), P("space")),
        check_vma=False,
    )
```

time: 139 us -> 93.8 us (0.67)
  blocking collectives: 30.4 us -> 0 us
  waiting for transfers between devices: 75.3 us -> 44.9 us
  starting transfers between devices: 11.4 us -> 29.2 us
  Pallas kernels: 0 us -> 16.4 us
  between operations: 14.1 us -> 0.92 us
  other arithmetic: 4.63 us -> 0.11 us
  matrix products: 2.39 us -> 0 us
  local copies, waits for them, and re-layouts: 0.37 us -> 1.81 us
    psum x1 -> x0, blocking collectives: 30.4 us -> none  [per_device(): mean_field = lax.psum(totals, 'snap') / (block_width * snap_count)]
    reduce_scatter x1 -> x0, waiting for transfers between devices: 26.1 us -> none  [per_device(): lax.psum_scatter(gram_band, 'space', scatter_dimension=0, tiled=True)]
    ppermute x4 -> x16, starting transfers between devices: 11.3 us -> 29.2 us  [the longest x4 19.8 us: to_hubs(): return lax.ppermute(x, 'snap', [(h ^ 2 * offset, h) for h in hubs])]
    pallas_call x0 -> x5, Pallas kernels: none -> 16.4 us  [kernel(): pl.pallas_call(body, out_shape=list(out_shapes), in_specs=[smem] * len(ta...]
    ppermute x4 -> x16, waiting for transfers between devices: 49.3 us -> 44.9 us  [the longest x3 27.3 us: per_device(): lax.ppermute(slabs[offset], 'snap', [(h, h ^ 2 * offset) for h in hubs])]
    dot_general x5 -> x0, matrix products: 2.39 us -> none  [cross_tiles(): lax.dot_general(left_block, right_block, (((0,), (0,)), ((), ())), prefer...]
    unnamed x5 -> x6, local copies, waits for them, and re-layouts: 0.08 us -> 1.73 us
    reduce_sum x1 -> x0, other arithmetic: 1.65 us -> none  [per_device(): totals = jnp.sum(snapshots.astype(jnp.float32), axis=1)]
  transfers between devices with their start and end apart: 5 -> 16, of which waited for: 5 -> 5; matrix products, arithmetic and copies ran while one was open for 0% -> 0% of each run, Pallas kernels for 0% -> 13%
where the time goes in v2:
time: 93.8 us; the launch traced here: 93.3 us
  waiting for transfers between devices  44.9 us (48%)
  starting transfers between devices  29.2 us (31%)
  Pallas kernels  16.4 us (17%)
  local copies, waits for them, and re-layouts  1.81 us (2%)
    ppermute x3, waiting for transfers between devices, per_device(): lax.ppermute(slabs[offset], 'snap', [(h, h ^ 2 * offset) for h in hubs])  27.3 us
    ppermute x4, starting transfers between devices, to_hubs(): return lax.ppermute(x, 'snap', [(h ^ 2 * offset, h) for h in hubs])  19.8 us
    ppermute x4, waiting for transfers between devices, to_hubs(): return lax.ppermute(x, 'snap', [(h ^ 2 * offset, h) for h in hubs])  17.5 us
    pallas_call x5, Pallas kernels, kernel(): pl.pallas_call(body, out_shape=list(out_shapes), in_specs=[smem] * len(ta...  16.4 us
    ppermute x5, starting transfers between devices, to_other_core(): return lax.ppermute(x, 'snap', [(h, h ^ 1) for h in hubs])  3.4 us
    ppermute x3, starting transfers between devices, per_device(): lax.ppermute(slabs[offset], 'snap', [(h, h ^ 2 * offset) for h in hubs])  3.25 us
    ppermute x4, starting transfers between devices, exchanged(): return lax.ppermute(x, ('snap', 'space'), pairs)  2.71 us
  transfers between devices with their start and end apart: 16, of which 5 were waited for; matrix products, arithmetic and copies ran while one was open for 0% of the time, Pallas kernels for 13%

profile of v2, /device:TPU:0, one launch (start us, length us, event | category | flops | bytes accessed | tf_op | source)
XLA Modules:
  0.0 93.3 jit_solution(11640075678625966533)
XLA Ops:
  0.6 0.0 copy-start
  0.6 2.9 %shard_map.50 = (bf16[2048,128]{1,0:T(8,128)(2,1)}, bf16[2048,128]{1,0:T(8,128)(2,1)}, bf16[2048,128]{1,0:T(8,128)(2,1)}, bf16[2048,128]{1,0:T(8,128)(2,1)}, f32[16,128]{1,0:T(8,128)}) custom-call(bf16[4096,128]{1,0:T(8,128)(2,1)} %rows_ref.1), custom_call_target="tpu_custom_call" | custom-call | flops 1000 | tf_op jit(solution)/shard_map/pallas_call | solution.py:224
  3.6 5.0 %collective-permute-start.3 = (bf16[2048,128]{1,0:T(8,128)(2,1)}, bf16[2048,128]{1,0:T(8,128)(2,1)S(1)}, u32[]{:S(2)}, u32[]{:S(2)}) collective-permute-start(bf16[2048,128]{1,0:T(8,128)(2,1)} %get-tuple-element.17), channel_id=1, source_target_pairs={{0,8},{4,12},{24,16},{28,20},{1,9},{5,13},{25,17},{29,21},{2,10},{... | collective-permute-start | bytes 1572872 | tf_op jit(solution)/shard_map/ppermute | solution.py:238
  8.6 0.7 collective-permute-start.5
  9.3 4.0 %collective-permute-start.9 = (bf16[2048,128]{1,0:T(8,128)(2,1)}, bf16[2048,128]{1,0:T(8,128)(2,1)S(1)}, u32[]{:S(2)}, u32[]{:S(2)}) collective-permute-start(bf16[2048,128]{1,0:T(8,128)(2,1)} %get-tuple-element.22), channel_id=1, source_target_pairs={{24,8},{28,12},{0,16},{4,20},{25,9},{29,13},{1,17},{5,21},{26,10},... | collective-permute-start | bytes 1572872 | tf_op jit(solution)/shard_map/ppermute | solution.py:238
  13.3 0.7 collective-permute-start.2
  14.0 7.2 %collective-permute-done.3.refs_2_ = bf16[2048,128]{1,0:T(8,128)(2,1)S(1)} collective-permute-done((bf16[2048,128]{1,0:T(8,128)(2,1)}, bf16[2048,128]{1,0:T(8,128)(2,1)S(1)}, u32[]{:S(2)}, u32[]{:S(2)}) %collective-permute-start.3) | collective-permute-done | bytes 524320 | tf_op jit(solution)/shard_map/ppermute | solution.py:238
  21.2 0.7 collective-permute-start.4
  21.8 0.0 collective-permute-done.5.refs_4_
  21.9 0.7 collective-permute-start.6
  22.6 8.7 %collective-permute-done.9.same_ref = bf16[2048,128]{1,0:T(8,128)(2,1)S(1)} collective-permute-done((bf16[2048,128]{1,0:T(8,128)(2,1)}, bf16[2048,128]{1,0:T(8,128)(2,1)S(1)}, u32[]{:S(2)}, u32[]{:S(2)}) %collective-permute-start.9) | collective-permute-done | bytes 524320 | tf_op jit(solution)/shard_map/ppermute | solution.py:238
  31.3 0.7 collective-permute-start.10
  32.0 10.2 %collective-permute-start = (f32[16,128]{1,0:T(8,128)}, f32[16,128]{1,0:T(8,128)S(1)}, u32[]{:S(2)}, u32[]{:S(2)}) collective-permute-start(f32[16,128]{1,0:T(8,128)} %get-tuple-element.15), channel_id=1, source_target_pairs={{24,8},{28,12},{0,16},{4,20},{25,9},{29,13},{1,17},{5,21},{26,10},... | collective-permute-start | bytes 24584 | tf_op jit(solution)/shard_map/ppermute | solution.py:238
  42.2 1.6 %collective-permute-done.late_same_ref = f32[16,128]{1,0:T(8,128)S(1)} collective-permute-done((f32[16,128]{1,0:T(8,128)}, f32[16,128]{1,0:T(8,128)S(1)}, u32[]{:S(2)}, u32[]{:S(2)}) %collective-permute-start) | collective-permute-done | bytes 8224 | tf_op jit(solution)/shard_map/ppermute | solution.py:238
  43.8 0.6 collective-permute-start.1
  44.5 0.0 copy-start.1
  44.5 0.7 copy-done.1
  45.2 1.0 %copy-done.2 = bf16[2048,128]{1,0:T(8,128)(2,1)S(1)} copy-done((bf16[2048,128]{1,0:T(8,128)(2,1)S(1)}, bf16[2048,128]{1,0:T(8,128)(2,1)}, u32[]{:S(2)}) %copy-start.2) | copy-done | bytes 524312
  46.2 7.0 %shard_map.51 = (bf16[768,2048]{1,0:T(8,128)(2,1)S(1)}, f32[16,128]{1,0:T(8,128)S(1)}, f32[2,12,32,128]{3,2,1,0:T(8,128)S(1)}, f32[2,12,32,128]{3,2,1,0:T(8,128)S(1)}) custom-call(s32[8,36]{1,0:T(8,128)S(1)} %copy-done.1, f32[16,128]{1,0:T(8,128)S(1)} %collective-permute-done.late_same_ref, f32[16,128]{1,0:T(8,128)S(1)} %collective-permute-done.1.late_other_ref, ...), custom_call_target="tpu_custom_call" | custom-call | flops 1207959552 | tf_op jit(solution)/shard_map/pallas_call | solution.py:224
  53.2 0.7 collective-permute-start.7
  53.9 4.8 %shard_map.52 = (f32[2,9,32,128]{3,2,1,0:T(8,128)S(1)}, f32[2,9,32,128]{3,2,1,0:T(8,128)S(1)}) custom-call(s32[8,27]{1,0:T(8,128)S(1)} %copy-done, f32[16,128]{1,0:T(8,128)S(1)} %get-tuple-element.19.mean_ref, bf16[2048,128]{1,0:T(8,128)(2,1)S(1)} %collective-permute-done.9.same_ref, bf16[2048,128]{1,0:T(8,128)(2,1)S(1)} %collective-permute-done.10.other_ref, ...), custom_call_target="tpu_custom_call" | custom-call | flops 1073741824 | tf_op jit(solution)/shard_map/pallas_call | solution.py:224
  58.7 0.7 collective-permute-start.11
  59.5 0.1 add.6
  59.6 0.7 collective-permute-start.8
  60.3 0.7 collective-permute-start.12
  61.0 0.9 shard_map.53
  62.0 1.3 %collective-permute-start.13 = (f32[40,640]{1,0:T(8,128)S(1)}, f32[40,640]{1,0:T(8,128)S(1)}, u32[]{:S(2)}, u32[]{:S(2)}) collective-permute-start(f32[40,640]{1,0:T(8,128)S(1)} %get-tuple-element.30), channel_id=1, source_target_pairs={{8,0},{12,4},{16,24},{20,28},{9,1},{13,5},{17,25},{21,29},{10,2},{... | collective-permute-start | bytes 307208 | tf_op jit(solution)/shard_map/ppermute | solution.py:316
  63.3 1.3 %collective-permute-start.14 = (f32[40,640]{1,0:T(8,128)S(1)}, f32[40,640]{1,0:T(8,128)S(1)}, u32[]{:S(2)}, u32[]{:S(2)}) collective-permute-start(f32[40,640]{1,0:T(8,128)S(1)} %get-tuple-element.29), channel_id=1, source_target_pairs={{8,24},{12,28},{16,0},{20,4},{9,25},{13,29},{17,1},{21,5},{10,26},... | collective-permute-start | bytes 307208 | tf_op jit(solution)/shard_map/ppermute | solution.py:316
  64.6 0.7 collective-permute-start.15
  65.2 25.2 %collective-permute-done.13.refs_0_ = f32[40,640]{1,0:T(8,128)S(1)} collective-permute-done((f32[40,640]{1,0:T(8,128)S(1)}, f32[40,640]{1,0:T(8,128)S(1)}, u32[]{:S(2)}, u32[]{:S(2)}) %collective-permute-start.13) | collective-permute-done | bytes 102432 | tf_op jit(solution)/shard_map/ppermute | solution.py:316
  90.5 2.1 %collective-permute-done.14.refs_1_ = f32[40,640]{1,0:T(8,128)S(1)} collective-permute-done((f32[40,640]{1,0:T(8,128)S(1)}, f32[40,640]{1,0:T(8,128)S(1)}, u32[]{:S(2)}, u32[]{:S(2)}) %collective-permute-start.14) | collective-permute-done | bytes 102432 | tf_op jit(solution)/shard_map/ppermute | solution.py:316
  92.6 0.7 shard_map.54
  (16 shorter events, 0.2 us)
Async XLA Ops:
  0.6 53.3 %copy-start = (s32[8,27]{1,0:T(8,128)S(1)}, s32[8,27]{1,0:T(8,128)}, u32[]{:S(2)}) copy-start(s32[8,27]{1,0:T(8,128)} %constant.5.clone.table_ref.late_ref) | copy-start | bytes 2596
  3.6 17.6 %collective-permute-start.3 = (bf16[2048,128]{1,0:T(8,128)(2,1)}, bf16[2048,128]{1,0:T(8,128)(2,1)S(1)}, u32[]{:S(2)}, u32[]{:S(2)}) collective-permute-start(bf16[2048,128]{1,0:T(8,128)(2,1)} %get-tuple-element.17), channel_id=1, source_target_pairs={{0,8},{4,12},{24,16},{28,20},{1,9},{5,13},{25,17},{29,21},{2,10},{... | collective-permute-start | bytes 1572872 | tf_op jit(solution)/shard_map/ppermute | solution.py:238
  8.6 13.3 %collective-permute-start.5 = (bf16[2048,128]{1,0:T(8,128)(2,1)}, bf16[2048,128]{1,0:T(8,128)(2,1)S(1)}, u32[]{:S(2)}, u32[]{:S(2)}) collective-permute-start(bf16[2048,128]{1,0:T(8,128)(2,1)} %get-tuple-element.18), channel_id=1, source_target_pairs={{16,8},{20,12},{8,16},{12,20},{17,9},{21,13},{9,17},{13,21},{18,10... | collective-permute-start | bytes 1572872 | tf_op jit(solution)/shard_map/ppermute | solution.py:238
  9.3 22.0 %collective-permute-start.9 = (bf16[2048,128]{1,0:T(8,128)(2,1)}, bf16[2048,128]{1,0:T(8,128)(2,1)S(1)}, u32[]{:S(2)}, u32[]{:S(2)}) collective-permute-start(bf16[2048,128]{1,0:T(8,128)(2,1)} %get-tuple-element.22), channel_id=1, source_target_pairs={{24,8},{28,12},{0,16},{4,20},{25,9},{29,13},{1,17},{5,21},{26,10},... | collective-permute-start | bytes 1572872 | tf_op jit(solution)/shard_map/ppermute | solution.py:238
  13.3 31.2 %collective-permute-start.2 = (bf16[2048,128]{1,0:T(8,128)(2,1)}, bf16[2048,128]{1,0:T(8,128)(2,1)S(1)}, u32[]{:S(2)}, u32[]{:S(2)}) collective-permute-start(bf16[2048,128]{1,0:T(8,128)(2,1)} %get-tuple-element.16.refs_0_), channel_id=1, source_target_pairs={{8,12},{12,8},{16,20},{20,16},{9,13},{13,9},{17,21},{21,17},{10,14... | collective-permute-start | bytes 1572872 | tf_op jit(solution)/shard_map/ppermute | solution.py:241
  21.2 23.3 %collective-permute-start.4 = (bf16[2048,128]{1,0:T(8,128)(2,1)S(1)}, bf16[2048,128]{1,0:T(8,128)(2,1)S(1)}, u32[]{:S(2)}, u32[]{:S(2)}) collective-permute-start(bf16[2048,128]{1,0:T(8,128)(2,1)S(1)} %collective-permute-done.3.refs_2_), channel_id=1, source_target_pairs={{8,12},{12,8},{16,20},{20,16},{9,13},{13,9},{17,21},{21,17},{10,14... | collective-permute-start | bytes 1572872 | tf_op jit(solution)/shard_map/ppermute | solution.py:241
  21.9 22.6 %collective-permute-start.6 = (bf16[2048,128]{1,0:T(8,128)(2,1)S(1)}, bf16[2048,128]{1,0:T(8,128)(2,1)S(1)}, u32[]{:S(2)}, u32[]{:S(2)}) collective-permute-start(bf16[2048,128]{1,0:T(8,128)(2,1)S(1)} %collective-permute-done.5.refs_4_), channel_id=1, source_target_pairs={{8,12},{12,8},{16,20},{20,16},{9,13},{13,9},{17,21},{21,17},{10,14... | collective-permute-start | bytes 1572872 | tf_op jit(solution)/shard_map/ppermute | solution.py:241
  31.3 22.6 %collective-permute-start.10 = (bf16[2048,128]{1,0:T(8,128)(2,1)S(1)}, bf16[2048,128]{1,0:T(8,128)(2,1)S(1)}, u32[]{:S(2)}, u32[]{:S(2)}) collective-permute-start(bf16[2048,128]{1,0:T(8,128)(2,1)S(1)} %collective-permute-done.9.same_ref), channel_id=1, source_target_pairs={{8,12},{12,8},{16,20},{20,16},{9,13},{13,9},{17,21},{21,17},{10,14... | collective-permute-start | bytes 1572872 | tf_op jit(solution)/shard_map/ppermute | solution.py:241
  32.0 11.8 %collective-permute-start = (f32[16,128]{1,0:T(8,128)}, f32[16,128]{1,0:T(8,128)S(1)}, u32[]{:S(2)}, u32[]{:S(2)}) collective-permute-start(f32[16,128]{1,0:T(8,128)} %get-tuple-element.15), channel_id=1, source_target_pairs={{24,8},{28,12},{0,16},{4,20},{25,9},{29,13},{1,17},{5,21},{26,10},... | collective-permute-start | bytes 24584 | tf_op jit(solution)/shard_map/ppermute | solution.py:238
  43.8 0.7 collective-permute-start.1
  44.5 0.7 copy-start.1
  45.2 1.0 %copy-start.2 = (bf16[2048,128]{1,0:T(8,128)(2,1)S(1)}, bf16[2048,128]{1,0:T(8,128)(2,1)}, u32[]{:S(2)}) copy-start(bf16[2048,128]{1,0:T(8,128)(2,1)} %get-tuple-element.16.refs_0_) | copy-start | bytes 1572868
  53.2 6.3 %collective-permute-start.7 = (f32[2,12,32,128]{3,2,1,0:T(8,128)S(1)}, f32[2,12,32,128]{3,2,1,0:T(8,128)S(1)}, u32[]{:S(2)}, u32[]{:S(2)}) collective-permute-start(f32[2,12,32,128]{3,2,1,0:T(8,128)S(1)} %get-tuple-element.21), channel_id=1, source_target_pairs={{8,9},{9,8},{10,11},{11,10},{12,14},{13,15},{14,12},{15,13},{16,17... | collective-permute-start | bytes 1179656 | tf_op jit(solution)/shard_map/ppermute | solution.py:298
  58.7 0.7 collective-permute-start.11
  59.6 1.4 %collective-permute-start.8 = (f32[1,12,32,128]{3,2,1,0:T(8,128)S(1)}, f32[1,12,32,128]{3,2,1,0:T(8,128)S(1)}, u32[]{:S(2)}, u32[]{:S(2)}) collective-permute-start(f32[1,12,32,128]{3,2,1,0:T(8,128)S(1)} %get-tuple-element.32), channel_id=1, source_target_pairs={{8,10},{9,11},{10,8},{11,9},{12,13},{13,12},{14,15},{15,14},{16,18... | collective-permute-start | bytes 589832 | tf_op jit(solution)/shard_map/ppermute | solution.py:298
  60.3 0.7 collective-permute-start.12
  62.0 28.5 %collective-permute-start.13 = (f32[40,640]{1,0:T(8,128)S(1)}, f32[40,640]{1,0:T(8,128)S(1)}, u32[]{:S(2)}, u32[]{:S(2)}) collective-permute-start(f32[40,640]{1,0:T(8,128)S(1)} %get-tuple-element.30), channel_id=1, source_target_pairs={{8,0},{12,4},{16,24},{20,28},{9,1},{13,5},{17,25},{21,29},{10,2},{... | collective-permute-start | bytes 307208 | tf_op jit(solution)/shard_map/ppermute | solution.py:316
  63.3 29.3 %collective-permute-start.14 = (f32[40,640]{1,0:T(8,128)S(1)}, f32[40,640]{1,0:T(8,128)S(1)}, u32[]{:S(2)}, u32[]{:S(2)}) collective-permute-start(f32[40,640]{1,0:T(8,128)S(1)} %get-tuple-element.29), channel_id=1, source_target_pairs={{8,24},{12,28},{16,0},{20,4},{9,25},{13,29},{17,1},{21,5},{10,26},... | collective-permute-start | bytes 307208 | tf_op jit(solution)/shard_map/ppermute | solution.py:316
  64.6 28.0 %collective-permute-start.15 = (f32[40,640]{1,0:T(8,128)S(1)}, f32[40,640]{1,0:T(8,128)S(1)}, u32[]{:S(2)}, u32[]{:S(2)}) collective-permute-start(f32[40,640]{1,0:T(8,128)S(1)} %get-tuple-element.28), channel_id=1, source_target_pairs={{8,16},{12,20},{16,8},{20,12},{9,17},{13,21},{17,9},{21,13},{10,18... | collective-permute-start | bytes 307208 | tf_op jit(solution)/shard_map/ppermute | solution.py:316

commit v3 on v0

v3 whole, which is shorter than its diff:
```python
import functools

import jax
import jax.numpy as jnp
import numpy as np
from jax import lax
from jax.experimental import pallas as pl
from jax.experimental.pallas import tpu as pltpu
from jax.sharding import PartitionSpec as P


LANES = 128


def completed(pairs, count):
    sources = [i for i in range(count) if i not in {p[0] for p in pairs}]
    targets = [i for i in range(count) if i not in {p[1] for p in pairs}]
    same = [i for i in sources if i in targets]
    left = zip([i for i in sources if i not in same], [i for i in targets if i not in same])
    return list(pairs) + [(i, i) for i in same] + list(left)


def place_tiles(wanted_late, tile_of, out_refs):
    me, space = lax.axis_index("snap"), lax.axis_index("space")
    snap_count = lax.axis_size("snap")
    chip_count, late = snap_count // 2, snap_count // 4
    band = chip_count + 1
    part_rows = out_refs[0].shape[1]

    def one(pair, slot):
        offset, k = pair // band, pair % band
        block = ((me // 2) ^ offset) * 2 + me % 2
        rel = ((block + k) % snap_count) ^ me
        is_late = jnp.logical_or(offset == late, rel // 2 == late)
        wanted = is_late if wanted_late else jnp.logical_not(is_late)

        @pl.when(wanted)
        def _():
            for n, out_ref in enumerate(out_refs):
                rows = pl.ds(pl.multiple_of((space ^ n) * part_rows, part_rows), part_rows)
                out_ref[slot] = tile_of(offset, rel, rows)

        return slot + jnp.where(wanted, 1, 0)

    lax.fori_loop(0, chip_count * band, one, 0)


def slot_count(snap_count, wanted_late):
    chip_count, late = snap_count // 2, snap_count // 4
    counts = []
    for me in range(snap_count):
        count = 0
        for offset in range(chip_count):
            block = ((me // 2) ^ offset) * 2 + me % 2
            for k in range(chip_count + 1):
                rel = ((block + k) % snap_count) ^ me
                count += (late in (offset, rel // 2)) == wanted_late
        counts.append(count)
    return max(counts)


def as_column(row):
    return jnp.transpose(jnp.broadcast_to(row, (LANES, LANES)))


def product(left, right):
    return lax.dot_general(left, right, (((1,), (0,)), ((), ())), preferred_element_type=jnp.float32)


def split_kernel(hub_of, offsets, rows_ref, *refs):
    pieces, sems = refs[:-1], refs[-1]
    me = lax.axis_index("snap")
    copies = []
    for n, offset in enumerate(offsets):
        first = pl.multiple_of(hub_of(me ^ (2 * offset)), pieces[0].shape[0])
        copies.append(pltpu.make_async_copy(rows_ref.at[pl.ds(first, pieces[0].shape[0]), :], pieces[n], sems.at[n]))
    for copy in copies:
        copy.start()
    for copy in copies:
        copy.wait()


def sums_kernel(piece_ref, sums_ref):
    for tile in range(sums_ref.shape[0]):
        values = piece_ref[tile * LANES : (tile + 1) * LANES, :].astype(jnp.float32)
        sums_ref[tile : tile + 1, :] = jnp.sum(jnp.transpose(values), axis=0, keepdims=True)


def early_kernel(total_columns, near, late_same_ref, late_other_ref, *refs):
    blocks = refs[:near]
    turned_ref, mean_ref, spread_ref, *out_refs = refs[near:-2]
    fluct_ref, tiles_ref = refs[-2:]
    rows, width = blocks[0].shape

    def one_tile(tile, carry):
        target = pl.ds(pl.multiple_of(tile * LANES, LANES), LANES)
        held = [ref[target, :].astype(jnp.float32) for ref in blocks]
        near_sum = jnp.sum(jnp.transpose(functools.reduce(jnp.add, held)), axis=0, keepdims=True)
        far_sum = late_same_ref[pl.ds(tile, 1), :] + late_other_ref[pl.ds(tile, 1), :]
        row = (near_sum + far_sum) * (1.0 / total_columns)
        mean_ref[pl.ds(tile, 1), :] = row
        mean = as_column(row)
        spread_ref[target, :] = mean
        for n in range(near):
            value = (held[n] - mean).astype(jnp.bfloat16)
            fluct_ref[target, n * width : (n + 1) * width] = value
            turned_ref[n * width : (n + 1) * width, target] = jnp.transpose(value)
        return carry

    lax.fori_loop(0, rows // LANES, one_tile, 0)
    half = near // 2
    for first in range(0, near * width, 2 * width):
        columns = slice(first, min(first + 2 * width, near * width))
        tiles_ref[:, columns] = product(turned_ref[0 : half * width, :], fluct_ref[:, columns])
    late = lax.axis_size("snap") // 4

    def tile_of(offset, rel, rows):
        other = rel // 2
        row = offset - jnp.where(offset > late, 1, 0)
        column = other - jnp.where(other > late, 1, 0) + half * (rel % 2)
        rows = pl.ds(pl.multiple_of(row * width + rows.start, rows.size), rows.size)
        return tiles_ref[rows, pl.ds(pl.multiple_of(column * width, width), width)]

    place_tiles(False, tile_of, out_refs)


def late_kernel(near, spread_ref, same_ref, other_ref, turned_ref, *refs):
    out_refs, (fluct_ref, far_turned_ref, tiles_ref) = refs[:-3], refs[-3:]
    rows, width = same_ref.shape

    def one_tile(tile, carry):
        target = pl.ds(pl.multiple_of(tile * LANES, LANES), LANES)
        mean = spread_ref[target, :]
        for n, ref in enumerate((same_ref, other_ref)):
            value = (ref[target, :].astype(jnp.float32) - mean).astype(jnp.bfloat16)
            fluct_ref[target, n * width : (n + 1) * width] = value
            far_turned_ref[n * width : (n + 1) * width, target] = jnp.transpose(value)
        return carry

    lax.fori_loop(0, rows // LANES, one_tile, 0)
    half = near // 2
    step = half * width
    for first in range(0, near * width, step):
        with_far = product(turned_ref[first : first + step, :], fluct_ref[...])
        for n in range(half):
            place = first // width + n
            tile = with_far[n * width : (n + 1) * width, :]
            tiles_ref[place] = jnp.transpose(tile[:, :width])
            if first == 0:
                tiles_ref[near + 2 + 2 * n] = tile[:, :width]
                tiles_ref[near + 3 + 2 * n] = tile[:, width:]
    both = product(far_turned_ref[...], fluct_ref[...])
    tiles_ref[near] = both[:width, :width]
    tiles_ref[near + 1] = jnp.transpose(both[width:, :width])
    late = lax.axis_size("snap") // 4

    def tile_of(offset, rel, rows):
        other = rel // 2
        row = offset - jnp.where(offset > late, 1, 0)
        column = other - jnp.where(other > late, 1, 0) + half * (rel % 2)
        turned = jnp.where(other == late, near + rel % 2, column)
        place = jnp.where(offset == late, turned, near + 2 + 2 * row + rel % 2)
        return tiles_ref[place, rows, :]

    place_tiles(True, tile_of, out_refs)


def joined_kernel(space_count, mean_ref, *refs):
    firsts, seconds, out_refs = refs[:space_count], refs[space_count : 2 * space_count], refs[2 * space_count :]
    me = lax.axis_index("snap")
    snap_count = lax.axis_size("snap")
    chip_count, late = snap_count // 2, snap_count // 4
    band = chip_count + 1
    _, part_rows, width = firsts[0].shape
    for offset, out_ref in enumerate(out_refs):
        if offset == 0:
            first_slot, second_slot = 0, 0
        block = ((me // 2) ^ offset) * 2 + me % 2
        for k in range(band):
            rel = ((block + k) % snap_count) ^ me
            is_late = jnp.logical_or(offset == late, rel // 2 == late)
            lanes = slice(k * width, (k + 1) * width)

            @pl.when(is_late)
            def _(out_ref=out_ref, lanes=lanes, slot=second_slot):
                out_ref[0:part_rows, lanes] = functools.reduce(jnp.add, [ref[slot] for ref in seconds])

            @pl.when(jnp.logical_not(is_late))
            def _(out_ref=out_ref, lanes=lanes, slot=first_slot):
                out_ref[0:part_rows, lanes] = functools.reduce(jnp.add, [ref[slot] for ref in firsts])

            second_slot = second_slot + jnp.where(is_late, 1, 0)
            first_slot = first_slot + jnp.where(is_late, 0, 1)
        for n in range(mean_ref.shape[0]):
            row = part_rows + n // band
            out_ref[row : row + 1, (n % band) * width : (n % band + 1) * width] = mean_ref[n : n + 1, :]


def collected_kernel(first_chip, scale, own_ref, *refs):
    others, (gram_ref, mean_ref) = refs[:-2], refs[-2:]
    chip = lax.axis_index("snap") // 2
    part_rows, columns = gram_ref.shape
    chip_count = len(others) + 1
    hub_chips = chip_count // 2
    slabs = (own_ref, *others)
    total = jnp.zeros((part_rows, columns), jnp.float32)
    for offset, ref in enumerate(slabs):
        hub = (chip ^ offset) - first_chip
        total = total + jnp.where((hub >= 0) & (hub < hub_chips), ref[0:part_rows, :], 0.0)
    gram_ref[...] = total * scale
    mean_rows = mean_ref.shape[0] // hub_chips
    band = columns // LANES
    for offset, ref in enumerate(slabs):
        hub = (chip ^ offset) - first_chip

        @pl.when((hub >= 0) & (hub < hub_chips))
        def _(ref=ref, hub=hub):
            for n in range(mean_rows):
                row = part_rows + n // band
                mean_ref[pl.ds(hub * mean_rows + n, 1), :] = ref[row : row + 1, (n % band) * LANES : (n % band + 1) * LANES]


def per_device(snapshots):
    snap_count = lax.axis_size("snap")
    space_count = lax.axis_size("space")
    row_count, width = snapshots.shape
    chip_count = snap_count // 2
    first_chip, hub_chips = chip_count // 4, chip_count // 2
    hubs = list(range(2 * first_chip, 2 * (first_chip + hub_chips)))
    rows = row_count // hub_chips
    band = chip_count + 1
    part_rows = width // space_count
    late = chip_count // 2
    early = [offset for offset in range(chip_count) if offset != late]
    near = 2 * len(early)
    vmem = pl.BlockSpec(memory_space=pltpu.VMEM)

    def shaped(dtype, *shape):
        return jax.ShapeDtypeStruct(shape, dtype)

    def kernel(body, operands, out_shapes, scratch=(), flops=1000, raw=False):
        sizes = [int(np.prod(s.shape)) * jnp.dtype(s.dtype).itemsize for s in (*operands, *out_shapes)]
        sizes += [int(np.prod(s.shape)) * jnp.dtype(s.dtype).itemsize for s in scratch if hasattr(s, "shape") and s.memory_space == pltpu.VMEM]
        return pl.pallas_call(
            body,
            out_shape=list(out_shapes),
            in_specs=[pl.BlockSpec(memory_space=pltpu.HBM) if raw else vmem] * len(operands),
            out_specs=[vmem] * len(out_shapes),
            scratch_shapes=list(scratch),
            cost_estimate=pl.CostEstimate(flops=flops, bytes_accessed=0, transcendentals=0),
            compiler_params=pltpu.CompilerParams(vmem_limit_bytes=sum(sizes) + (6 << 20)),
        )(*operands)

    def hub_of(device):
        return jnp.clip(device // 2 - first_chip, 0, hub_chips - 1) * rows

    def to_hubs(x, offset, name):
        pairs = [(h ^ (2 * offset), h) for h in hubs]
        full = name == "sums" or all(h ^ (2 * offset) in hubs for h in hubs)
        return lax.ppermute(x, "snap", completed(pairs, snap_count) if full else pairs)

    def to_other_core(x):
        return lax.ppermute(x, "snap", [(i, i ^ 1) for i in range(snap_count)])

    piece = shaped(snapshots.dtype, rows, width)
    sums = shaped(jnp.float32, rows // LANES, LANES)
    offsets = early + [late]
    pieces = kernel(
        functools.partial(split_kernel, hub_of, offsets),
        [snapshots],
        [piece] * chip_count,
        [pltpu.SemaphoreType.DMA((chip_count,))],
        raw=True,
    )
    (far_sums,) = kernel(sums_kernel, [pieces[-1]], [sums])
    late_same = to_hubs(far_sums, late, "sums")
    blocks = {0: pieces[0]}
    for offset, x in zip(offsets[1:], pieces[1:]):
        blocks[offset] = to_hubs(x, offset, "bulk")
    late_other = to_other_core(late_same)
    passed = {offset: to_other_core(blocks[offset]) for offset in offsets}

    first_slots, second_slots = slot_count(snap_count, False), slot_count(snap_count, True)
    turned, mean_rows, spread, *first = kernel(
        functools.partial(early_kernel, width * snap_count, near),
        [late_same, late_other] + [blocks[offset] for offset in early] + [passed[offset] for offset in early],
        [shaped(jnp.bfloat16, near * width, rows), sums, shaped(jnp.float32, rows, LANES)]
        + [shaped(jnp.float32, first_slots, part_rows, width)] * space_count,
        [pltpu.VMEM((rows, near * width), jnp.bfloat16), pltpu.VMEM((near // 2 * width, near * width), jnp.float32)],
        flops=near * near * width * width * rows,
    )
    second = kernel(
        functools.partial(late_kernel, near),
        [spread, blocks[late], passed[late], turned],
        [shaped(jnp.float32, second_slots, part_rows, width)] * space_count,
        [
            pltpu.VMEM((rows, 2 * width), jnp.bfloat16),
            pltpu.VMEM((2 * width, rows), jnp.bfloat16),
            pltpu.VMEM((2 * near + 2, width, width), jnp.float32),
        ],
        flops=4 * snap_count * width * width * rows,
    )

    def over_space(parts):
        got = [parts[0]]
        for n in range(1, space_count):
            got.append(lax.ppermute(parts[n], "space", [(s, s ^ n) for s in range(space_count)]))
        return got

    mean_space = -(-(-(-(rows // LANES) // band)) // 8) * 8
    slab = shaped(jnp.float32, part_rows + mean_space, band * width)
    slabs = kernel(
        functools.partial(joined_kernel, space_count),
        [mean_rows, *over_space(first), *over_space(second)],
        [slab] * chip_count,
    )

    own = [slabs[0]]
    for offset in range(1, chip_count):
        pairs = completed([(h, h ^ (2 * offset)) for h in hubs], snap_count)
        own.append(lax.ppermute(slabs[offset], "snap", pairs))
    gram_band, mean_field = kernel(
        functools.partial(collected_kernel, first_chip, 1.0 / (row_count * space_count)),
        own,
        [shaped(jnp.float32, part_rows, band * width), shaped(jnp.float32, row_count // LANES, LANES)],
    )
    return gram_band, mean_field.reshape(row_count)


def solution(mesh):
    return jax.shard_map(
        per_device,
        mesh=mesh,
        in_specs=(P("space", "snap"),),
        out_specs=(P(("snap", "space"), None), P("space")),
        check_vma=False,
    )
```

time: 139 us -> 77.3 us (0.56)
  waiting for transfers between devices: 75.3 us -> 34.9 us
  blocking collectives: 30.4 us -> 0 us
  starting transfers between devices: 11.4 us -> 27.5 us
  between operations: 14.1 us -> 0.75 us
  Pallas kernels: 0 us -> 12.1 us
  other arithmetic: 4.63 us -> 0 us
  matrix products: 2.39 us -> 0 us
    psum x1 -> x0, blocking collectives: 30.4 us -> none  [per_device(): mean_field = lax.psum(totals, 'snap') / (block_width * snap_count)]
    reduce_scatter x1 -> x0, waiting for transfers between devices: 26.1 us -> none  [per_device(): lax.psum_scatter(gram_band, 'space', scatter_dimension=0, tiled=True)]
    ppermute x4 -> x18, starting transfers between devices: 11.3 us -> 27.5 us  [the longest x4 15 us: to_hubs(): lax.ppermute(x, 'snap', completed(pairs, snap_count) if full else pairs)]
    ppermute x4 -> x18, waiting for transfers between devices: 49.3 us -> 34.9 us  [the longest x4 18.5 us: to_hubs(): lax.ppermute(x, 'snap', completed(pairs, snap_count) if full else pairs)]
    pallas_call x0 -> x6, Pallas kernels: none -> 12.1 us  [kernel(): pl.pallas_call(body, out_shape=list(out_shapes), in_specs=[pl.BlockSpec(m...]
    dot_general x5 -> x0, matrix products: 2.39 us -> none  [cross_tiles(): lax.dot_general(left_block, right_block, (((0,), (0,)), ((), ())), prefer...]
    reduce_sum x1 -> x0, other arithmetic: 1.65 us -> none  [per_device(): totals = jnp.sum(snapshots.astype(jnp.float32), axis=1)]
    mul x1 -> x0, other arithmetic: 1.53 us -> none  [per_device(): return (gram_band * (1.0 / (row_count * space_count)), mean_field)]
  transfers between devices with their start and end apart: 5 -> 18, of which waited for: 5 -> 8; matrix products, arithmetic and copies ran while one was open for 0% -> 0% of each run, Pallas kernels for 0% -> 10%
where the time goes in v3:
time: 77.3 us; the launch traced here: 76.5 us
  waiting for transfers between devices  34.9 us (45%)
  starting transfers between devices  27.5 us (36%)
  Pallas kernels  12.1 us (16%)
  local copies, waits for them, and re-layouts  1.22 us (2%)
    ppermute x4, waiting for transfers between devices, to_hubs(): lax.ppermute(x, 'snap', completed(pairs, snap_count) if full else pairs)  18.5 us
    ppermute x4, starting transfers between devices, to_hubs(): lax.ppermute(x, 'snap', completed(pairs, snap_count) if full else pairs)  15 us
    pallas_call x6, Pallas kernels, kernel(): pl.pallas_call(body, out_shape=list(out_shapes), in_specs=[pl.BlockSpec(m...  12.1 us
    ppermute x6, waiting for transfers between devices, over_space(): lax.ppermute(parts[n], 'space', [(s, s ^ n) for s in range(space_count)])  10 us
    ppermute x6, starting transfers between devices, over_space(): lax.ppermute(parts[n], 'space', [(s, s ^ n) for s in range(space_count)])  9 us
    ppermute x3, waiting for transfers between devices, per_device(): own.append(lax.ppermute(slabs[offset], 'snap', pairs))  5.17 us
    ppermute x3, starting transfers between devices, per_device(): own.append(lax.ppermute(slabs[offset], 'snap', pairs))  2.96 us
  transfers between devices with their start and end apart: 18, of which 8 were waited for; matrix products, arithmetic and copies ran while one was open for 0% of the time, Pallas kernels for 10%

profile of v3, /device:TPU:0, one launch (start us, length us, event | category | flops | bytes accessed | tf_op | source)
XLA Modules:
  0.0 76.5 jit_solution(2038186016401103187)
XLA Ops:
  0.6 1.2 %copy-done = bf16[4096,128]{1,0:T(8,128)(2,1)S(1)} copy-done((bf16[4096,128]{1,0:T(8,128)(2,1)S(1)}, bf16[4096,128]{1,0:T(8,128)(2,1)}, u32[]{:S(2)}) %copy-start) | copy-done | bytes 1048600
  1.9 0.2 shard_map.30
  2.0 5.0 %collective-permute-start.2 = (bf16[2048,128]{1,0:T(8,128)(2,1)S(1)}, bf16[2048,128]{1,0:T(8,128)(2,1)S(1)}, u32[]{:S(2)}, u32[]{:S(2)}) collective-permute-start(bf16[2048,128]{1,0:T(8,128)(2,1)S(1)} %get-tuple-element.25), channel_id=1, source_target_pairs={{0,8},{4,12},{24,16},{28,20},{1,9},{5,13},{25,17},{29,21},{2,10},{... | collective-permute-start | bytes 1572872 | tf_op jit(solution)/shard_map/ppermute | solution.py:260
  7.0 0.7 collective-permute-start.3
  7.7 4.0 %collective-permute-start.10 = (bf16[2048,128]{1,0:T(8,128)(2,1)S(1)}, bf16[2048,128]{1,0:T(8,128)(2,1)S(1)}, u32[]{:S(2)}, u32[]{:S(2)}) collective-permute-start(bf16[2048,128]{1,0:T(8,128)(2,1)S(1)} %get-tuple-element.23.piece_ref), channel_id=1, source_target_pairs={{24,8},{28,12},{0,16},{4,20},{25,9},{29,13},{1,17},{5,21},{26,10},... | collective-permute-start | bytes 1572872 | tf_op jit(solution)/shard_map/ppermute | solution.py:260
  11.7 0.1 collective-permute-start.4
  11.8 7.5 %collective-permute-done.2.refs_1_ = bf16[2048,128]{1,0:T(8,128)(2,1)S(1)} collective-permute-done((bf16[2048,128]{1,0:T(8,128)(2,1)S(1)}, bf16[2048,128]{1,0:T(8,128)(2,1)S(1)}, u32[]{:S(2)}, u32[]{:S(2)}) %collective-permute-start.2) | collective-permute-done | bytes 524320 | tf_op jit(solution)/shard_map/ppermute | solution.py:260
  19.3 0.0 collective-permute-start.5
  19.3 0.0 collective-permute-done.3.refs_2_
  19.3 0.5 collective-permute-start.6
  19.8 9.6 %collective-permute-done.10.same_ref = bf16[2048,128]{1,0:T(8,128)(2,1)S(1)} collective-permute-done((bf16[2048,128]{1,0:T(8,128)(2,1)S(1)}, bf16[2048,128]{1,0:T(8,128)(2,1)S(1)}, u32[]{:S(2)}, u32[]{:S(2)}) %collective-permute-start.10) | collective-permute-done | bytes 524320 | tf_op jit(solution)/shard_map/ppermute | solution.py:260
  29.5 0.2 shard_map.31
  29.7 5.3 %collective-permute-start = (f32[16,128]{1,0:T(8,128)S(1)}, f32[16,128]{1,0:T(8,128)S(1)}, u32[]{:S(2)}, u32[]{:S(2)}) collective-permute-start(f32[16,128]{1,0:T(8,128)S(1)} %shard_map.31), channel_id=1, source_target_pairs={{24,8},{28,12},{0,16},{4,20},{8,0},{12,4},{16,24},{20,28},{25,9},{... | collective-permute-start | bytes 24584 | tf_op jit(solution)/shard_map/ppermute | solution.py:260
  35.0 1.4 %collective-permute-done.late_same_ref = f32[16,128]{1,0:T(8,128)S(1)} collective-permute-done((f32[16,128]{1,0:T(8,128)S(1)}, f32[16,128]{1,0:T(8,128)S(1)}, u32[]{:S(2)}, u32[]{:S(2)}) %collective-permute-start) | collective-permute-done | bytes 8224 | tf_op jit(solution)/shard_map/ppermute | solution.py:260
  36.4 1.2 %collective-permute-done.1.late_other_ref = f32[16,128]{1,0:T(8,128)S(1)} collective-permute-done((f32[16,128]{1,0:T(8,128)S(1)}, f32[16,128]{1,0:T(8,128)S(1)}, u32[]{:S(2)}, u32[]{:S(2)}) %collective-permute-start.1) | collective-permute-done | bytes 8224 | tf_op jit(solution)/shard_map/ppermute | solution.py:263
  37.5 7.3 %shard_map.32 = (bf16[768,2048]{1,0:T(8,128)(2,1)S(1)}, f32[16,128]{1,0:T(8,128)S(1)}, f32[2048,128]{1,0:T(8,128)S(1)}, f32[12,32,128]{2,1,0:T(8,128)S(1)}, f32[...) custom-call(f32[16,128]{1,0:T(8,128)S(1)} %collective-permute-done.late_same_ref, ...), custom_call_target="tpu_custom_call" | custom-call | flops 1207959552 | tf_op jit(solution)/shard_map/pallas_call | solution.py:244
  44.9 3.3 %shard_map.33 = (f32[9,32,128]{2,1,0:T(8,128)S(1)}, f32[9,32,128]{2,1,0:T(8,128)S(1)}, f32[9,32,128]{2,1,0:T(8,128)S(1)}, f32[9,32,128]{2,1,0:T(8,128)S(1)}) custom-call(f32[2048,128]{1,0:T(8,128)S(1)} %get-tuple-element.32.spread_ref, bf16[2048,128]{1,0:T(8,128)(2,1)S(1)} %collective-permute-done.10.same_ref, ...), custom_call_target="tpu_custom_call" | custom-call | flops 1073741824 | tf_op jit(solution)/shard_map/pallas_call | solution.py:244
  48.2 1.6 %collective-permute-start.12 = (f32[9,32,128]{2,1,0:T(8,128)S(1)}, f32[9,32,128]{2,1,0:T(8,128)S(1)}, u32[]{:S(2)}, u32[]{:S(2)}) collective-permute-start(f32[9,32,128]{2,1,0:T(8,128)S(1)} %get-tuple-element.35), channel_id=1, source_target_pairs={{0,1},{1,0},{2,3},{3,2},{4,5},{5,4},{6,7},{7,6},{8,9},{9,8},{10,11... | collective-permute-start | bytes 442376 | tf_op jit(solution)/shard_map/ppermute | solution.py:307
  49.8 0.5 collective-permute-start.7
  50.3 1.5 %collective-permute-start.8 = (f32[12,32,128]{2,1,0:T(8,128)S(1)}, f32[12,32,128]{2,1,0:T(8,128)S(1)}, u32[]{:S(2)}, u32[]{:S(2)}) collective-permute-start(f32[12,32,128]{2,1,0:T(8,128)S(1)} %get-tuple-element.30), channel_id=1, source_target_pairs={{0,2},{1,3},{2,0},{3,1},{4,6},{5,7},{6,4},{7,5},{8,10},{9,11},{10,... | collective-permute-start | bytes 589832 | tf_op jit(solution)/shard_map/ppermute | solution.py:307
  51.8 1.4 %collective-permute-start.9 = (f32[12,32,128]{2,1,0:T(8,128)S(1)}, f32[12,32,128]{2,1,0:T(8,128)S(1)}, u32[]{:S(2)}, u32[]{:S(2)}) collective-permute-start(f32[12,32,128]{2,1,0:T(8,128)S(1)} %get-tuple-element.31), channel_id=1, source_target_pairs={{0,3},{1,2},{2,1},{3,0},{4,7},{5,6},{6,5},{7,4},{8,11},{9,10},{10,... | collective-permute-start | bytes 589832 | tf_op jit(solution)/shard_map/ppermute | solution.py:307
  53.3 1.5 %collective-permute-start.13 = (f32[9,32,128]{2,1,0:T(8,128)S(1)}, f32[9,32,128]{2,1,0:T(8,128)S(1)}, u32[]{:S(2)}, u32[]{:S(2)}) collective-permute-start(f32[9,32,128]{2,1,0:T(8,128)S(1)} %get-tuple-element.36), channel_id=1, source_target_pairs={{0,2},{1,3},{2,0},{3,1},{4,6},{5,7},{6,4},{7,5},{8,10},{9,11},{10,... | collective-permute-start | bytes 442376 | tf_op jit(solution)/shard_map/ppermute | solution.py:307
  54.8 0.2 collective-permute-done.12.refs_5_
  55.0 2.4 %collective-permute-start.14 = (f32[9,32,128]{2,1,0:T(8,128)S(1)}, f32[9,32,128]{2,1,0:T(8,128)S(1)}, u32[]{:S(2)}, u32[]{:S(2)}) collective-permute-start(f32[9,32,128]{2,1,0:T(8,128)S(1)} %get-tuple-element.37), channel_id=1, source_target_pairs={{0,3},{1,2},{2,1},{3,0},{4,7},{5,6},{6,5},{7,4},{8,11},{9,10},{10,... | collective-permute-start | bytes 442376 | tf_op jit(solution)/shard_map/ppermute | solution.py:307
  57.4 9.8 %collective-permute-done.13.refs_6_ = f32[9,32,128]{2,1,0:T(8,128)S(1)} collective-permute-done((f32[9,32,128]{2,1,0:T(8,128)S(1)}, f32[9,32,128]{2,1,0:T(8,128)S(1)}, u32[]{:S(2)}, u32[]{:S(2)}) %collective-permute-start.13) | collective-permute-done | bytes 147488 | tf_op jit(solution)/shard_map/ppermute | solution.py:307
  67.3 0.4 shard_map.34
  67.7 2.2 %collective-permute-start.15 = (f32[40,640]{1,0:T(8,128)S(1)}, f32[40,640]{1,0:T(8,128)S(1)}, u32[]{:S(2)}, u32[]{:S(2)}) collective-permute-start(f32[40,640]{1,0:T(8,128)S(1)} %get-tuple-element.39), channel_id=1, source_target_pairs={{8,0},{12,4},{16,24},{20,28},{0,8},{4,12},{24,16},{28,20},{9,1},{1... | collective-permute-start | bytes 307208 | tf_op jit(solution)/shard_map/ppermute | solution.py:321
  69.9 0.1 collective-permute-start.16
  70.0 0.7 collective-permute-start.17
  70.7 3.0 %collective-permute-done.15.refs_0_ = f32[40,640]{1,0:T(8,128)S(1)} collective-permute-done((f32[40,640]{1,0:T(8,128)S(1)}, f32[40,640]{1,0:T(8,128)S(1)}, u32[]{:S(2)}, u32[]{:S(2)}) %collective-permute-start.15) | collective-permute-done | bytes 102432 | tf_op jit(solution)/shard_map/ppermute | solution.py:321
  73.7 2.2 %collective-permute-done.16.refs_1_ = f32[40,640]{1,0:T(8,128)S(1)} collective-permute-done((f32[40,640]{1,0:T(8,128)S(1)}, f32[40,640]{1,0:T(8,128)S(1)}, u32[]{:S(2)}, u32[]{:S(2)}) %collective-permute-start.16) | collective-permute-done | bytes 102432 | tf_op jit(solution)/shard_map/ppermute | solution.py:321
  75.8 0.7 shard_map.35
  (12 shorter events, 0.0 us)
Async XLA Ops:
  0.6 1.2 %copy-start = (bf16[4096,128]{1,0:T(8,128)(2,1)S(1)}, bf16[4096,128]{1,0:T(8,128)(2,1)}, u32[]{:S(2)}) copy-start(bf16[4096,128]{1,0:T(8,128)(2,1)} %rows_ref.1) | copy-start | bytes 3145732
  2.0 17.3 %collective-permute-start.2 = (bf16[2048,128]{1,0:T(8,128)(2,1)S(1)}, bf16[2048,128]{1,0:T(8,128)(2,1)S(1)}, u32[]{:S(2)}, u32[]{:S(2)}) collective-permute-start(bf16[2048,128]{1,0:T(8,128)(2,1)S(1)} %get-tuple-element.25), channel_id=1, source_target_pairs={{0,8},{4,12},{24,16},{28,20},{1,9},{5,13},{25,17},{29,21},{2,10},{... | collective-permute-start | bytes 1572872 | tf_op jit(solution)/shard_map/ppermute | solution.py:260
  7.0 12.3 %collective-permute-start.3 = (bf16[2048,128]{1,0:T(8,128)(2,1)S(1)}, bf16[2048,128]{1,0:T(8,128)(2,1)S(1)}, u32[]{:S(2)}, u32[]{:S(2)}) collective-permute-start(bf16[2048,128]{1,0:T(8,128)(2,1)S(1)} %get-tuple-element.26), channel_id=1, source_target_pairs={{16,8},{20,12},{8,16},{12,20},{0,0},{4,4},{24,24},{28,28},{17,9},{... | collective-permute-start | bytes 1572872 | tf_op jit(solution)/shard_map/ppermute | solution.py:260
  7.7 21.7 %collective-permute-start.10 = (bf16[2048,128]{1,0:T(8,128)(2,1)S(1)}, bf16[2048,128]{1,0:T(8,128)(2,1)S(1)}, u32[]{:S(2)}, u32[]{:S(2)}) collective-permute-start(bf16[2048,128]{1,0:T(8,128)(2,1)S(1)} %get-tuple-element.23.piece_ref), channel_id=1, source_target_pairs={{24,8},{28,12},{0,16},{4,20},{25,9},{29,13},{1,17},{5,21},{26,10},... | collective-permute-start | bytes 1572872 | tf_op jit(solution)/shard_map/ppermute | solution.py:260
  11.7 25.8 %collective-permute-start.4 = (bf16[2048,128]{1,0:T(8,128)(2,1)S(1)}, bf16[2048,128]{1,0:T(8,128)(2,1)S(1)}, u32[]{:S(2)}, u32[]{:S(2)}) collective-permute-start(bf16[2048,128]{1,0:T(8,128)(2,1)S(1)} %get-tuple-element.24.refs_0_), channel_id=1, source_target_pairs={{0,4},{4,0},{8,12},{12,8},{16,20},{20,16},{24,28},{28,24},{1,5},{5... | collective-permute-start | bytes 1572872 | tf_op jit(solution)/shard_map/ppermute | solution.py:263
  19.3 18.2 %collective-permute-start.5 = (bf16[2048,128]{1,0:T(8,128)(2,1)S(1)}, bf16[2048,128]{1,0:T(8,128)(2,1)S(1)}, u32[]{:S(2)}, u32[]{:S(2)}) collective-permute-start(bf16[2048,128]{1,0:T(8,128)(2,1)S(1)} %collective-permute-done.2.refs_1_), channel_id=1, source_target_pairs={{0,4},{4,0},{8,12},{12,8},{16,20},{20,16},{24,28},{28,24},{1,5},{5... | collective-permute-start | bytes 1572872 | tf_op jit(solution)/shard_map/ppermute | solution.py:263
  19.3 18.2 %collective-permute-start.6 = (bf16[2048,128]{1,0:T(8,128)(2,1)S(1)}, bf16[2048,128]{1,0:T(8,128)(2,1)S(1)}, u32[]{:S(2)}, u32[]{:S(2)}) collective-permute-start(bf16[2048,128]{1,0:T(8,128)(2,1)S(1)} %collective-permute-done.3.refs_2_), channel_id=1, source_target_pairs={{0,4},{4,0},{8,12},{12,8},{16,20},{20,16},{24,28},{28,24},{1,5},{5... | collective-permute-start | bytes 1572872 | tf_op jit(solution)/shard_map/ppermute | solution.py:263
  29.5 15.4 %collective-permute-start.11 = (bf16[2048,128]{1,0:T(8,128)(2,1)S(1)}, bf16[2048,128]{1,0:T(8,128)(2,1)S(1)}, u32[]{:S(2)}, u32[]{:S(2)}) collective-permute-start(bf16[2048,128]{1,0:T(8,128)(2,1)S(1)} %collective-permute-done.10.same_ref), channel_id=1, source_target_pairs={{0,4},{4,0},{8,12},{12,8},{16,20},{20,16},{24,28},{28,24},{1,5},{5... | collective-permute-start | bytes 1572872 | tf_op jit(solution)/shard_map/ppermute | solution.py:263
  29.7 6.7 %collective-permute-start = (f32[16,128]{1,0:T(8,128)S(1)}, f32[16,128]{1,0:T(8,128)S(1)}, u32[]{:S(2)}, u32[]{:S(2)}) collective-permute-start(f32[16,128]{1,0:T(8,128)S(1)} %shard_map.31), channel_id=1, source_target_pairs={{24,8},{28,12},{0,16},{4,20},{8,0},{12,4},{16,24},{20,28},{25,9},{... | collective-permute-start | bytes 24584 | tf_op jit(solution)/shard_map/ppermute | solution.py:260
  36.4 1.2 %collective-permute-start.1 = (f32[16,128]{1,0:T(8,128)S(1)}, f32[16,128]{1,0:T(8,128)S(1)}, u32[]{:S(2)}, u32[]{:S(2)}) collective-permute-start(f32[16,128]{1,0:T(8,128)S(1)} %collective-permute-done.late_same_ref), channel_id=1, source_target_pairs={{0,4},{4,0},{8,12},{12,8},{16,20},{20,16},{24,28},{28,24},{1,5},{5... | collective-permute-start | bytes 24584 | tf_op jit(solution)/shard_map/ppermute | solution.py:263
  48.2 6.8 %collective-permute-start.12 = (f32[9,32,128]{2,1,0:T(8,128)S(1)}, f32[9,32,128]{2,1,0:T(8,128)S(1)}, u32[]{:S(2)}, u32[]{:S(2)}) collective-permute-start(f32[9,32,128]{2,1,0:T(8,128)S(1)} %get-tuple-element.35), channel_id=1, source_target_pairs={{0,1},{1,0},{2,3},{3,2},{4,5},{5,4},{6,7},{7,6},{8,9},{9,8},{10,11... | collective-permute-start | bytes 442376 | tf_op jit(solution)/shard_map/ppermute | solution.py:307
  49.8 17.5 %collective-permute-start.7 = (f32[12,32,128]{2,1,0:T(8,128)S(1)}, f32[12,32,128]{2,1,0:T(8,128)S(1)}, u32[]{:S(2)}, u32[]{:S(2)}) collective-permute-start(f32[12,32,128]{2,1,0:T(8,128)S(1)} %get-tuple-element.29), channel_id=1, source_target_pairs={{0,1},{1,0},{2,3},{3,2},{4,5},{5,4},{6,7},{7,6},{8,9},{9,8},{10,11... | collective-permute-start | bytes 589832 | tf_op jit(solution)/shard_map/ppermute | solution.py:307
  50.3 17.0 %collective-permute-start.8 = (f32[12,32,128]{2,1,0:T(8,128)S(1)}, f32[12,32,128]{2,1,0:T(8,128)S(1)}, u32[]{:S(2)}, u32[]{:S(2)}) collective-permute-start(f32[12,32,128]{2,1,0:T(8,128)S(1)} %get-tuple-element.30), channel_id=1, source_target_pairs={{0,2},{1,3},{2,0},{3,1},{4,6},{5,7},{6,4},{7,5},{8,10},{9,11},{10,... | collective-permute-start | bytes 589832 | tf_op jit(solution)/shard_map/ppermute | solution.py:307
  51.8 15.4 %collective-permute-start.9 = (f32[12,32,128]{2,1,0:T(8,128)S(1)}, f32[12,32,128]{2,1,0:T(8,128)S(1)}, u32[]{:S(2)}, u32[]{:S(2)}) collective-permute-start(f32[12,32,128]{2,1,0:T(8,128)S(1)} %get-tuple-element.31), channel_id=1, source_target_pairs={{0,3},{1,2},{2,1},{3,0},{4,7},{5,6},{6,5},{7,4},{8,11},{9,10},{10,... | collective-permute-start | bytes 589832 | tf_op jit(solution)/shard_map/ppermute | solution.py:307
  53.3 14.0 %collective-permute-start.13 = (f32[9,32,128]{2,1,0:T(8,128)S(1)}, f32[9,32,128]{2,1,0:T(8,128)S(1)}, u32[]{:S(2)}, u32[]{:S(2)}) collective-permute-start(f32[9,32,128]{2,1,0:T(8,128)S(1)} %get-tuple-element.36), channel_id=1, source_target_pairs={{0,2},{1,3},{2,0},{3,1},{4,6},{5,7},{6,4},{7,5},{8,10},{9,11},{10,... | collective-permute-start | bytes 442376 | tf_op jit(solution)/shard_map/ppermute | solution.py:307
  55.0 12.3 %collective-permute-start.14 = (f32[9,32,128]{2,1,0:T(8,128)S(1)}, f32[9,32,128]{2,1,0:T(8,128)S(1)}, u32[]{:S(2)}, u32[]{:S(2)}) collective-permute-start(f32[9,32,128]{2,1,0:T(8,128)S(1)} %get-tuple-element.37), channel_id=1, source_target_pairs={{0,3},{1,2},{2,1},{3,0},{4,7},{5,6},{6,5},{7,4},{8,11},{9,10},{10,... | collective-permute-start | bytes 442376 | tf_op jit(solution)/shard_map/ppermute | solution.py:307
  67.7 6.0 %collective-permute-start.15 = (f32[40,640]{1,0:T(8,128)S(1)}, f32[40,640]{1,0:T(8,128)S(1)}, u32[]{:S(2)}, u32[]{:S(2)}) collective-permute-start(f32[40,640]{1,0:T(8,128)S(1)} %get-tuple-element.39), channel_id=1, source_target_pairs={{8,0},{12,4},{16,24},{20,28},{0,8},{4,12},{24,16},{28,20},{9,1},{1... | collective-permute-start | bytes 307208 | tf_op jit(solution)/shard_map/ppermute | solution.py:321
  69.9 5.9 %collective-permute-start.16 = (f32[40,640]{1,0:T(8,128)S(1)}, f32[40,640]{1,0:T(8,128)S(1)}, u32[]{:S(2)}, u32[]{:S(2)}) collective-permute-start(f32[40,640]{1,0:T(8,128)S(1)} %get-tuple-element.40), channel_id=1, source_target_pairs={{8,24},{12,28},{16,0},{20,4},{0,8},{4,12},{24,16},{28,20},{9,25},{... | collective-permute-start | bytes 307208 | tf_op jit(solution)/shard_map/ppermute | solution.py:321
  70.0 5.8 %collective-permute-start.17 = (f32[40,640]{1,0:T(8,128)S(1)}, f32[40,640]{1,0:T(8,128)S(1)}, u32[]{:S(2)}, u32[]{:S(2)}) collective-permute-start(f32[40,640]{1,0:T(8,128)S(1)} %get-tuple-element.41), channel_id=1, source_target_pairs={{8,16},{12,20},{16,8},{20,12},{0,0},{4,4},{24,24},{28,28},{9,17},{... | collective-permute-start | bytes 307208 | tf_op jit(solution)/shard_map/ppermute | solution.py:321

commit v4 on v3

--- a/solution.py
+++ b/solution.py
@@ -1,4 +1,5 @@
 import functools
+import math
 
 import jax
 import jax.numpy as jnp
@@ -67,6 +68,17 @@
     return lax.dot_general(left, right, (((1,), (0,)), ((), ())), preferred_element_type=jnp.float32)
 
 
+def over_tiles(count, one_tile):
+    group = math.gcd(count, 4)
+
+    def some(step, carry):
+        for n in range(group):
+            one_tile(step * group + n)
+        return carry
+
+    lax.fori_loop(0, count // group, some, 0)
+
+
 def split_kernel(hub_of, offsets, rows_ref, *refs):
     pieces, sems = refs[:-1], refs[-1]
     me = lax.axis_index("snap")
@@ -92,7 +104,7 @@
     fluct_ref, tiles_ref = refs[-2:]
     rows, width = blocks[0].shape
 
-    def one_tile(tile, carry):
+    def one_tile(tile):
         target = pl.ds(pl.multiple_of(tile * LANES, LANES), LANES)
         held = [ref[target, :].astype(jnp.float32) for ref in blocks]
         near_sum = jnp.sum(jnp.transpose(functools.reduce(jnp.add, held)), axis=0, keepdims=True)
@@ -105,9 +117,8 @@
             value = (held[n] - mean).astype(jnp.bfloat16)
             fluct_ref[target, n * width : (n + 1) * width] = value
             turned_ref[n * width : (n + 1) * width, target] = jnp.transpose(value)
-        return carry
-
-    lax.fori_loop(0, rows // LANES, one_tile, 0)
+
+    over_tiles(rows // LANES, one_tile)
     half = near // 2
     for first in range(0, near * width, 2 * width):
         columns = slice(first, min(first + 2 * width, near * width))
@@ -128,16 +139,15 @@
     out_refs, (fluct_ref, far_turned_ref, tiles_ref) = refs[:-3], refs[-3:]
     rows, width = same_ref.shape
 
-    def one_tile(tile, carry):
+    def one_tile(tile):
         target = pl.ds(pl.multiple_of(tile * LANES, LANES), LANES)
         mean = spread_ref[target, :]
         for n, ref in enumerate((same_ref, other_ref)):
             value = (ref[target, :].astype(jnp.float32) - mean).astype(jnp.bfloat16)
             fluct_ref[target, n * width : (n + 1) * width] = value
             far_turned_ref[n * width : (n + 1) * width, target] = jnp.transpose(value)
-        return carry
-
-    lax.fori_loop(0, rows // LANES, one_tile, 0)
+
+    over_tiles(rows // LANES, one_tile)
     half = near // 2
     step = half * width
     for first in range(0, near * width, step):
@@ -267,7 +277,7 @@
     offsets = early + [late]
     pieces = kernel(
         functools.partial(split_kernel, hub_of, offsets),
-        [snapshots],
+        [pltpu.with_memory_space_constraint(snapshots, pltpu.HBM)],
         [piece] * chip_count,
         [pltpu.SemaphoreType.DMA((chip_count,))],
         raw=True,

time: 77.3 us -> 75.4 us (0.975)
  local copies, waits for them, and re-layouts: 1.22 us -> 0 us
    unnamed x2 -> x0, local copies, waits for them, and re-layouts: 1.22 us -> none
  transfers between devices with their start and end apart: 18 -> 18, of which waited for: 8 -> 8; matrix products, arithmetic and copies ran while one was open for 0% -> 0% of each run, Pallas kernels for 10% -> 8%
where the time goes in v4:
time: 75.4 us; the launch traced here: 74.6 us
  waiting for transfers between devices  34.9 us (46%)
  starting transfers between devices  27.5 us (36%)
  Pallas kernels  11.5 us (15%)
    ppermute x4, waiting for transfers between devices, to_hubs(): lax.ppermute(x, 'snap', completed(pairs, snap_count) if full else pairs)  18.5 us
    ppermute x4, starting transfers between devices, to_hubs(): lax.ppermute(x, 'snap', completed(pairs, snap_count) if full else pairs)  15 us
    pallas_call x6, Pallas kernels, kernel(): pl.pallas_call(body, out_shape=list(out_shapes), in_specs=[pl.BlockSpec(m...  11.5 us
    ppermute x6, waiting for transfers between devices, over_space(): lax.ppermute(parts[n], 'space', [(s, s ^ n) for s in range(space_count)])  10 us
    ppermute x6, starting transfers between devices, over_space(): lax.ppermute(parts[n], 'space', [(s, s ^ n) for s in range(space_count)])  9.01 us
    ppermute x3, waiting for transfers between devices, per_device(): own.append(lax.ppermute(slabs[offset], 'snap', pairs))  5.18 us
    ppermute x3, starting transfers between devices, per_device(): own.append(lax.ppermute(slabs[offset], 'snap', pairs))  2.96 us
  transfers between devices with their start and end apart: 18, of which 8 were waited for; matrix products, arithmetic and copies ran while one was open for 0% of the time, Pallas kernels for 8%

profile of v4, /device:TPU:0, one launch (start us, length us, event | category | flops | bytes accessed | tf_op | source)
XLA Modules:
  0.0 74.6 jit_solution(12496941847739545901)
XLA Ops:
  0.6 1.6 %shard_map.30 = (bf16[2048,128]{1,0:T(8,128)(2,1)S(1)}, bf16[2048,128]{1,0:T(8,128)(2,1)S(1)}, bf16[2048,128]{1,0:T(8,128)(2,1)S(1)}, bf16[2048,128]{1,0:T(8,128)(2,1)S(1)}) custom-call(bf16[4096,128]{1,0:T(8,128)(2,1)} %rows_ref.1), custom_call_target="tpu_custom_call" | custom-call | flops 1000 | tf_op jit(solution)/shard_map/pallas_call | solution.py:254
  2.2 5.0 %collective-permute-start.2 = (bf16[2048,128]{1,0:T(8,128)(2,1)S(1)}, bf16[2048,128]{1,0:T(8,128)(2,1)S(1)}, u32[]{:S(2)}, u32[]{:S(2)}) collective-permute-start(bf16[2048,128]{1,0:T(8,128)(2,1)S(1)} %get-tuple-element.25), channel_id=1, source_target_pairs={{0,8},{4,12},{24,16},{28,20},{1,9},{5,13},{25,17},{29,21},{2,10},{... | collective-permute-start | bytes 1572872 | tf_op jit(solution)/shard_map/ppermute | solution.py:270
  7.2 0.7 collective-permute-start.3
  7.9 4.0 %collective-permute-start.10 = (bf16[2048,128]{1,0:T(8,128)(2,1)S(1)}, bf16[2048,128]{1,0:T(8,128)(2,1)S(1)}, u32[]{:S(2)}, u32[]{:S(2)}) collective-permute-start(bf16[2048,128]{1,0:T(8,128)(2,1)S(1)} %get-tuple-element.23.piece_ref), channel_id=1, source_target_pairs={{24,8},{28,12},{0,16},{4,20},{25,9},{29,13},{1,17},{5,21},{26,10},... | collective-permute-start | bytes 1572872 | tf_op jit(solution)/shard_map/ppermute | solution.py:270
  11.9 0.1 collective-permute-start.4
  12.0 7.5 %collective-permute-done.2.refs_1_ = bf16[2048,128]{1,0:T(8,128)(2,1)S(1)} collective-permute-done((bf16[2048,128]{1,0:T(8,128)(2,1)S(1)}, bf16[2048,128]{1,0:T(8,128)(2,1)S(1)}, u32[]{:S(2)}, u32[]{:S(2)}) %collective-permute-start.2) | collective-permute-done | bytes 524320 | tf_op jit(solution)/shard_map/ppermute | solution.py:270
  19.5 0.0 collective-permute-start.5
  19.5 0.0 collective-permute-done.3.refs_2_
  19.5 0.5 collective-permute-start.6
  20.0 9.6 %collective-permute-done.10.same_ref = bf16[2048,128]{1,0:T(8,128)(2,1)S(1)} collective-permute-done((bf16[2048,128]{1,0:T(8,128)(2,1)S(1)}, bf16[2048,128]{1,0:T(8,128)(2,1)S(1)}, u32[]{:S(2)}, u32[]{:S(2)}) %collective-permute-start.10) | collective-permute-done | bytes 524320 | tf_op jit(solution)/shard_map/ppermute | solution.py:270
  29.6 0.2 shard_map.31
  29.8 5.3 %collective-permute-start = (f32[16,128]{1,0:T(8,128)S(1)}, f32[16,128]{1,0:T(8,128)S(1)}, u32[]{:S(2)}, u32[]{:S(2)}) collective-permute-start(f32[16,128]{1,0:T(8,128)S(1)} %shard_map.31), channel_id=1, source_target_pairs={{24,8},{28,12},{0,16},{4,20},{8,0},{12,4},{16,24},{20,28},{25,9},{... | collective-permute-start | bytes 24584 | tf_op jit(solution)/shard_map/ppermute | solution.py:270
  35.1 1.4 %collective-permute-done.late_same_ref = f32[16,128]{1,0:T(8,128)S(1)} collective-permute-done((f32[16,128]{1,0:T(8,128)S(1)}, f32[16,128]{1,0:T(8,128)S(1)}, u32[]{:S(2)}, u32[]{:S(2)}) %collective-permute-start) | collective-permute-done | bytes 8224 | tf_op jit(solution)/shard_map/ppermute | solution.py:270
  36.5 1.2 %collective-permute-done.1.late_other_ref = f32[16,128]{1,0:T(8,128)S(1)} collective-permute-done((f32[16,128]{1,0:T(8,128)S(1)}, f32[16,128]{1,0:T(8,128)S(1)}, u32[]{:S(2)}, u32[]{:S(2)}) %collective-permute-start.1) | collective-permute-done | bytes 8224 | tf_op jit(solution)/shard_map/ppermute | solution.py:273
  37.7 0.0 collective-permute-done.4.refs_3_
  37.7 5.9 %shard_map.32 = (bf16[768,2048]{1,0:T(8,128)(2,1)S(1)}, f32[16,128]{1,0:T(8,128)S(1)}, f32[2048,128]{1,0:T(8,128)S(1)}, f32[12,32,128]{2,1,0:T(8,128)S(1)}, f32[...) custom-call(f32[16,128]{1,0:T(8,128)S(1)} %collective-permute-done.late_same_ref, ...), custom_call_target="tpu_custom_call" | custom-call | flops 1207959552 | tf_op jit(solution)/shard_map/pallas_call | solution.py:254
  43.7 2.7 %shard_map.33 = (f32[9,32,128]{2,1,0:T(8,128)S(1)}, f32[9,32,128]{2,1,0:T(8,128)S(1)}, f32[9,32,128]{2,1,0:T(8,128)S(1)}, f32[9,32,128]{2,1,0:T(8,128)S(1)}) custom-call(f32[2048,128]{1,0:T(8,128)S(1)} %get-tuple-element.32.spread_ref, bf16[2048,128]{1,0:T(8,128)(2,1)S(1)} %collective-permute-done.10.same_ref, ...), custom_call_target="tpu_custom_call" | custom-call | flops 1073741824 | tf_op jit(solution)/shard_map/pallas_call | solution.py:254
  46.3 1.6 %collective-permute-start.12 = (f32[9,32,128]{2,1,0:T(8,128)S(1)}, f32[9,32,128]{2,1,0:T(8,128)S(1)}, u32[]{:S(2)}, u32[]{:S(2)}) collective-permute-start(f32[9,32,128]{2,1,0:T(8,128)S(1)} %get-tuple-element.35), channel_id=1, source_target_pairs={{0,1},{1,0},{2,3},{3,2},{4,5},{5,4},{6,7},{7,6},{8,9},{9,8},{10,11... | collective-permute-start | bytes 442376 | tf_op jit(solution)/shard_map/ppermute | solution.py:317
  47.9 0.5 collective-permute-start.7
  48.4 1.5 %collective-permute-start.8 = (f32[12,32,128]{2,1,0:T(8,128)S(1)}, f32[12,32,128]{2,1,0:T(8,128)S(1)}, u32[]{:S(2)}, u32[]{:S(2)}) collective-permute-start(f32[12,32,128]{2,1,0:T(8,128)S(1)} %get-tuple-element.30), channel_id=1, source_target_pairs={{0,2},{1,3},{2,0},{3,1},{4,6},{5,7},{6,4},{7,5},{8,10},{9,11},{10,... | collective-permute-start | bytes 589832 | tf_op jit(solution)/shard_map/ppermute | solution.py:317
  49.9 1.4 %collective-permute-start.9 = (f32[12,32,128]{2,1,0:T(8,128)S(1)}, f32[12,32,128]{2,1,0:T(8,128)S(1)}, u32[]{:S(2)}, u32[]{:S(2)}) collective-permute-start(f32[12,32,128]{2,1,0:T(8,128)S(1)} %get-tuple-element.31), channel_id=1, source_target_pairs={{0,3},{1,2},{2,1},{3,0},{4,7},{5,6},{6,5},{7,4},{8,11},{9,10},{10,... | collective-permute-start | bytes 589832 | tf_op jit(solution)/shard_map/ppermute | solution.py:317
  51.4 1.5 %collective-permute-start.13 = (f32[9,32,128]{2,1,0:T(8,128)S(1)}, f32[9,32,128]{2,1,0:T(8,128)S(1)}, u32[]{:S(2)}, u32[]{:S(2)}) collective-permute-start(f32[9,32,128]{2,1,0:T(8,128)S(1)} %get-tuple-element.36), channel_id=1, source_target_pairs={{0,2},{1,3},{2,0},{3,1},{4,6},{5,7},{6,4},{7,5},{8,10},{9,11},{10,... | collective-permute-start | bytes 442376 | tf_op jit(solution)/shard_map/ppermute | solution.py:317
  52.9 0.2 collective-permute-done.12.refs_5_
  53.1 2.4 %collective-permute-start.14 = (f32[9,32,128]{2,1,0:T(8,128)S(1)}, f32[9,32,128]{2,1,0:T(8,128)S(1)}, u32[]{:S(2)}, u32[]{:S(2)}) collective-permute-start(f32[9,32,128]{2,1,0:T(8,128)S(1)} %get-tuple-element.37), channel_id=1, source_target_pairs={{0,3},{1,2},{2,1},{3,0},{4,7},{5,6},{6,5},{7,4},{8,11},{9,10},{10,... | collective-permute-start | bytes 442376 | tf_op jit(solution)/shard_map/ppermute | solution.py:317
  55.6 9.8 %collective-permute-done.13.refs_6_ = f32[9,32,128]{2,1,0:T(8,128)S(1)} collective-permute-done((f32[9,32,128]{2,1,0:T(8,128)S(1)}, f32[9,32,128]{2,1,0:T(8,128)S(1)}, u32[]{:S(2)}, u32[]{:S(2)}) %collective-permute-start.13) | collective-permute-done | bytes 147488 | tf_op jit(solution)/shard_map/ppermute | solution.py:317
  65.4 0.4 shard_map.34
  65.8 2.2 %collective-permute-start.15 = (f32[40,640]{1,0:T(8,128)S(1)}, f32[40,640]{1,0:T(8,128)S(1)}, u32[]{:S(2)}, u32[]{:S(2)}) collective-permute-start(f32[40,640]{1,0:T(8,128)S(1)} %get-tuple-element.39), channel_id=1, source_target_pairs={{8,0},{12,4},{16,24},{20,28},{0,8},{4,12},{24,16},{28,20},{9,1},{1... | collective-permute-start | bytes 307208 | tf_op jit(solution)/shard_map/ppermute | solution.py:331
  68.0 0.1 collective-permute-start.16
  68.1 0.7 collective-permute-start.17
  68.8 3.0 %collective-permute-done.15.refs_0_ = f32[40,640]{1,0:T(8,128)S(1)} collective-permute-done((f32[40,640]{1,0:T(8,128)S(1)}, f32[40,640]{1,0:T(8,128)S(1)}, u32[]{:S(2)}, u32[]{:S(2)}) %collective-permute-start.15) | collective-permute-done | bytes 102432 | tf_op jit(solution)/shard_map/ppermute | solution.py:331
  71.8 2.2 %collective-permute-done.16.refs_1_ = f32[40,640]{1,0:T(8,128)S(1)} collective-permute-done((f32[40,640]{1,0:T(8,128)S(1)}, f32[40,640]{1,0:T(8,128)S(1)}, u32[]{:S(2)}, u32[]{:S(2)}) %collective-permute-start.16) | collective-permute-done | bytes 102432 | tf_op jit(solution)/shard_map/ppermute | solution.py:331
  73.9 0.7 shard_map.35
  (10 shorter events, 0.0 us)
Async XLA Ops:
  2.2 17.3 %collective-permute-start.2 = (bf16[2048,128]{1,0:T(8,128)(2,1)S(1)}, bf16[2048,128]{1,0:T(8,128)(2,1)S(1)}, u32[]{:S(2)}, u32[]{:S(2)}) collective-permute-start(bf16[2048,128]{1,0:T(8,128)(2,1)S(1)} %get-tuple-element.25), channel_id=1, source_target_pairs={{0,8},{4,12},{24,16},{28,20},{1,9},{5,13},{25,17},{29,21},{2,10},{... | collective-permute-start | bytes 1572872 | tf_op jit(solution)/shard_map/ppermute | solution.py:270
  7.2 12.3 %collective-permute-start.3 = (bf16[2048,128]{1,0:T(8,128)(2,1)S(1)}, bf16[2048,128]{1,0:T(8,128)(2,1)S(1)}, u32[]{:S(2)}, u32[]{:S(2)}) collective-permute-start(bf16[2048,128]{1,0:T(8,128)(2,1)S(1)} %get-tuple-element.26), channel_id=1, source_target_pairs={{16,8},{20,12},{8,16},{12,20},{0,0},{4,4},{24,24},{28,28},{17,9},{... | collective-permute-start | bytes 1572872 | tf_op jit(solution)/shard_map/ppermute | solution.py:270
  7.9 21.7 %collective-permute-start.10 = (bf16[2048,128]{1,0:T(8,128)(2,1)S(1)}, bf16[2048,128]{1,0:T(8,128)(2,1)S(1)}, u32[]{:S(2)}, u32[]{:S(2)}) collective-permute-start(bf16[2048,128]{1,0:T(8,128)(2,1)S(1)} %get-tuple-element.23.piece_ref), channel_id=1, source_target_pairs={{24,8},{28,12},{0,16},{4,20},{25,9},{29,13},{1,17},{5,21},{26,10},... | collective-permute-start | bytes 1572872 | tf_op jit(solution)/shard_map/ppermute | solution.py:270
  11.9 25.8 %collective-permute-start.4 = (bf16[2048,128]{1,0:T(8,128)(2,1)S(1)}, bf16[2048,128]{1,0:T(8,128)(2,1)S(1)}, u32[]{:S(2)}, u32[]{:S(2)}) collective-permute-start(bf16[2048,128]{1,0:T(8,128)(2,1)S(1)} %get-tuple-element.24.refs_0_), channel_id=1, source_target_pairs={{0,4},{4,0},{8,12},{12,8},{16,20},{20,16},{24,28},{28,24},{1,5},{5... | collective-permute-start | bytes 1572872 | tf_op jit(solution)/shard_map/ppermute | solution.py:273
  19.5 18.2 %collective-permute-start.5 = (bf16[2048,128]{1,0:T(8,128)(2,1)S(1)}, bf16[2048,128]{1,0:T(8,128)(2,1)S(1)}, u32[]{:S(2)}, u32[]{:S(2)}) collective-permute-start(bf16[2048,128]{1,0:T(8,128)(2,1)S(1)} %collective-permute-done.2.refs_1_), channel_id=1, source_target_pairs={{0,4},{4,0},{8,12},{12,8},{16,20},{20,16},{24,28},{28,24},{1,5},{5... | collective-permute-start | bytes 1572872 | tf_op jit(solution)/shard_map/ppermute | solution.py:273
  19.5 18.2 %collective-permute-start.6 = (bf16[2048,128]{1,0:T(8,128)(2,1)S(1)}, bf16[2048,128]{1,0:T(8,128)(2,1)S(1)}, u32[]{:S(2)}, u32[]{:S(2)}) collective-permute-start(bf16[2048,128]{1,0:T(8,128)(2,1)S(1)} %collective-permute-done.3.refs_2_), channel_id=1, source_target_pairs={{0,4},{4,0},{8,12},{12,8},{16,20},{20,16},{24,28},{28,24},{1,5},{5... | collective-permute-start | bytes 1572872 | tf_op jit(solution)/shard_map/ppermute | solution.py:273
  29.6 14.0 %collective-permute-start.11 = (bf16[2048,128]{1,0:T(8,128)(2,1)S(1)}, bf16[2048,128]{1,0:T(8,128)(2,1)S(1)}, u32[]{:S(2)}, u32[]{:S(2)}) collective-permute-start(bf16[2048,128]{1,0:T(8,128)(2,1)S(1)} %collective-permute-done.10.same_ref), channel_id=1, source_target_pairs={{0,4},{4,0},{8,12},{12,8},{16,20},{20,16},{24,28},{28,24},{1,5},{5... | collective-permute-start | bytes 1572872 | tf_op jit(solution)/shard_map/ppermute | solution.py:273
  29.8 6.7 %collective-permute-start = (f32[16,128]{1,0:T(8,128)S(1)}, f32[16,128]{1,0:T(8,128)S(1)}, u32[]{:S(2)}, u32[]{:S(2)}) collective-permute-start(f32[16,128]{1,0:T(8,128)S(1)} %shard_map.31), channel_id=1, source_target_pairs={{24,8},{28,12},{0,16},{4,20},{8,0},{12,4},{16,24},{20,28},{25,9},{... | collective-permute-start | bytes 24584 | tf_op jit(solution)/shard_map/ppermute | solution.py:270
  36.5 1.2 %collective-permute-start.1 = (f32[16,128]{1,0:T(8,128)S(1)}, f32[16,128]{1,0:T(8,128)S(1)}, u32[]{:S(2)}, u32[]{:S(2)}) collective-permute-start(f32[16,128]{1,0:T(8,128)S(1)} %collective-permute-done.late_same_ref), channel_id=1, source_target_pairs={{0,4},{4,0},{8,12},{12,8},{16,20},{20,16},{24,28},{28,24},{1,5},{5... | collective-permute-start | bytes 24584 | tf_op jit(solution)/shard_map/ppermute | solution.py:273
  46.3 6.8 %collective-permute-start.12 = (f32[9,32,128]{2,1,0:T(8,128)S(1)}, f32[9,32,128]{2,1,0:T(8,128)S(1)}, u32[]{:S(2)}, u32[]{:S(2)}) collective-permute-start(f32[9,32,128]{2,1,0:T(8,128)S(1)} %get-tuple-element.35), channel_id=1, source_target_pairs={{0,1},{1,0},{2,3},{3,2},{4,5},{5,4},{6,7},{7,6},{8,9},{9,8},{10,11... | collective-permute-start | bytes 442376 | tf_op jit(solution)/shard_map/ppermute | solution.py:317
  47.9 17.5 %collective-permute-start.7 = (f32[12,32,128]{2,1,0:T(8,128)S(1)}, f32[12,32,128]{2,1,0:T(8,128)S(1)}, u32[]{:S(2)}, u32[]{:S(2)}) collective-permute-start(f32[12,32,128]{2,1,0:T(8,128)S(1)} %get-tuple-element.29), channel_id=1, source_target_pairs={{0,1},{1,0},{2,3},{3,2},{4,5},{5,4},{6,7},{7,6},{8,9},{9,8},{10,11... | collective-permute-start | bytes 589832 | tf_op jit(solution)/shard_map/ppermute | solution.py:317
  48.4 17.0 %collective-permute-start.8 = (f32[12,32,128]{2,1,0:T(8,128)S(1)}, f32[12,32,128]{2,1,0:T(8,128)S(1)}, u32[]{:S(2)}, u32[]{:S(2)}) collective-permute-start(f32[12,32,128]{2,1,0:T(8,128)S(1)} %get-tuple-element.30), channel_id=1, source_target_pairs={{0,2},{1,3},{2,0},{3,1},{4,6},{5,7},{6,4},{7,5},{8,10},{9,11},{10,... | collective-permute-start | bytes 589832 | tf_op jit(solution)/shard_map/ppermute | solution.py:317
  49.9 15.4 %collective-permute-start.9 = (f32[12,32,128]{2,1,0:T(8,128)S(1)}, f32[12,32,128]{2,1,0:T(8,128)S(1)}, u32[]{:S(2)}, u32[]{:S(2)}) collective-permute-start(f32[12,32,128]{2,1,0:T(8,128)S(1)} %get-tuple-element.31), channel_id=1, source_target_pairs={{0,3},{1,2},{2,1},{3,0},{4,7},{5,6},{6,5},{7,4},{8,11},{9,10},{10,... | collective-permute-start | bytes 589832 | tf_op jit(solution)/shard_map/ppermute | solution.py:317
  51.4 14.0 %collective-permute-start.13 = (f32[9,32,128]{2,1,0:T(8,128)S(1)}, f32[9,32,128]{2,1,0:T(8,128)S(1)}, u32[]{:S(2)}, u32[]{:S(2)}) collective-permute-start(f32[9,32,128]{2,1,0:T(8,128)S(1)} %get-tuple-element.36), channel_id=1, source_target_pairs={{0,2},{1,3},{2,0},{3,1},{4,6},{5,7},{6,4},{7,5},{8,10},{9,11},{10,... | collective-permute-start | bytes 442376 | tf_op jit(solution)/shard_map/ppermute | solution.py:317
  53.1 12.2 %collective-permute-start.14 = (f32[9,32,128]{2,1,0:T(8,128)S(1)}, f32[9,32,128]{2,1,0:T(8,128)S(1)}, u32[]{:S(2)}, u32[]{:S(2)}) collective-permute-start(f32[9,32,128]{2,1,0:T(8,128)S(1)} %get-tuple-element.37), channel_id=1, source_target_pairs={{0,3},{1,2},{2,1},{3,0},{4,7},{5,6},{6,5},{7,4},{8,11},{9,10},{10,... | collective-permute-start | bytes 442376 | tf_op jit(solution)/shard_map/ppermute | solution.py:317
  65.8 6.0 %collective-permute-start.15 = (f32[40,640]{1,0:T(8,128)S(1)}, f32[40,640]{1,0:T(8,128)S(1)}, u32[]{:S(2)}, u32[]{:S(2)}) collective-permute-start(f32[40,640]{1,0:T(8,128)S(1)} %get-tuple-element.39), channel_id=1, source_target_pairs={{8,0},{12,4},{16,24},{20,28},{0,8},{4,12},{24,16},{28,20},{9,1},{1... | collective-permute-start | bytes 307208 | tf_op jit(solution)/shard_map/ppermute | solution.py:331
  68.0 5.9 %collective-permute-start.16 = (f32[40,640]{1,0:T(8,128)S(1)}, f32[40,640]{1,0:T(8,128)S(1)}, u32[]{:S(2)}, u32[]{:S(2)}) collective-permute-start(f32[40,640]{1,0:T(8,128)S(1)} %get-tuple-element.40), channel_id=1, source_target_pairs={{8,24},{12,28},{16,0},{20,4},{0,8},{4,12},{24,16},{28,20},{9,25},{... | collective-permute-start | bytes 307208 | tf_op jit(solution)/shard_map/ppermute | solution.py:331
  68.1 5.8 %collective-permute-start.17 = (f32[40,640]{1,0:T(8,128)S(1)}, f32[40,640]{1,0:T(8,128)S(1)}, u32[]{:S(2)}, u32[]{:S(2)}) collective-permute-start(f32[40,640]{1,0:T(8,128)S(1)} %get-tuple-element.41), channel_id=1, source_target_pairs={{8,16},{12,20},{16,8},{20,12},{0,0},{4,4},{24,24},{28,28},{9,17},{... | collective-permute-start | bytes 307208 | tf_op jit(solution)/shard_map/ppermute | solution.py:331

commit v5 on v4

--- a/solution.py
+++ b/solution.py
@@ -175,52 +175,123 @@
     place_tiles(True, tile_of, out_refs)
 
 
-def joined_kernel(space_count, mean_ref, *refs):
-    firsts, seconds, out_refs = refs[:space_count], refs[space_count : 2 * space_count], refs[2 * space_count :]
+def late_rounds(chip_count):
+    snap_count = 2 * chip_count
+    late = chip_count // 2
+    wanted = []
+    for chip in range(chip_count // 4, 3 * chip_count // 4):
+        for offset in range(1, chip_count):
+            counts = []
+            for me in (2 * chip, 2 * chip + 1):
+                block = ((me // 2) ^ offset) * 2 + me % 2
+                rels = [((block + k) % snap_count) ^ me for k in range(chip_count + 1)]
+                counts.append(sum(late in (offset, rel // 2) for rel in rels))
+            if max(counts):
+                wanted.append((-max(counts), chip, chip ^ offset))
+    rounds = []
+    for count, source, target in sorted(wanted):
+        for pairs, _ in rounds:
+            if source not in pairs and target not in pairs.values():
+                pairs[source] = target
+                break
+        else:
+            rounds.append(({source: target}, -count))
+    return rounds
+
+
+def is_far(chip, core, offset, k):
+    snap_count = lax.axis_size("snap")
+    late = snap_count // 4
+    me = chip * 2 + core
+    rel = (((chip ^ offset) * 2 + core + k) % snap_count) ^ me
+    return jnp.logical_or(offset == late, rel // 2 == late)
+
+
+def joined_near_kernel(space_count, mean_ref, *refs):
+    firsts, out_refs = refs[:space_count], refs[space_count:]
     me = lax.axis_index("snap")
-    snap_count = lax.axis_size("snap")
-    chip_count, late = snap_count // 2, snap_count // 4
-    band = chip_count + 1
     _, part_rows, width = firsts[0].shape
+    band = out_refs[0].shape[1] // width
+    slot = 0
     for offset, out_ref in enumerate(out_refs):
-        if offset == 0:
-            first_slot, second_slot = 0, 0
-        block = ((me // 2) ^ offset) * 2 + me % 2
         for k in range(band):
-            rel = ((block + k) % snap_count) ^ me
-            is_late = jnp.logical_or(offset == late, rel // 2 == late)
+            far = is_far(me // 2, me % 2, offset, k)
             lanes = slice(k * width, (k + 1) * width)
 
-            @pl.when(is_late)
-            def _(out_ref=out_ref, lanes=lanes, slot=second_slot):
-                out_ref[0:part_rows, lanes] = functools.reduce(jnp.add, [ref[slot] for ref in seconds])
-
-            @pl.when(jnp.logical_not(is_late))
-            def _(out_ref=out_ref, lanes=lanes, slot=first_slot):
+            @pl.when(far)
+            def _(out_ref=out_ref, lanes=lanes):
+                out_ref[0:part_rows, lanes] = jnp.zeros((part_rows, width), jnp.float32)
+
+            @pl.when(jnp.logical_not(far))
+            def _(out_ref=out_ref, lanes=lanes, slot=slot):
                 out_ref[0:part_rows, lanes] = functools.reduce(jnp.add, [ref[slot] for ref in firsts])
 
-            second_slot = second_slot + jnp.where(is_late, 1, 0)
-            first_slot = first_slot + jnp.where(is_late, 0, 1)
+            slot = slot + jnp.where(far, 0, 1)
         for n in range(mean_ref.shape[0]):
             row = part_rows + n // band
             out_ref[row : row + 1, (n % band) * width : (n % band + 1) * width] = mean_ref[n : n + 1, :]
 
 
-def collected_kernel(first_chip, scale, own_ref, *refs):
-    others, (gram_ref, mean_ref) = refs[:-2], refs[-2:]
-    chip = lax.axis_index("snap") // 2
+def joined_far_kernel(rounds, space_count, *refs):
+    seconds, out_refs = refs[:space_count], refs[space_count:]
+    me = lax.axis_index("snap")
+    chip = me // 2
+    _, _, width = seconds[0].shape
+    chip_count = lax.axis_size("snap") // 2
+    band = chip_count + 1
+    slot = 0
+    for offset in range(chip_count):
+        here = [(0, chip_count)] if offset == 0 else []
+        here += [(n + 1, source) for n, (pairs, _) in enumerate(rounds) for source in pairs if pairs[source] == source ^ offset]
+        place = 0
+        for k in range(band):
+            far = is_far(chip, me % 2, offset, k)
+            for n, source in here:
+                mine = far if source == chip_count else jnp.logical_and(far, chip == source)
+
+                @pl.when(mine)
+                def _(n=n, slot=slot, place=place):
+                    total = functools.reduce(jnp.add, [ref[slot] for ref in seconds])
+                    lanes = pl.ds(pl.multiple_of(place * width, width), width)
+                    out_refs[n][:, lanes] = total
+
+            slot = slot + jnp.where(far, 1, 0)
+            place = place + jnp.where(far, 1, 0)
+
+
+def collected_kernel(first_chip, rounds, scale, *refs):
+    me = lax.axis_index("snap")
+    chip, core = me // 2, me % 2
+    chip_count = lax.axis_size("snap") // 2
+    hub_chips = chip_count // 2
+    nears, fars, (gram_ref, mean_ref) = refs[:chip_count], refs[chip_count:-2], refs[-2:]
     part_rows, columns = gram_ref.shape
-    chip_count = len(others) + 1
-    hub_chips = chip_count // 2
-    slabs = (own_ref, *others)
     total = jnp.zeros((part_rows, columns), jnp.float32)
-    for offset, ref in enumerate(slabs):
+    for offset, ref in enumerate(nears):
         hub = (chip ^ offset) - first_chip
         total = total + jnp.where((hub >= 0) & (hub < hub_chips), ref[0:part_rows, :], 0.0)
     gram_ref[...] = total * scale
+    for n, ref in enumerate(fars):
+        hub = chip - first_chip
+        source = jnp.where((hub >= 0) & (hub < hub_chips), chip, -1)
+        if n:
+            source = -1
+            for a, b in rounds[n - 1][0].items():
+                source = jnp.where(chip == b, a, source)
+        place = 0
+        for k in range(columns // LANES):
+            far = jnp.logical_and(source >= 0, is_far(source, core, source ^ chip, k))
+            lanes = slice(k * LANES, (k + 1) * LANES)
+
+            @pl.when(far)
+            def _(ref=ref, lanes=lanes, place=place):
+                sent = ref[:, pl.ds(pl.multiple_of(place * LANES, LANES), LANES)]
+                gram_ref[:, lanes] = gram_ref[:, lanes] + sent * scale
+
+            place = place + jnp.where(far, 1, 0)
     mean_rows = mean_ref.shape[0] // hub_chips
     band = columns // LANES
-    for offset, ref in enumerate(slabs):
+    for offset, ref in enumerate(nears):
         hub = (chip ^ offset) - first_chip
 
         @pl.when((hub >= 0) & (hub < hub_chips))
@@ -266,7 +337,7 @@
 
     def to_hubs(x, offset, name):
         pairs = [(h ^ (2 * offset), h) for h in hubs]
-        full = name == "sums" or all(h ^ (2 * offset) in hubs for h in hubs)
+        full = name == "sums" or offset != late
         return lax.ppermute(x, "snap", completed(pairs, snap_count) if full else pairs)
 
     def to_other_core(x):
@@ -319,19 +390,27 @@
 
     mean_space = -(-(-(-(rows // LANES) // band)) // 8) * 8
     slab = shaped(jnp.float32, part_rows + mean_space, band * width)
-    slabs = kernel(
-        functools.partial(joined_kernel, space_count),
-        [mean_rows, *over_space(first), *over_space(second)],
-        [slab] * chip_count,
-    )
-
-    own = [slabs[0]]
+    near_slabs = kernel(
+        functools.partial(joined_near_kernel, space_count), [mean_rows, *over_space(first)], [slab] * chip_count
+    )
+
+    nears = [near_slabs[0]]
     for offset in range(1, chip_count):
         pairs = completed([(h, h ^ (2 * offset)) for h in hubs], snap_count)
-        own.append(lax.ppermute(slabs[offset], "snap", pairs))
+        nears.append(lax.ppermute(near_slabs[offset], "snap", pairs))
+    rounds = late_rounds(chip_count)
+    far_slabs = kernel(
+        functools.partial(joined_far_kernel, rounds, space_count),
+        over_space(second),
+        [shaped(jnp.float32, part_rows, count * width) for count in [band] + [count for _, count in rounds]],
+    )
+    fars = [far_slabs[0]]
+    for n, (pairs, _) in enumerate(rounds):
+        devices = [(2 * a + core, 2 * b + core) for a, b in pairs.items() for core in (0, 1)]
+        fars.append(lax.ppermute(far_slabs[n + 1], "snap", completed(devices, snap_count)))
     gram_band, mean_field = kernel(
-        functools.partial(collected_kernel, first_chip, 1.0 / (row_count * space_count)),
-        own,
+        functools.partial(collected_kernel, first_chip, rounds, 1.0 / (row_count * space_count)),
+        nears + fars,
         [shaped(jnp.float32, part_rows, band * width), shaped(jnp.float32, row_count // LANES, LANES)],
     )
     return gram_band, mean_field.reshape(row_count)

time: 75.4 us -> 70.7 us (0.938)
  waiting for transfers between devices: 34.9 us -> 27.2 us
  starting transfers between devices: 27.5 us -> 30.7 us
    ppermute x6, waiting for transfers between devices: 10 us -> 5.33 us  [over_space(): lax.ppermute(parts[n], 'space', [(s, s ^ n) for s in range(space_count)])]
    ppermute x3 -> x5, starting transfers between devices: 2.96 us -> 5.79 us  [the longest x2 2.99 us: per_device(): lax.ppermute(far_slabs[n + 1], 'snap', completed(devices, snap_count))]
    ppermute x4, starting transfers between devices: 15 us -> 16.7 us  [to_hubs(): lax.ppermute(x, 'snap', completed(pairs, snap_count) if full else pairs)]
    ppermute x4, waiting for transfers between devices: 18.5 us -> 16.8 us  [to_hubs(): lax.ppermute(x, 'snap', completed(pairs, snap_count) if full else pairs)]
    ppermute x6, starting transfers between devices: 9.01 us -> 7.61 us  [over_space(): lax.ppermute(parts[n], 'space', [(s, s ^ n) for s in range(space_count)])]
    ppermute x3 -> x5, waiting for transfers between devices: 5.18 us -> 3.89 us  [the longest x2 3.88 us: per_device(): lax.ppermute(far_slabs[n + 1], 'snap', completed(devices, snap_count))]
    pallas_call x6 -> x7, Pallas kernels: 11.5 us -> 11.9 us  [kernel(): pl.pallas_call(body, out_shape=list(out_shapes), in_specs=[pl.BlockSpec(m...]
  transfers between devices with their start and end apart: 18 -> 20, of which waited for: 8 -> 8; matrix products, arithmetic and copies ran while one was open for 0% -> 0% of each run, Pallas kernels for 8% -> 13%
where the time goes in v5:
time: 70.7 us; the launch traced here: 70.5 us
  starting transfers between devices  30.7 us (43%)
  waiting for transfers between devices  27.2 us (38%)
  Pallas kernels  11.9 us (17%)
  between operations  0.74 us (1%)
    ppermute x4, waiting for transfers between devices, to_hubs(): lax.ppermute(x, 'snap', completed(pairs, snap_count) if full else pairs)  16.8 us
    ppermute x4, starting transfers between devices, to_hubs(): lax.ppermute(x, 'snap', completed(pairs, snap_count) if full else pairs)  16.7 us
    pallas_call x7, Pallas kernels, kernel(): pl.pallas_call(body, out_shape=list(out_shapes), in_specs=[pl.BlockSpec(m...  11.9 us
    ppermute x6, starting transfers between devices, over_space(): lax.ppermute(parts[n], 'space', [(s, s ^ n) for s in range(space_count)])  7.61 us
    ppermute x6, waiting for transfers between devices, over_space(): lax.ppermute(parts[n], 'space', [(s, s ^ n) for s in range(space_count)])  5.33 us
    ppermute x2, waiting for transfers between devices, per_device(): lax.ppermute(far_slabs[n + 1], 'snap', completed(devices, snap_count))  3.88 us
    ppermute x2, starting transfers between devices, per_device(): lax.ppermute(far_slabs[n + 1], 'snap', completed(devices, snap_count))  2.99 us
    ppermute x3, starting transfers between devices, per_device(): nears.append(lax.ppermute(near_slabs[offset], 'snap', pairs))  2.8 us
  transfers between devices with their start and end apart: 20, of which 8 were waited for; matrix products, arithmetic and copies ran while one was open for 0% of the time, Pallas kernels for 13%

profile of v5, /device:TPU:0, one launch (start us, length us, event | category | flops | bytes accessed | tf_op | source)
XLA Modules:
  0.0 70.5 jit_solution(11939804327042072058)
XLA Ops:
  0.6 1.6 %shard_map.30 = (bf16[2048,128]{1,0:T(8,128)(2,1)S(1)}, bf16[2048,128]{1,0:T(8,128)(2,1)S(1)}, bf16[2048,128]{1,0:T(8,128)(2,1)S(1)}, bf16[2048,128]{1,0:T(8,128)(2,1)S(1)}) custom-call(bf16[4096,128]{1,0:T(8,128)(2,1)} %rows_ref.1), custom_call_target="tpu_custom_call" | custom-call | flops 1000 | tf_op jit(solution)/shard_map/pallas_call | solution.py:325
  2.2 3.1 %collective-permute-start.2 = (bf16[2048,128]{1,0:T(8,128)(2,1)S(1)}, bf16[2048,128]{1,0:T(8,128)(2,1)S(1)}, u32[]{:S(2)}, u32[]{:S(2)}) collective-permute-start(bf16[2048,128]{1,0:T(8,128)(2,1)S(1)} %get-tuple-element.28), channel_id=1, source_target_pairs={{0,8},{4,12},{24,16},{28,20},{8,0},{12,4},{16,24},{20,28},{1,9},{5... | collective-permute-start | bytes 1572872 | tf_op jit(solution)/shard_map/ppermute | solution.py:341
  5.3 0.7 collective-permute-start.3
  6.0 5.8 %collective-permute-start.13 = (bf16[2048,128]{1,0:T(8,128)(2,1)S(1)}, bf16[2048,128]{1,0:T(8,128)(2,1)S(1)}, u32[]{:S(2)}, u32[]{:S(2)}) collective-permute-start(bf16[2048,128]{1,0:T(8,128)(2,1)S(1)} %get-tuple-element.26.piece_ref), channel_id=1, source_target_pairs={{24,8},{28,12},{0,16},{4,20},{25,9},{29,13},{1,17},{5,21},{26,10},... | collective-permute-start | bytes 1572872 | tf_op jit(solution)/shard_map/ppermute | solution.py:341
  11.8 0.1 collective-permute-start.4
  11.9 5.8 %collective-permute-done.2.refs_1_ = bf16[2048,128]{1,0:T(8,128)(2,1)S(1)} collective-permute-done((bf16[2048,128]{1,0:T(8,128)(2,1)S(1)}, bf16[2048,128]{1,0:T(8,128)(2,1)S(1)}, u32[]{:S(2)}, u32[]{:S(2)}) %collective-permute-start.2) | collective-permute-done | bytes 524320 | tf_op jit(solution)/shard_map/ppermute | solution.py:341
  17.6 0.5 collective-permute-start.6
  18.2 9.6 %collective-permute-done.13.same_ref = bf16[2048,128]{1,0:T(8,128)(2,1)S(1)} collective-permute-done((bf16[2048,128]{1,0:T(8,128)(2,1)S(1)}, bf16[2048,128]{1,0:T(8,128)(2,1)S(1)}, u32[]{:S(2)}, u32[]{:S(2)}) %collective-permute-start.13) | collective-permute-done | bytes 524320 | tf_op jit(solution)/shard_map/ppermute | solution.py:341
  27.8 0.2 shard_map.31
  28.0 7.2 %collective-permute-start = (f32[16,128]{1,0:T(8,128)S(1)}, f32[16,128]{1,0:T(8,128)S(1)}, u32[]{:S(2)}, u32[]{:S(2)}) collective-permute-start(f32[16,128]{1,0:T(8,128)S(1)} %shard_map.31), channel_id=1, source_target_pairs={{24,8},{28,12},{0,16},{4,20},{8,0},{12,4},{16,24},{20,28},{25,9},{... | collective-permute-start | bytes 24584 | tf_op jit(solution)/shard_map/ppermute | solution.py:341
  35.2 1.4 %collective-permute-done.late_same_ref = f32[16,128]{1,0:T(8,128)S(1)} collective-permute-done((f32[16,128]{1,0:T(8,128)S(1)}, f32[16,128]{1,0:T(8,128)S(1)}, u32[]{:S(2)}, u32[]{:S(2)}) %collective-permute-start) | collective-permute-done | bytes 8224 | tf_op jit(solution)/shard_map/ppermute | solution.py:341
  36.6 1.2 %collective-permute-done.1.late_other_ref = f32[16,128]{1,0:T(8,128)S(1)} collective-permute-done((f32[16,128]{1,0:T(8,128)S(1)}, f32[16,128]{1,0:T(8,128)S(1)}, u32[]{:S(2)}, u32[]{:S(2)}) %collective-permute-start.1) | collective-permute-done | bytes 8224 | tf_op jit(solution)/shard_map/ppermute | solution.py:344
  37.8 5.9 %shard_map.32 = (bf16[768,2048]{1,0:T(8,128)(2,1)S(1)}, f32[16,128]{1,0:T(8,128)S(1)}, f32[2048,128]{1,0:T(8,128)S(1)}, f32[12,32,128]{2,1,0:T(8,128)S(1)}, f32[...) custom-call(f32[16,128]{1,0:T(8,128)S(1)} %collective-permute-done.late_same_ref, ...), custom_call_target="tpu_custom_call" | custom-call | flops 1207959552 | tf_op jit(solution)/shard_map/pallas_call | solution.py:325
  43.7 1.6 %collective-permute-start.7 = (f32[12,32,128]{2,1,0:T(8,128)S(1)}, f32[12,32,128]{2,1,0:T(8,128)S(1)}, u32[]{:S(2)}, u32[]{:S(2)}) collective-permute-start(f32[12,32,128]{2,1,0:T(8,128)S(1)} %get-tuple-element.32), channel_id=1, source_target_pairs={{0,1},{1,0},{2,3},{3,2},{4,5},{5,4},{6,7},{7,6},{8,9},{9,8},{10,11... | collective-permute-start | bytes 589832 | tf_op jit(solution)/shard_map/ppermute | solution.py:388
  45.2 1.5 %collective-permute-start.8 = (f32[12,32,128]{2,1,0:T(8,128)S(1)}, f32[12,32,128]{2,1,0:T(8,128)S(1)}, u32[]{:S(2)}, u32[]{:S(2)}) collective-permute-start(f32[12,32,128]{2,1,0:T(8,128)S(1)} %get-tuple-element.33), channel_id=1, source_target_pairs={{0,2},{1,3},{2,0},{3,1},{4,6},{5,7},{6,4},{7,5},{8,10},{9,11},{10,... | collective-permute-start | bytes 589832 | tf_op jit(solution)/shard_map/ppermute | solution.py:388
  46.8 0.5 collective-permute-start.9
  47.3 2.7 %shard_map.34 = (f32[9,32,128]{2,1,0:T(8,128)S(1)}, f32[9,32,128]{2,1,0:T(8,128)S(1)}, f32[9,32,128]{2,1,0:T(8,128)S(1)}, f32[9,32,128]{2,1,0:T(8,128)S(1)}) custom-call(f32[2048,128]{1,0:T(8,128)S(1)} %get-tuple-element.39.spread_ref, bf16[2048,128]{1,0:T(8,128)(2,1)S(1)} %collective-permute-done.13.same_ref, ...), custom_call_target="tpu_custom_call" | custom-call | flops 1073741824 | tf_op jit(solution)/shard_map/pallas_call | solution.py:325
  49.9 1.6 %collective-permute-start.15 = (f32[9,32,128]{2,1,0:T(8,128)S(1)}, f32[9,32,128]{2,1,0:T(8,128)S(1)}, u32[]{:S(2)}, u32[]{:S(2)}) collective-permute-start(f32[9,32,128]{2,1,0:T(8,128)S(1)} %get-tuple-element.42), channel_id=1, source_target_pairs={{0,1},{1,0},{2,3},{3,2},{4,5},{5,4},{6,7},{7,6},{8,9},{9,8},{10,11... | collective-permute-start | bytes 442376 | tf_op jit(solution)/shard_map/ppermute | solution.py:388
  51.5 1.5 %collective-permute-start.16 = (f32[9,32,128]{2,1,0:T(8,128)S(1)}, f32[9,32,128]{2,1,0:T(8,128)S(1)}, u32[]{:S(2)}, u32[]{:S(2)}) collective-permute-start(f32[9,32,128]{2,1,0:T(8,128)S(1)} %get-tuple-element.43), channel_id=1, source_target_pairs={{0,2},{1,3},{2,0},{3,1},{4,6},{5,7},{6,4},{7,5},{8,10},{9,11},{10,... | collective-permute-start | bytes 442376 | tf_op jit(solution)/shard_map/ppermute | solution.py:388
  53.0 1.0 %collective-permute-start.17 = (f32[9,32,128]{2,1,0:T(8,128)S(1)}, f32[9,32,128]{2,1,0:T(8,128)S(1)}, u32[]{:S(2)}, u32[]{:S(2)}) collective-permute-start(f32[9,32,128]{2,1,0:T(8,128)S(1)} %get-tuple-element.44), channel_id=1, source_target_pairs={{0,3},{1,2},{2,1},{3,0},{4,7},{5,6},{6,5},{7,4},{8,11},{9,10},{10,... | collective-permute-start | bytes 442376 | tf_op jit(solution)/shard_map/ppermute | solution.py:388
  54.0 2.3 %collective-permute-done.8.refs_2_ = f32[12,32,128]{2,1,0:T(8,128)S(1)} collective-permute-done((f32[12,32,128]{2,1,0:T(8,128)S(1)}, f32[12,32,128]{2,1,0:T(8,128)S(1)}, u32[]{:S(2)}, u32[]{:S(2)}) %collective-permute-start.8) | collective-permute-done | bytes 196640 | tf_op jit(solution)/shard_map/ppermute | solution.py:388
  56.3 0.5 collective-permute-done.9.refs_3_
  56.7 0.3 shard_map.33
  57.1 2.1 %collective-permute-start.10 = (f32[40,640]{1,0:T(8,128)S(1)}, f32[40,640]{1,0:T(8,128)S(1)}, u32[]{:S(2)}, u32[]{:S(2)}) collective-permute-start(f32[40,640]{1,0:T(8,128)S(1)} %get-tuple-element.36), channel_id=1, source_target_pairs={{8,0},{12,4},{16,24},{20,28},{0,8},{4,12},{24,16},{28,20},{9,1},{1... | collective-permute-start | bytes 307208 | tf_op jit(solution)/shard_map/ppermute | solution.py:400
  59.2 0.1 collective-permute-start.11
  59.2 0.7 collective-permute-start.12
  59.9 2.6 %collective-permute-done.16.refs_2_ = f32[9,32,128]{2,1,0:T(8,128)S(1)} collective-permute-done((f32[9,32,128]{2,1,0:T(8,128)S(1)}, f32[9,32,128]{2,1,0:T(8,128)S(1)}, u32[]{:S(2)}, u32[]{:S(2)}) %collective-permute-start.16) | collective-permute-done | bytes 147488 | tf_op jit(solution)/shard_map/ppermute | solution.py:388
  62.5 0.2 shard_map.35
  62.7 2.3 %collective-permute-start.18 = (f32[32,640]{1,0:T(8,128)S(1)}, f32[32,640]{1,0:T(8,128)S(1)}, u32[]{:S(2)}, u32[]{:S(2)}) collective-permute-start(f32[32,640]{1,0:T(8,128)S(1)} %get-tuple-element.46), channel_id=1, source_target_pairs={{8,24},{12,28},{16,0},{20,4},{0,8},{4,12},{24,16},{28,20},{9,25},{... | collective-permute-start | bytes 245768 | tf_op jit(solution)/shard_map/ppermute | solution.py:410
  65.0 0.7 collective-permute-start.19
  65.7 3.9 %collective-permute-done.18.refs_5_ = f32[32,640]{1,0:T(8,128)S(1)} collective-permute-done((f32[32,640]{1,0:T(8,128)S(1)}, f32[32,640]{1,0:T(8,128)S(1)}, u32[]{:S(2)}, u32[]{:S(2)}) %collective-permute-start.18) | collective-permute-done | bytes 81952 | tf_op jit(solution)/shard_map/ppermute | solution.py:410
  69.6 0.9 %shard_map.36 = (f32[32,640]{1,0:T(8,128)}, f32[32,128]{1,0:T(8,128)}) custom-call(f32[40,640]{1,0:T(8,128)S(1)} %get-tuple-element.35.refs_0_, f32[40,640]{1,0:T(8,128)S(1)} %collective-permute-done.10.refs_1_, f32[40,640]{1,0:T(8,128)S(1)} %collective-permute-done.11.refs_2_, f32[40,640]{1,0:T(8,128)S(1)} %collective-permute-done.12.refs_3_, ...), custom_call_target="tpu_custom_call" | custom-call | flops 1000 | tf_op jit(solution)/shard_map/pallas_call | solution.py:325
  (15 shorter events, 0.0 us)
Async XLA Ops:
  2.2 15.4 %collective-permute-start.2 = (bf16[2048,128]{1,0:T(8,128)(2,1)S(1)}, bf16[2048,128]{1,0:T(8,128)(2,1)S(1)}, u32[]{:S(2)}, u32[]{:S(2)}) collective-permute-start(bf16[2048,128]{1,0:T(8,128)(2,1)S(1)} %get-tuple-element.28), channel_id=1, source_target_pairs={{0,8},{4,12},{24,16},{28,20},{8,0},{12,4},{16,24},{20,28},{1,9},{5... | collective-permute-start | bytes 1572872 | tf_op jit(solution)/shard_map/ppermute | solution.py:341
  5.3 12.3 %collective-permute-start.3 = (bf16[2048,128]{1,0:T(8,128)(2,1)S(1)}, bf16[2048,128]{1,0:T(8,128)(2,1)S(1)}, u32[]{:S(2)}, u32[]{:S(2)}) collective-permute-start(bf16[2048,128]{1,0:T(8,128)(2,1)S(1)} %get-tuple-element.29), channel_id=1, source_target_pairs={{16,8},{20,12},{8,16},{12,20},{0,0},{4,4},{24,24},{28,28},{17,9},{... | collective-permute-start | bytes 1572872 | tf_op jit(solution)/shard_map/ppermute | solution.py:341
  6.0 21.8 %collective-permute-start.13 = (bf16[2048,128]{1,0:T(8,128)(2,1)S(1)}, bf16[2048,128]{1,0:T(8,128)(2,1)S(1)}, u32[]{:S(2)}, u32[]{:S(2)}) collective-permute-start(bf16[2048,128]{1,0:T(8,128)(2,1)S(1)} %get-tuple-element.26.piece_ref), channel_id=1, source_target_pairs={{24,8},{28,12},{0,16},{4,20},{25,9},{29,13},{1,17},{5,21},{26,10},... | collective-permute-start | bytes 1572872 | tf_op jit(solution)/shard_map/ppermute | solution.py:341
  11.8 26.0 %collective-permute-start.4 = (bf16[2048,128]{1,0:T(8,128)(2,1)S(1)}, bf16[2048,128]{1,0:T(8,128)(2,1)S(1)}, u32[]{:S(2)}, u32[]{:S(2)}) collective-permute-start(bf16[2048,128]{1,0:T(8,128)(2,1)S(1)} %get-tuple-element.27.refs_0_), channel_id=1, source_target_pairs={{0,4},{4,0},{8,12},{12,8},{16,20},{20,16},{24,28},{28,24},{1,5},{5... | collective-permute-start | bytes 1572872 | tf_op jit(solution)/shard_map/ppermute | solution.py:344
  17.6 20.1 %collective-permute-start.5 = (bf16[2048,128]{1,0:T(8,128)(2,1)S(1)}, bf16[2048,128]{1,0:T(8,128)(2,1)S(1)}, u32[]{:S(2)}, u32[]{:S(2)}) collective-permute-start(bf16[2048,128]{1,0:T(8,128)(2,1)S(1)} %collective-permute-done.2.refs_1_), channel_id=1, source_target_pairs={{0,4},{4,0},{8,12},{12,8},{16,20},{20,16},{24,28},{28,24},{1,5},{5... | collective-permute-start | bytes 1572872 | tf_op jit(solution)/shard_map/ppermute | solution.py:344
  17.6 20.1 %collective-permute-start.6 = (bf16[2048,128]{1,0:T(8,128)(2,1)S(1)}, bf16[2048,128]{1,0:T(8,128)(2,1)S(1)}, u32[]{:S(2)}, u32[]{:S(2)}) collective-permute-start(bf16[2048,128]{1,0:T(8,128)(2,1)S(1)} %collective-permute-done.3.refs_2_), channel_id=1, source_target_pairs={{0,4},{4,0},{8,12},{12,8},{16,20},{20,16},{24,28},{28,24},{1,5},{5... | collective-permute-start | bytes 1572872 | tf_op jit(solution)/shard_map/ppermute | solution.py:344
  27.8 19.5 %collective-permute-start.14 = (bf16[2048,128]{1,0:T(8,128)(2,1)S(1)}, bf16[2048,128]{1,0:T(8,128)(2,1)S(1)}, u32[]{:S(2)}, u32[]{:S(2)}) collective-permute-start(bf16[2048,128]{1,0:T(8,128)(2,1)S(1)} %collective-permute-done.13.same_ref), channel_id=1, source_target_pairs={{0,4},{4,0},{8,12},{12,8},{16,20},{20,16},{24,28},{28,24},{1,5},{5... | collective-permute-start | bytes 1572872 | tf_op jit(solution)/shard_map/ppermute | solution.py:344
  28.0 8.6 %collective-permute-start = (f32[16,128]{1,0:T(8,128)S(1)}, f32[16,128]{1,0:T(8,128)S(1)}, u32[]{:S(2)}, u32[]{:S(2)}) collective-permute-start(f32[16,128]{1,0:T(8,128)S(1)} %shard_map.31), channel_id=1, source_target_pairs={{24,8},{28,12},{0,16},{4,20},{8,0},{12,4},{16,24},{20,28},{25,9},{... | collective-permute-start | bytes 24584 | tf_op jit(solution)/shard_map/ppermute | solution.py:341
  36.6 1.2 %collective-permute-start.1 = (f32[16,128]{1,0:T(8,128)S(1)}, f32[16,128]{1,0:T(8,128)S(1)}, u32[]{:S(2)}, u32[]{:S(2)}) collective-permute-start(f32[16,128]{1,0:T(8,128)S(1)} %collective-permute-done.late_same_ref), channel_id=1, source_target_pairs={{0,4},{4,0},{8,12},{12,8},{16,20},{20,16},{24,28},{28,24},{1,5},{5... | collective-permute-start | bytes 24584 | tf_op jit(solution)/shard_map/ppermute | solution.py:344
  43.7 9.3 %collective-permute-start.7 = (f32[12,32,128]{2,1,0:T(8,128)S(1)}, f32[12,32,128]{2,1,0:T(8,128)S(1)}, u32[]{:S(2)}, u32[]{:S(2)}) collective-permute-start(f32[12,32,128]{2,1,0:T(8,128)S(1)} %get-tuple-element.32), channel_id=1, source_target_pairs={{0,1},{1,0},{2,3},{3,2},{4,5},{5,4},{6,7},{7,6},{8,9},{9,8},{10,11... | collective-permute-start | bytes 589832 | tf_op jit(solution)/shard_map/ppermute | solution.py:388
  45.2 11.0 %collective-permute-start.8 = (f32[12,32,128]{2,1,0:T(8,128)S(1)}, f32[12,32,128]{2,1,0:T(8,128)S(1)}, u32[]{:S(2)}, u32[]{:S(2)}) collective-permute-start(f32[12,32,128]{2,1,0:T(8,128)S(1)} %get-tuple-element.33), channel_id=1, source_target_pairs={{0,2},{1,3},{2,0},{3,1},{4,6},{5,7},{6,4},{7,5},{8,10},{9,11},{10,... | collective-permute-start | bytes 589832 | tf_op jit(solution)/shard_map/ppermute | solution.py:388
  46.8 10.0 %collective-permute-start.9 = (f32[12,32,128]{2,1,0:T(8,128)S(1)}, f32[12,32,128]{2,1,0:T(8,128)S(1)}, u32[]{:S(2)}, u32[]{:S(2)}) collective-permute-start(f32[12,32,128]{2,1,0:T(8,128)S(1)} %get-tuple-element.34), channel_id=1, source_target_pairs={{0,3},{1,2},{2,1},{3,0},{4,7},{5,6},{6,5},{7,4},{8,11},{9,10},{10,... | collective-permute-start | bytes 589832 | tf_op jit(solution)/shard_map/ppermute | solution.py:388
  49.9 9.3 %collective-permute-start.15 = (f32[9,32,128]{2,1,0:T(8,128)S(1)}, f32[9,32,128]{2,1,0:T(8,128)S(1)}, u32[]{:S(2)}, u32[]{:S(2)}) collective-permute-start(f32[9,32,128]{2,1,0:T(8,128)S(1)} %get-tuple-element.42), channel_id=1, source_target_pairs={{0,1},{1,0},{2,3},{3,2},{4,5},{5,4},{6,7},{7,6},{8,9},{9,8},{10,11... | collective-permute-start | bytes 442376 | tf_op jit(solution)/shard_map/ppermute | solution.py:388
  51.5 11.0 %collective-permute-start.16 = (f32[9,32,128]{2,1,0:T(8,128)S(1)}, f32[9,32,128]{2,1,0:T(8,128)S(1)}, u32[]{:S(2)}, u32[]{:S(2)}) collective-permute-start(f32[9,32,128]{2,1,0:T(8,128)S(1)} %get-tuple-element.43), channel_id=1, source_target_pairs={{0,2},{1,3},{2,0},{3,1},{4,6},{5,7},{6,4},{7,5},{8,10},{9,11},{10,... | collective-permute-start | bytes 442376 | tf_op jit(solution)/shard_map/ppermute | solution.py:388
  53.0 9.5 %collective-permute-start.17 = (f32[9,32,128]{2,1,0:T(8,128)S(1)}, f32[9,32,128]{2,1,0:T(8,128)S(1)}, u32[]{:S(2)}, u32[]{:S(2)}) collective-permute-start(f32[9,32,128]{2,1,0:T(8,128)S(1)} %get-tuple-element.44), channel_id=1, source_target_pairs={{0,3},{1,2},{2,1},{3,0},{4,7},{5,6},{6,5},{7,4},{8,11},{9,10},{10,... | collective-permute-start | bytes 442376 | tf_op jit(solution)/shard_map/ppermute | solution.py:388
  57.1 12.5 %collective-permute-start.10 = (f32[40,640]{1,0:T(8,128)S(1)}, f32[40,640]{1,0:T(8,128)S(1)}, u32[]{:S(2)}, u32[]{:S(2)}) collective-permute-start(f32[40,640]{1,0:T(8,128)S(1)} %get-tuple-element.36), channel_id=1, source_target_pairs={{8,0},{12,4},{16,24},{20,28},{0,8},{4,12},{24,16},{28,20},{9,1},{1... | collective-permute-start | bytes 307208 | tf_op jit(solution)/shard_map/ppermute | solution.py:400
  59.2 10.4 %collective-permute-start.11 = (f32[40,640]{1,0:T(8,128)S(1)}, f32[40,640]{1,0:T(8,128)S(1)}, u32[]{:S(2)}, u32[]{:S(2)}) collective-permute-start(f32[40,640]{1,0:T(8,128)S(1)} %get-tuple-element.37), channel_id=1, source_target_pairs={{8,24},{12,28},{16,0},{20,4},{0,8},{4,12},{24,16},{28,20},{9,25},{... | collective-permute-start | bytes 307208 | tf_op jit(solution)/shard_map/ppermute | solution.py:400
  59.2 10.3 %collective-permute-start.12 = (f32[40,640]{1,0:T(8,128)S(1)}, f32[40,640]{1,0:T(8,128)S(1)}, u32[]{:S(2)}, u32[]{:S(2)}) collective-permute-start(f32[40,640]{1,0:T(8,128)S(1)} %get-tuple-element.38), channel_id=1, source_target_pairs={{8,16},{12,20},{16,8},{20,12},{0,0},{4,4},{24,24},{28,28},{9,17},{... | collective-permute-start | bytes 307208 | tf_op jit(solution)/shard_map/ppermute | solution.py:400
  62.7 6.9 %collective-permute-start.18 = (f32[32,640]{1,0:T(8,128)S(1)}, f32[32,640]{1,0:T(8,128)S(1)}, u32[]{:S(2)}, u32[]{:S(2)}) collective-permute-start(f32[32,640]{1,0:T(8,128)S(1)} %get-tuple-element.46), channel_id=1, source_target_pairs={{8,24},{12,28},{16,0},{20,4},{0,8},{4,12},{24,16},{28,20},{9,25},{... | collective-permute-start | bytes 245768 | tf_op jit(solution)/shard_map/ppermute | solution.py:410
  65.0 0.7 collective-permute-start.19

commit v6 on v5

--- a/solution.py
+++ b/solution.py
@@ -135,42 +135,53 @@
     place_tiles(False, tile_of, out_refs)
 
 
-def late_kernel(near, spread_ref, same_ref, other_ref, turned_ref, *refs):
-    out_refs, (fluct_ref, far_turned_ref, tiles_ref) = refs[:-3], refs[-3:]
+def far_same_kernel(spread_ref, same_ref, turned_ref, far_turned_ref, tiles_ref, fluct_ref):
     rows, width = same_ref.shape
+    near = turned_ref.shape[0] // width
 
     def one_tile(tile):
         target = pl.ds(pl.multiple_of(tile * LANES, LANES), LANES)
-        mean = spread_ref[target, :]
-        for n, ref in enumerate((same_ref, other_ref)):
-            value = (ref[target, :].astype(jnp.float32) - mean).astype(jnp.bfloat16)
-            fluct_ref[target, n * width : (n + 1) * width] = value
-            far_turned_ref[n * width : (n + 1) * width, target] = jnp.transpose(value)
+        value = (same_ref[target, :].astype(jnp.float32) - spread_ref[target, :]).astype(jnp.bfloat16)
+        fluct_ref[target, :] = value
+        far_turned_ref[:, target] = jnp.transpose(value)
 
     over_tiles(rows // LANES, one_tile)
     half = near // 2
-    step = half * width
-    for first in range(0, near * width, step):
-        with_far = product(turned_ref[first : first + step, :], fluct_ref[...])
+    for first in range(0, near, half):
+        column = product(turned_ref[first * width : (first + half) * width, :], fluct_ref[...])
         for n in range(half):
-            place = first // width + n
-            tile = with_far[n * width : (n + 1) * width, :]
-            tiles_ref[place] = jnp.transpose(tile[:, :width])
+            tile = column[n * width : (n + 1) * width, :]
+            tiles_ref[first + n] = jnp.transpose(tile)
             if first == 0:
-                tiles_ref[near + 2 + 2 * n] = tile[:, :width]
-                tiles_ref[near + 3 + 2 * n] = tile[:, width:]
-    both = product(far_turned_ref[...], fluct_ref[...])
-    tiles_ref[near] = both[:width, :width]
-    tiles_ref[near + 1] = jnp.transpose(both[width:, :width])
+                tiles_ref[near + 1 + n] = tile
+    tiles_ref[near] = product(far_turned_ref[...], fluct_ref[...])
+
+
+def far_other_kernel(near, spread_ref, other_ref, turned_ref, far_turned_ref, held_ref, *refs):
+    out_refs, (fluct_ref, tiles_ref) = refs[:-2], refs[-2:]
+    rows, width = other_ref.shape
+
+    def one_tile(tile):
+        target = pl.ds(pl.multiple_of(tile * LANES, LANES), LANES)
+        fluct_ref[target, :] = (other_ref[target, :].astype(jnp.float32) - spread_ref[target, :]).astype(jnp.bfloat16)
+
+    over_tiles(rows // LANES, one_tile)
+    half = near // 2
+    column = product(turned_ref[0 : half * width, :], fluct_ref[...])
+    for n in range(half):
+        tiles_ref[n] = column[n * width : (n + 1) * width, :]
+    tiles_ref[half] = product(far_turned_ref[...], fluct_ref[...])
     late = lax.axis_size("snap") // 4
 
     def tile_of(offset, rel, rows):
-        other = rel // 2
+        other, odd = rel // 2, rel % 2
         row = offset - jnp.where(offset > late, 1, 0)
-        column = other - jnp.where(other > late, 1, 0) + half * (rel % 2)
-        turned = jnp.where(other == late, near + rel % 2, column)
-        place = jnp.where(offset == late, turned, near + 2 + 2 * row + rel % 2)
-        return tiles_ref[place, rows, :]
+        column = other - jnp.where(other > late, 1, 0) + half * odd
+        place = jnp.where(offset == late, jnp.where(other == late, near, column), near + 1 + row)
+        fresh = jnp.logical_and(other == late, odd == 1)
+        place = jnp.where(fresh, 0, place)
+        new = jnp.where(fresh, jnp.where(offset == late, half, row), 0)
+        return jnp.where(fresh, tiles_ref[new, rows, :], held_ref[place, rows, :])
 
     place_tiles(True, tile_of, out_refs)
 
@@ -212,8 +223,10 @@
     me = lax.axis_index("snap")
     _, part_rows, width = firsts[0].shape
     band = out_refs[0].shape[1] // width
+    chip_count = len(out_refs) + 1
+    near_refs = dict(zip([offset for offset in range(chip_count) if offset != chip_count // 2], out_refs))
     slot = 0
-    for offset, out_ref in enumerate(out_refs):
+    for offset, out_ref in near_refs.items():
         for k in range(band):
             far = is_far(me // 2, me % 2, offset, k)
             lanes = slice(k * width, (k + 1) * width)
@@ -227,16 +240,24 @@
                 out_ref[0:part_rows, lanes] = functools.reduce(jnp.add, [ref[slot] for ref in firsts])
 
             slot = slot + jnp.where(far, 0, 1)
-        for n in range(mean_ref.shape[0]):
-            row = part_rows + n // band
-            out_ref[row : row + 1, (n % band) * width : (n % band + 1) * width] = mean_ref[n : n + 1, :]
-
-
-def joined_far_kernel(rounds, space_count, *refs):
+        put_means(mean_ref, out_ref, part_rows)
+
+
+def put_means(mean_ref, out_ref, first_row):
+    across = out_ref.shape[1] // LANES
+    for n in range(mean_ref.shape[0]):
+        lanes = slice((n % across) * LANES, (n % across + 1) * LANES)
+        out_ref[first_row + n // across : first_row + n // across + 1, lanes] = mean_ref[n : n + 1, :]
+
+
+def joined_far_kernel(rounds, space_count, mean_ref, *refs):
     seconds, out_refs = refs[:space_count], refs[space_count:]
+    for out_ref in out_refs:
+        if out_ref.shape[0] > seconds[0].shape[1]:
+            put_means(mean_ref, out_ref, seconds[0].shape[1])
     me = lax.axis_index("snap")
     chip = me // 2
-    _, _, width = seconds[0].shape
+    _, part_rows, width = seconds[0].shape
     chip_count = lax.axis_size("snap") // 2
     band = chip_count + 1
     slot = 0
@@ -253,7 +274,7 @@
                 def _(n=n, slot=slot, place=place):
                     total = functools.reduce(jnp.add, [ref[slot] for ref in seconds])
                     lanes = pl.ds(pl.multiple_of(place * width, width), width)
-                    out_refs[n][:, lanes] = total
+                    out_refs[n][0:part_rows, lanes] = total
 
             slot = slot + jnp.where(far, 1, 0)
             place = place + jnp.where(far, 1, 0)
@@ -264,10 +285,12 @@
     chip, core = me // 2, me % 2
     chip_count = lax.axis_size("snap") // 2
     hub_chips = chip_count // 2
-    nears, fars, (gram_ref, mean_ref) = refs[:chip_count], refs[chip_count:-2], refs[-2:]
+    late = chip_count // 2
+    nears, fars, (gram_ref, mean_ref) = refs[: chip_count - 1], refs[chip_count - 1 : -2], refs[-2:]
+    nears = dict(zip([offset for offset in range(chip_count) if offset != late], nears))
     part_rows, columns = gram_ref.shape
     total = jnp.zeros((part_rows, columns), jnp.float32)
-    for offset, ref in enumerate(nears):
+    for offset, ref in nears.items():
         hub = (chip ^ offset) - first_chip
         total = total + jnp.where((hub >= 0) & (hub < hub_chips), ref[0:part_rows, :], 0.0)
     gram_ref[...] = total * scale
@@ -285,20 +308,21 @@
 
             @pl.when(far)
             def _(ref=ref, lanes=lanes, place=place):
-                sent = ref[:, pl.ds(pl.multiple_of(place * LANES, LANES), LANES)]
+                sent = ref[0:part_rows, pl.ds(pl.multiple_of(place * LANES, LANES), LANES)]
                 gram_ref[:, lanes] = gram_ref[:, lanes] + sent * scale
 
             place = place + jnp.where(far, 1, 0)
     mean_rows = mean_ref.shape[0] // hub_chips
-    band = columns // LANES
-    for offset, ref in enumerate(nears):
+    holders = nears | {late: next(ref for ref in fars if ref.shape[0] > part_rows)}
+    for offset, ref in holders.items():
         hub = (chip ^ offset) - first_chip
+        across = ref.shape[1] // LANES
 
         @pl.when((hub >= 0) & (hub < hub_chips))
-        def _(ref=ref, hub=hub):
+        def _(ref=ref, hub=hub, across=across):
             for n in range(mean_rows):
-                row = part_rows + n // band
-                mean_ref[pl.ds(hub * mean_rows + n, 1), :] = ref[row : row + 1, (n % band) * LANES : (n % band + 1) * LANES]
+                row, lanes = part_rows + n // across, slice((n % across) * LANES, (n % across + 1) * LANES)
+                mean_ref[pl.ds(hub * mean_rows + n, 1), :] = ref[row : row + 1, lanes]
 
 
 def per_device(snapshots):
@@ -370,16 +394,20 @@
         [pltpu.VMEM((rows, near * width), jnp.bfloat16), pltpu.VMEM((near // 2 * width, near * width), jnp.float32)],
         flops=near * near * width * width * rows,
     )
+    flops = 2 * snap_count * width * width * rows
+    far_turned, held = kernel(
+        far_same_kernel,
+        [spread, blocks[late], turned],
+        [shaped(jnp.bfloat16, width, rows), shaped(jnp.float32, near + near // 2 + 1, width, width)],
+        [pltpu.VMEM((rows, width), jnp.bfloat16)],
+        flops=flops,
+    )
     second = kernel(
-        functools.partial(late_kernel, near),
-        [spread, blocks[late], passed[late], turned],
+        functools.partial(far_other_kernel, near),
+        [spread, passed[late], turned, far_turned, held],
         [shaped(jnp.float32, second_slots, part_rows, width)] * space_count,
-        [
-            pltpu.VMEM((rows, 2 * width), jnp.bfloat16),
-            pltpu.VMEM((2 * width, rows), jnp.bfloat16),
-            pltpu.VMEM((2 * near + 2, width, width), jnp.float32),
-        ],
-        flops=4 * snap_count * width * width * rows,
+        [pltpu.VMEM((rows, width), jnp.bfloat16), pltpu.VMEM((near // 2 + 1, width, width), jnp.float32)],
+        flops=flops,
     )
 
     def over_space(parts):
@@ -391,18 +419,23 @@
     mean_space = -(-(-(-(rows // LANES) // band)) // 8) * 8
     slab = shaped(jnp.float32, part_rows + mean_space, band * width)
     near_slabs = kernel(
-        functools.partial(joined_near_kernel, space_count), [mean_rows, *over_space(first)], [slab] * chip_count
+        functools.partial(joined_near_kernel, space_count), [mean_rows, *over_space(first)], [slab] * len(early)
     )
 
     nears = [near_slabs[0]]
-    for offset in range(1, chip_count):
+    for offset, x in zip(early[1:], near_slabs[1:]):
         pairs = completed([(h, h ^ (2 * offset)) for h in hubs], snap_count)
-        nears.append(lax.ppermute(near_slabs[offset], "snap", pairs))
+        nears.append(lax.ppermute(x, "snap", pairs))
     rounds = late_rounds(chip_count)
+
+    def far_slab(pairs, count):
+        below = -(-(-(-(rows // LANES) // count)) // 8) * 8 if any(a ^ b == late for a, b in pairs.items()) else 0
+        return shaped(jnp.float32, part_rows + below, count * width)
+
     far_slabs = kernel(
         functools.partial(joined_far_kernel, rounds, space_count),
-        over_space(second),
-        [shaped(jnp.float32, part_rows, count * width) for count in [band] + [count for _, count in rounds]],
+        [mean_rows, *over_space(second)],
+        [shaped(jnp.float32, part_rows, band * width)] + [far_slab(*sent) for sent in rounds],
     )
     fars = [far_slabs[0]]
     for n, (pairs, _) in enumerate(rounds):

time: 70.7 us -> 79.3 us (1.12)
  the two profiles are of different devices: /device:TPU:0 before, /device:TPU:12 now
where the time goes in v6:
time: 79.3 us; the launch traced here: 79.1 us
  waiting for transfers between devices  43.8 us (55%)
  starting transfers between devices  22 us (28%)
  Pallas kernels  12.5 us (16%)
    ppermute x4, waiting for transfers between devices, to_hubs(): lax.ppermute(x, 'snap', completed(pairs, snap_count) if full else pairs)  26 us
    pallas_call x8, Pallas kernels, kernel(): pl.pallas_call(body, out_shape=list(out_shapes), in_specs=[pl.BlockSpec(m...  12.5 us
    ppermute x6, waiting for transfers between devices, over_space(): lax.ppermute(parts[n], 'space', [(s, s ^ n) for s in range(space_count)])  12.1 us
    ppermute x6, starting transfers between devices, over_space(): lax.ppermute(parts[n], 'space', [(s, s ^ n) for s in range(space_count)])  6.98 us
    ppermute x4, starting transfers between devices, to_hubs(): lax.ppermute(x, 'snap', completed(pairs, snap_count) if full else pairs)  6.46 us
    ppermute x2, starting transfers between devices, per_device(): nears.append(lax.ppermute(x, 'snap', pairs))  5.46 us
    ppermute x2, waiting for transfers between devices, per_device(): lax.ppermute(far_slabs[n + 1], 'snap', completed(devices, snap_count))  4.5 us
    ppermute x2, starting transfers between devices, per_device(): lax.ppermute(far_slabs[n + 1], 'snap', completed(devices, snap_count))  2.51 us
  transfers between devices with their start and end apart: 19, of which 7 were waited for; matrix products, arithmetic and copies ran while one was open for 0% of the time, Pallas kernels for 11%

profile of v6, /device:TPU:12, one launch (start us, length us, event | category | flops | bytes accessed | tf_op | source)
XLA Modules:
  0.0 79.1 jit_solution(10687263874442529830)
XLA Ops:
  0.6 1.6 %shard_map.30 = (bf16[2048,128]{1,0:T(8,128)(2,1)S(1)}, bf16[2048,128]{1,0:T(8,128)(2,1)S(1)}, bf16[2048,128]{1,0:T(8,128)(2,1)S(1)}, bf16[2048,128]{1,0:T(8,128)(2,1)S(1)}) custom-call(bf16[4096,128]{1,0:T(8,128)(2,1)} %rows_ref.1), custom_call_target="tpu_custom_call" | custom-call | flops 1000 | tf_op jit(solution)/shard_map/pallas_call | solution.py:349
  2.2 0.5 collective-permute-start.2
  2.7 4.6 %collective-permute-start.3 = (bf16[2048,128]{1,0:T(8,128)(2,1)S(1)}, bf16[2048,128]{1,0:T(8,128)(2,1)S(1)}, u32[]{:S(2)}, u32[]{:S(2)}) collective-permute-start(bf16[2048,128]{1,0:T(8,128)(2,1)S(1)} %get-tuple-element.30), channel_id=1, source_target_pairs={{16,8},{20,12},{8,16},{12,20},{0,0},{4,4},{24,24},{28,28},{17,9},{... | collective-permute-start | bytes 1572872 | tf_op jit(solution)/shard_map/ppermute | solution.py:365
  7.3 1.3 %collective-permute-start.12 = (bf16[2048,128]{1,0:T(8,128)(2,1)S(1)}, bf16[2048,128]{1,0:T(8,128)(2,1)S(1)}, u32[]{:S(2)}, u32[]{:S(2)}) collective-permute-start(bf16[2048,128]{1,0:T(8,128)(2,1)S(1)} %get-tuple-element.27.piece_ref), channel_id=1, source_target_pairs={{24,8},{28,12},{0,16},{4,20},{25,9},{29,13},{1,17},{5,21},{26,10},... | collective-permute-start | bytes 1572872 | tf_op jit(solution)/shard_map/ppermute | solution.py:365
  8.6 0.1 collective-permute-start.4
  8.7 8.4 %collective-permute-done.2.refs_1_ = bf16[2048,128]{1,0:T(8,128)(2,1)S(1)} collective-permute-done((bf16[2048,128]{1,0:T(8,128)(2,1)S(1)}, bf16[2048,128]{1,0:T(8,128)(2,1)S(1)}, u32[]{:S(2)}, u32[]{:S(2)}) %collective-permute-start.2) | collective-permute-done | bytes 524320 | tf_op jit(solution)/shard_map/ppermute | solution.py:365
  17.1 0.0 collective-permute-start.5
  17.1 13.1 %collective-permute-done.3.refs_2_ = bf16[2048,128]{1,0:T(8,128)(2,1)S(1)} collective-permute-done((bf16[2048,128]{1,0:T(8,128)(2,1)S(1)}, bf16[2048,128]{1,0:T(8,128)(2,1)S(1)}, u32[]{:S(2)}, u32[]{:S(2)}) %collective-permute-start.3) | collective-permute-done | bytes 524320 | tf_op jit(solution)/shard_map/ppermute | solution.py:365
  30.2 0.5 collective-permute-start.13
  30.7 0.2 shard_map.31
  30.9 0.1 collective-permute-start
  31.0 4.5 %collective-permute-done.late_same_ref = f32[16,128]{1,0:T(8,128)S(1)} collective-permute-done((f32[16,128]{1,0:T(8,128)S(1)}, f32[16,128]{1,0:T(8,128)S(1)}, u32[]{:S(2)}, u32[]{:S(2)}) %collective-permute-start) | collective-permute-done | bytes 8224 | tf_op jit(solution)/shard_map/ppermute | solution.py:365
  35.5 1.2 %collective-permute-done.1.late_other_ref = f32[16,128]{1,0:T(8,128)S(1)} collective-permute-done((f32[16,128]{1,0:T(8,128)S(1)}, f32[16,128]{1,0:T(8,128)S(1)}, u32[]{:S(2)}, u32[]{:S(2)}) %collective-permute-start.1) | collective-permute-done | bytes 8224 | tf_op jit(solution)/shard_map/ppermute | solution.py:368
  36.7 5.9 %shard_map.32 = (bf16[768,2048]{1,0:T(8,128)(2,1)S(1)}, f32[16,128]{1,0:T(8,128)S(1)}, f32[2048,128]{1,0:T(8,128)S(1)}, f32[12,32,128]{2,1,0:T(8,128)S(1)}, f32[...) custom-call(f32[16,128]{1,0:T(8,128)S(1)} %collective-permute-done.late_same_ref, ...), custom_call_target="tpu_custom_call" | custom-call | flops 1207959552 | tf_op jit(solution)/shard_map/pallas_call | solution.py:349
  42.7 1.5 %shard_map.34 = (bf16[128,2048]{1,0:T(8,128)(2,1)S(1)}, f32[10,128,128]{2,1,0:T(8,128)S(1)}) custom-call(f32[2048,128]{1,0:T(8,128)S(1)} %get-tuple-element.39.spread_ref, bf16[2048,128]{1,0:T(8,128)(2,1)S(1)} %collective-permute-done.12.same_ref, bf16[768,2048]{1,0:T(8,128)(2,1)S(1)} %get-tuple-element.40.turned_ref), custom_call_target="tpu_custom_call" | custom-call | flops 536870912 | tf_op jit(solution)/shard_map/pallas_call | solution.py:349
  44.2 1.6 %shard_map.35 = (f32[9,32,128]{2,1,0:T(8,128)S(1)}, f32[9,32,128]{2,1,0:T(8,128)S(1)}, f32[9,32,128]{2,1,0:T(8,128)S(1)}, f32[9,32,128]{2,1,0:T(8,128)S(1)}) custom-call(f32[2048,128]{1,0:T(8,128)S(1)} %get-tuple-element.39.spread_ref, bf16[2048,128]{1,0:T(8,128)(2,1)S(1)} %collective-permute-done.13.other_ref, ...), custom_call_target="tpu_custom_call" | custom-call | flops 536870912 | tf_op jit(solution)/shard_map/pallas_call | solution.py:349
  45.8 1.6 %collective-permute-start.14 = (f32[9,32,128]{2,1,0:T(8,128)S(1)}, f32[9,32,128]{2,1,0:T(8,128)S(1)}, u32[]{:S(2)}, u32[]{:S(2)}) collective-permute-start(f32[9,32,128]{2,1,0:T(8,128)S(1)} %get-tuple-element.44), channel_id=1, source_target_pairs={{0,1},{1,0},{2,3},{3,2},{4,5},{5,4},{6,7},{7,6},{8,9},{9,8},{10,11... | collective-permute-start | bytes 442376 | tf_op jit(solution)/shard_map/ppermute | solution.py:416
  47.4 0.5 collective-permute-start.7
  47.9 0.5 collective-permute-start.8
  48.4 2.4 %collective-permute-start.9 = (f32[12,32,128]{2,1,0:T(8,128)S(1)}, f32[12,32,128]{2,1,0:T(8,128)S(1)}, u32[]{:S(2)}, u32[]{:S(2)}) collective-permute-start(f32[12,32,128]{2,1,0:T(8,128)S(1)} %get-tuple-element.35), channel_id=1, source_target_pairs={{0,3},{1,2},{2,1},{3,0},{4,7},{5,6},{6,5},{7,4},{8,11},{9,10},{10,... | collective-permute-start | bytes 589832 | tf_op jit(solution)/shard_map/ppermute | solution.py:416
  50.9 0.5 collective-permute-start.15
  51.4 1.2 %collective-permute-done.14.refs_1_ = f32[9,32,128]{2,1,0:T(8,128)S(1)} collective-permute-done((f32[9,32,128]{2,1,0:T(8,128)S(1)}, f32[9,32,128]{2,1,0:T(8,128)S(1)}, u32[]{:S(2)}, u32[]{:S(2)}) %collective-permute-start.14) | collective-permute-done | bytes 147488 | tf_op jit(solution)/shard_map/ppermute | solution.py:416
  52.6 1.4 %collective-permute-start.16 = (f32[9,32,128]{2,1,0:T(8,128)S(1)}, f32[9,32,128]{2,1,0:T(8,128)S(1)}, u32[]{:S(2)}, u32[]{:S(2)}) collective-permute-start(f32[9,32,128]{2,1,0:T(8,128)S(1)} %get-tuple-element.46), channel_id=1, source_target_pairs={{0,3},{1,2},{2,1},{3,0},{4,7},{5,6},{6,5},{7,4},{8,11},{9,10},{10,... | collective-permute-start | bytes 442376 | tf_op jit(solution)/shard_map/ppermute | solution.py:416
  54.0 10.8 %collective-permute-done.15.refs_2_ = f32[9,32,128]{2,1,0:T(8,128)S(1)} collective-permute-done((f32[9,32,128]{2,1,0:T(8,128)S(1)}, f32[9,32,128]{2,1,0:T(8,128)S(1)}, u32[]{:S(2)}, u32[]{:S(2)}) %collective-permute-start.15) | collective-permute-done | bytes 147488 | tf_op jit(solution)/shard_map/ppermute | solution.py:416
  64.9 0.3 shard_map.36
  65.2 0.3 collective-permute-start.17
  65.5 0.4 shard_map.33
  65.9 1.8 %collective-permute-start.10 = (f32[40,640]{1,0:T(8,128)S(1)}, f32[40,640]{1,0:T(8,128)S(1)}, u32[]{:S(2)}, u32[]{:S(2)}) collective-permute-start(f32[40,640]{1,0:T(8,128)S(1)} %get-tuple-element.37), channel_id=1, source_target_pairs={{8,0},{12,4},{16,24},{20,28},{0,8},{4,12},{24,16},{28,20},{9,1},{1... | collective-permute-start | bytes 307208 | tf_op jit(solution)/shard_map/ppermute | solution.py:428
  67.8 3.6 %collective-permute-start.11 = (f32[40,640]{1,0:T(8,128)S(1)}, f32[40,640]{1,0:T(8,128)S(1)}, u32[]{:S(2)}, u32[]{:S(2)}) collective-permute-start(f32[40,640]{1,0:T(8,128)S(1)} %get-tuple-element.38), channel_id=1, source_target_pairs={{8,16},{12,20},{16,8},{20,12},{0,0},{4,4},{24,24},{28,28},{9,17},{... | collective-permute-start | bytes 307208 | tf_op jit(solution)/shard_map/ppermute | solution.py:428
  71.4 2.2 %collective-permute-start.18 = (f32[32,256]{1,0:T(8,128)S(1)}, f32[32,256]{1,0:T(8,128)S(1)}, u32[]{:S(2)}, u32[]{:S(2)}) collective-permute-start(f32[32,256]{1,0:T(8,128)S(1)} %get-tuple-element.49), channel_id=1, source_target_pairs={{8,16},{12,20},{16,24},{20,28},{0,0},{4,4},{24,8},{28,12},{9,17},{... | collective-permute-start | bytes 98312 | tf_op jit(solution)/shard_map/ppermute | solution.py:443
  73.6 4.5 %collective-permute-done.18.refs_5_ = f32[32,256]{1,0:T(8,128)S(1)} collective-permute-done((f32[32,256]{1,0:T(8,128)S(1)}, f32[32,256]{1,0:T(8,128)S(1)}, u32[]{:S(2)}, u32[]{:S(2)}) %collective-permute-start.18) | collective-permute-done | bytes 32800 | tf_op jit(solution)/shard_map/ppermute | solution.py:443
  78.1 0.9 %shard_map.37 = (f32[32,640]{1,0:T(8,128)}, f32[32,128]{1,0:T(8,128)}) custom-call(f32[40,640]{1,0:T(8,128)S(1)} %get-tuple-element.36.refs_0_, f32[40,640]{1,0:T(8,128)S(1)} %collective-permute-done.10.refs_1_, f32[40,640]{1,0:T(8,128)S(1)} %collective-permute-done.11.refs_2_, f32[32,640]{1,0:T(8,128)S(1)} %get-tuple-element.47.refs_3_, ...), custom_call_target="tpu_custom_call" | custom-call | flops 1000 | tf_op jit(solution)/shard_map/pallas_call | solution.py:349
  (14 shorter events, 0.0 us)
Async XLA Ops:
  2.2 14.9 %collective-permute-start.2 = (bf16[2048,128]{1,0:T(8,128)(2,1)S(1)}, bf16[2048,128]{1,0:T(8,128)(2,1)S(1)}, u32[]{:S(2)}, u32[]{:S(2)}) collective-permute-start(bf16[2048,128]{1,0:T(8,128)(2,1)S(1)} %get-tuple-element.29), channel_id=1, source_target_pairs={{0,8},{4,12},{24,16},{28,20},{8,0},{12,4},{16,24},{20,28},{1,9},{5... | collective-permute-start | bytes 1572872 | tf_op jit(solution)/shard_map/ppermute | solution.py:365
  2.7 27.5 %collective-permute-start.3 = (bf16[2048,128]{1,0:T(8,128)(2,1)S(1)}, bf16[2048,128]{1,0:T(8,128)(2,1)S(1)}, u32[]{:S(2)}, u32[]{:S(2)}) collective-permute-start(bf16[2048,128]{1,0:T(8,128)(2,1)S(1)} %get-tuple-element.30), channel_id=1, source_target_pairs={{16,8},{20,12},{8,16},{12,20},{0,0},{4,4},{24,24},{28,28},{17,9},{... | collective-permute-start | bytes 1572872 | tf_op jit(solution)/shard_map/ppermute | solution.py:365
  7.3 22.9 %collective-permute-start.12 = (bf16[2048,128]{1,0:T(8,128)(2,1)S(1)}, bf16[2048,128]{1,0:T(8,128)(2,1)S(1)}, u32[]{:S(2)}, u32[]{:S(2)}) collective-permute-start(bf16[2048,128]{1,0:T(8,128)(2,1)S(1)} %get-tuple-element.27.piece_ref), channel_id=1, source_target_pairs={{24,8},{28,12},{0,16},{4,20},{25,9},{29,13},{1,17},{5,21},{26,10},... | collective-permute-start | bytes 1572872 | tf_op jit(solution)/shard_map/ppermute | solution.py:365
  8.6 28.1 %collective-permute-start.4 = (bf16[2048,128]{1,0:T(8,128)(2,1)S(1)}, bf16[2048,128]{1,0:T(8,128)(2,1)S(1)}, u32[]{:S(2)}, u32[]{:S(2)}) collective-permute-start(bf16[2048,128]{1,0:T(8,128)(2,1)S(1)} %get-tuple-element.28.refs_0_), channel_id=1, source_target_pairs={{0,4},{4,0},{8,12},{12,8},{16,20},{20,16},{24,28},{28,24},{1,5},{5... | collective-permute-start | bytes 1572872 | tf_op jit(solution)/shard_map/ppermute | solution.py:368
  17.1 19.6 %collective-permute-start.5 = (bf16[2048,128]{1,0:T(8,128)(2,1)S(1)}, bf16[2048,128]{1,0:T(8,128)(2,1)S(1)}, u32[]{:S(2)}, u32[]{:S(2)}) collective-permute-start(bf16[2048,128]{1,0:T(8,128)(2,1)S(1)} %collective-permute-done.2.refs_1_), channel_id=1, source_target_pairs={{0,4},{4,0},{8,12},{12,8},{16,20},{20,16},{24,28},{28,24},{1,5},{5... | collective-permute-start | bytes 1572872 | tf_op jit(solution)/shard_map/ppermute | solution.py:368
  30.2 6.5 %collective-permute-start.6 = (bf16[2048,128]{1,0:T(8,128)(2,1)S(1)}, bf16[2048,128]{1,0:T(8,128)(2,1)S(1)}, u32[]{:S(2)}, u32[]{:S(2)}) collective-permute-start(bf16[2048,128]{1,0:T(8,128)(2,1)S(1)} %collective-permute-done.3.refs_2_), channel_id=1, source_target_pairs={{0,4},{4,0},{8,12},{12,8},{16,20},{20,16},{24,28},{28,24},{1,5},{5... | collective-permute-start | bytes 1572872 | tf_op jit(solution)/shard_map/ppermute | solution.py:368
  30.2 14.0 %collective-permute-start.13 = (bf16[2048,128]{1,0:T(8,128)(2,1)S(1)}, bf16[2048,128]{1,0:T(8,128)(2,1)S(1)}, u32[]{:S(2)}, u32[]{:S(2)}) collective-permute-start(bf16[2048,128]{1,0:T(8,128)(2,1)S(1)} %collective-permute-done.12.same_ref), channel_id=1, source_target_pairs={{0,4},{4,0},{8,12},{12,8},{16,20},{20,16},{24,28},{28,24},{1,5},{5... | collective-permute-start | bytes 1572872 | tf_op jit(solution)/shard_map/ppermute | solution.py:368
  30.9 4.6 %collective-permute-start = (f32[16,128]{1,0:T(8,128)S(1)}, f32[16,128]{1,0:T(8,128)S(1)}, u32[]{:S(2)}, u32[]{:S(2)}) collective-permute-start(f32[16,128]{1,0:T(8,128)S(1)} %shard_map.31), channel_id=1, source_target_pairs={{24,8},{28,12},{0,16},{4,20},{8,0},{12,4},{16,24},{20,28},{25,9},{... | collective-permute-start | bytes 24584 | tf_op jit(solution)/shard_map/ppermute | solution.py:365
  35.5 1.2 %collective-permute-start.1 = (f32[16,128]{1,0:T(8,128)S(1)}, f32[16,128]{1,0:T(8,128)S(1)}, u32[]{:S(2)}, u32[]{:S(2)}) collective-permute-start(f32[16,128]{1,0:T(8,128)S(1)} %collective-permute-done.late_same_ref), channel_id=1, source_target_pairs={{0,4},{4,0},{8,12},{12,8},{16,20},{20,16},{24,28},{28,24},{1,5},{5... | collective-permute-start | bytes 24584 | tf_op jit(solution)/shard_map/ppermute | solution.py:368
  45.8 6.8 %collective-permute-start.14 = (f32[9,32,128]{2,1,0:T(8,128)S(1)}, f32[9,32,128]{2,1,0:T(8,128)S(1)}, u32[]{:S(2)}, u32[]{:S(2)}) collective-permute-start(f32[9,32,128]{2,1,0:T(8,128)S(1)} %get-tuple-element.44), channel_id=1, source_target_pairs={{0,1},{1,0},{2,3},{3,2},{4,5},{5,4},{6,7},{7,6},{8,9},{9,8},{10,11... | collective-permute-start | bytes 442376 | tf_op jit(solution)/shard_map/ppermute | solution.py:416
  47.4 18.2 %collective-permute-start.7 = (f32[12,32,128]{2,1,0:T(8,128)S(1)}, f32[12,32,128]{2,1,0:T(8,128)S(1)}, u32[]{:S(2)}, u32[]{:S(2)}) collective-permute-start(f32[12,32,128]{2,1,0:T(8,128)S(1)} %get-tuple-element.33), channel_id=1, source_target_pairs={{0,1},{1,0},{2,3},{3,2},{4,5},{5,4},{6,7},{7,6},{8,9},{9,8},{10,11... | collective-permute-start | bytes 589832 | tf_op jit(solution)/shard_map/ppermute | solution.py:416
  47.9 17.6 %collective-permute-start.8 = (f32[12,32,128]{2,1,0:T(8,128)S(1)}, f32[12,32,128]{2,1,0:T(8,128)S(1)}, u32[]{:S(2)}, u32[]{:S(2)}) collective-permute-start(f32[12,32,128]{2,1,0:T(8,128)S(1)} %get-tuple-element.34), channel_id=1, source_target_pairs={{0,2},{1,3},{2,0},{3,1},{4,6},{5,7},{6,4},{7,5},{8,10},{9,11},{10,... | collective-permute-start | bytes 589832 | tf_op jit(solution)/shard_map/ppermute | solution.py:416
  48.4 17.1 %collective-permute-start.9 = (f32[12,32,128]{2,1,0:T(8,128)S(1)}, f32[12,32,128]{2,1,0:T(8,128)S(1)}, u32[]{:S(2)}, u32[]{:S(2)}) collective-permute-start(f32[12,32,128]{2,1,0:T(8,128)S(1)} %get-tuple-element.35), channel_id=1, source_target_pairs={{0,3},{1,2},{2,1},{3,0},{4,7},{5,6},{6,5},{7,4},{8,11},{9,10},{10,... | collective-permute-start | bytes 589832 | tf_op jit(solution)/shard_map/ppermute | solution.py:416
  50.9 14.0 %collective-permute-start.15 = (f32[9,32,128]{2,1,0:T(8,128)S(1)}, f32[9,32,128]{2,1,0:T(8,128)S(1)}, u32[]{:S(2)}, u32[]{:S(2)}) collective-permute-start(f32[9,32,128]{2,1,0:T(8,128)S(1)} %get-tuple-element.45), channel_id=1, source_target_pairs={{0,2},{1,3},{2,0},{3,1},{4,6},{5,7},{6,4},{7,5},{8,10},{9,11},{10,... | collective-permute-start | bytes 442376 | tf_op jit(solution)/shard_map/ppermute | solution.py:416
  52.6 12.3 %collective-permute-start.16 = (f32[9,32,128]{2,1,0:T(8,128)S(1)}, f32[9,32,128]{2,1,0:T(8,128)S(1)}, u32[]{:S(2)}, u32[]{:S(2)}) collective-permute-start(f32[9,32,128]{2,1,0:T(8,128)S(1)} %get-tuple-element.46), channel_id=1, source_target_pairs={{0,3},{1,2},{2,1},{3,0},{4,7},{5,6},{6,5},{7,4},{8,11},{9,10},{10,... | collective-permute-start | bytes 442376 | tf_op jit(solution)/shard_map/ppermute | solution.py:416
  65.2 12.9 %collective-permute-start.17 = (f32[40,640]{1,0:T(8,128)S(1)}, f32[40,640]{1,0:T(8,128)S(1)}, u32[]{:S(2)}, u32[]{:S(2)}) collective-permute-start(f32[40,640]{1,0:T(8,128)S(1)} %get-tuple-element.48), channel_id=1, source_target_pairs={{8,24},{12,28},{16,0},{20,4},{0,8},{4,12},{24,16},{28,20},{9,25},{... | collective-permute-start | bytes 307208 | tf_op jit(solution)/shard_map/ppermute | solution.py:443
  65.9 12.2 %collective-permute-start.10 = (f32[40,640]{1,0:T(8,128)S(1)}, f32[40,640]{1,0:T(8,128)S(1)}, u32[]{:S(2)}, u32[]{:S(2)}) collective-permute-start(f32[40,640]{1,0:T(8,128)S(1)} %get-tuple-element.37), channel_id=1, source_target_pairs={{8,0},{12,4},{16,24},{20,28},{0,8},{4,12},{24,16},{28,20},{9,1},{1... | collective-permute-start | bytes 307208 | tf_op jit(solution)/shard_map/ppermute | solution.py:428
  67.8 10.4 %collective-permute-start.11 = (f32[40,640]{1,0:T(8,128)S(1)}, f32[40,640]{1,0:T(8,128)S(1)}, u32[]{:S(2)}, u32[]{:S(2)}) collective-permute-start(f32[40,640]{1,0:T(8,128)S(1)} %get-tuple-element.38), channel_id=1, source_target_pairs={{8,16},{12,20},{16,8},{20,12},{0,0},{4,4},{24,24},{28,28},{9,17},{... | collective-permute-start | bytes 307208 | tf_op jit(solution)/shard_map/ppermute | solution.py:428
  71.4 6.7 %collective-permute-start.18 = (f32[32,256]{1,0:T(8,128)S(1)}, f32[32,256]{1,0:T(8,128)S(1)}, u32[]{:S(2)}, u32[]{:S(2)}) collective-permute-start(f32[32,256]{1,0:T(8,128)S(1)} %get-tuple-element.49), channel_id=1, source_target_pairs={{8,16},{12,20},{16,24},{20,28},{0,0},{4,4},{24,8},{28,12},{9,17},{... | collective-permute-start | bytes 98312 | tf_op jit(solution)/shard_map/ppermute | solution.py:443

commit v7 on v6

v7 whole, which is shorter than its diff:
```python
import functools
import math

import jax
import jax.numpy as jnp
import numpy as np
from jax import lax
from jax.experimental import pallas as pl
from jax.experimental.pallas import tpu as pltpu
from jax.sharding import PartitionSpec as P


LANES = 128


def completed(pairs, count):
    sources = [i for i in range(count) if i not in {p[0] for p in pairs}]
    targets = [i for i in range(count) if i not in {p[1] for p in pairs}]
    same = [i for i in sources if i in targets]
    left = zip([i for i in sources if i not in same], [i for i in targets if i not in same])
    return list(pairs) + [(i, i) for i in same] + list(left)


def tile_kind(chip, core, offset, k, snap_count):
    chip_count, late = snap_count // 2, snap_count // 4
    me = chip * 2 + core
    rel = (((chip ^ offset) * 2 + core + k) % snap_count) ^ me
    other = rel // 2
    is_hub = (chip >= chip_count // 4) & (chip < 3 * chip_count // 4)
    kept_other = (other != late) & (other != late ^ 1)
    kept_offset = (offset != late) & (offset != late ^ 1)
    near_hub = (offset != late) & (other != late)
    near_end = ((offset == 0) & (other <= 1)) | ((offset == 1) & (other == 0))
    far = is_hub & (((offset == late) & kept_other) | ((other == late) & kept_offset))
    return (is_hub & near_hub) | ((is_hub ^ True) & near_end), far, rel


def near_column(offset, late, count):
    return jnp.where(offset == late ^ 1, count - 1, offset - jnp.where(offset > late, 2, 0))


def place_tiles(wanted_far, tile_of, out_refs):
    me, space = lax.axis_index("snap"), lax.axis_index("space")
    snap_count = lax.axis_size("snap")
    chip_count = snap_count // 2
    band = chip_count + 1
    part_rows = out_refs[0].shape[1]

    def one(pair, slot):
        offset, k = pair // band, pair % band
        near, far, rel = tile_kind(me // 2, me % 2, offset, k, snap_count)
        wanted = far if wanted_far else near

        @pl.when(wanted)
        def _():
            for n, out_ref in enumerate(out_refs):
                rows = pl.ds(pl.multiple_of((space ^ n) * part_rows, part_rows), part_rows)
                out_ref[slot] = tile_of(offset, rel, rows)

        return slot + jnp.where(wanted, 1, 0)

    lax.fori_loop(0, chip_count * band, one, 0)


def slot_count(snap_count, wanted_far):
    chip_count = snap_count // 2
    pairs = [(offset, k) for offset in range(chip_count) for k in range(chip_count + 1)]
    devices = [(chip, core) for chip in range(chip_count) for core in (0, 1)]
    return max(sum(tile_kind(*device, *pair, snap_count)[int(wanted_far)] for pair in pairs) for device in devices)


def as_column(row):
    return jnp.transpose(jnp.broadcast_to(row, (LANES, LANES)))


def product(left, right):
    return lax.dot_general(left, right, (((1,), (0,)), ((), ())), preferred_element_type=jnp.float32)


def over_tiles(count, one_tile):
    group = math.gcd(count, 4)

    def some(step, carry):
        for n in range(group):
            one_tile(step * group + n)
        return carry

    lax.fori_loop(0, count // group, some, 0)


def split_kernel(hub_of, offsets, rows_ref, *refs):
    pieces, sems = refs[:-1], refs[-1]
    me = lax.axis_index("snap")
    copies = []
    for n, offset in enumerate(offsets):
        first = pl.multiple_of(hub_of(me ^ (2 * offset)), pieces[0].shape[0])
        copies.append(pltpu.make_async_copy(rows_ref.at[pl.ds(first, pieces[0].shape[0]), :], pieces[n], sems.at[n]))
    for copy in copies:
        copy.start()
    for copy in copies:
        copy.wait()


def sums_kernel(*refs):
    pieces, sums_ref = refs[:-1], refs[-1]
    count = pieces[0].shape[0] // LANES
    for n, piece_ref in enumerate(pieces):
        for tile in range(count):
            values = piece_ref[tile * LANES : (tile + 1) * LANES, :].astype(jnp.float32)
            row = n * count + tile
            sums_ref[row : row + 1, :] = jnp.sum(jnp.transpose(values), axis=0, keepdims=True)


def chip_sums_kernel(own_ref, mate_ref, *out_refs):
    count = out_refs[0].shape[0]
    for n, out_ref in enumerate(out_refs):
        rows = slice(n * count, (n + 1) * count)
        out_ref[...] = own_ref[rows, :] + mate_ref[rows, :]


def early_kernel(total_columns, near, late_sums_ref, *refs):
    half = near // 2
    rest_sums, blocks = refs[: half - 2], refs[half - 2 : half - 2 + near]
    turned_ref, mean_ref, spread_ref, *out_refs = refs[half - 2 + near : -2]
    fluct_ref, tiles_ref = refs[-2:]
    rows, width = blocks[0].shape
    late = lax.axis_size("snap") // 4
    chip = lax.axis_index("snap") // 2
    is_hub = (chip >= late // 2) & (chip < late // 2 + late)

    def one_tile(tile):
        target = pl.ds(pl.multiple_of(tile * LANES, LANES), LANES)
        held = [ref[target, :].astype(jnp.float32) for ref in blocks]
        always = functools.reduce(jnp.add, [held[n] for n in range(near) if n % half < 2])
        at_hubs = functools.reduce(jnp.add, [held[n] for n in range(near) if n % half >= 2])
        near_sum = jnp.sum(jnp.transpose(always + jnp.where(is_hub, at_hubs, 0.0)), axis=0, keepdims=True)
        rest = functools.reduce(jnp.add, [ref[pl.ds(tile, 1), :] for ref in rest_sums])
        far_sum = late_sums_ref[pl.ds(tile, 1), :] + jnp.where(is_hub, 0.0, rest)
        row = (near_sum + far_sum) * (1.0 / total_columns)
        mean_ref[pl.ds(tile, 1), :] = row
        mean = as_column(row)
        spread_ref[target, :] = mean
        for n in range(near):
            value = (held[n] - mean).astype(jnp.bfloat16)
            fluct_ref[target, n * width : (n + 1) * width] = value
            if n < near - 1:
                turned_ref[n * width : (n + 1) * width, target] = jnp.transpose(value)

    over_tiles(rows // LANES, one_tile)
    for first in range(0, near * width, 2 * width):
        columns = slice(first, min(first + 2 * width, near * width))
        tiles_ref[:, columns] = product(turned_ref[0 : half * width, :], fluct_ref[:, columns])

    def tile_of(offset, rel, rows):
        row = near_column(offset, late, half)
        column = near_column(rel // 2, late, half) + half * (rel % 2)
        rows = pl.ds(pl.multiple_of(row * width + rows.start, rows.size), rows.size)
        return tiles_ref[rows, pl.ds(pl.multiple_of(column * width, width), width)]

    place_tiles(False, tile_of, out_refs)


def far_same_kernel(half, spread_ref, same_ref, turned_ref, tiles_ref, fluct_ref):
    rows, width = same_ref.shape

    def one_tile(tile):
        target = pl.ds(pl.multiple_of(tile * LANES, LANES), LANES)
        fluct_ref[target, :] = (same_ref[target, :].astype(jnp.float32) - spread_ref[target, :]).astype(jnp.bfloat16)

    over_tiles(rows // LANES, one_tile)
    kept = half - 1
    for odd in (0, 1):
        first = odd * half * width
        column = product(turned_ref[first : first + kept * width, :], fluct_ref[...])
        for n in range(kept):
            tile = column[n * width : (n + 1) * width, :]
            tiles_ref[odd * kept + n] = jnp.transpose(tile)
            if not odd:
                tiles_ref[2 * kept + n] = tile


def far_other_kernel(half, spread_ref, other_ref, turned_ref, held_ref, *refs):
    out_refs, (fluct_ref, tiles_ref) = refs[:-2], refs[-2:]
    rows, width = other_ref.shape

    def one_tile(tile):
        target = pl.ds(pl.multiple_of(tile * LANES, LANES), LANES)
        fluct_ref[target, :] = (other_ref[target, :].astype(jnp.float32) - spread_ref[target, :]).astype(jnp.bfloat16)

    over_tiles(rows // LANES, one_tile)
    kept = half - 1
    column = product(turned_ref[0 : kept * width, :], fluct_ref[...])
    for n in range(kept):
        tiles_ref[n] = column[n * width : (n + 1) * width, :]
    late = lax.axis_size("snap") // 4

    def tile_of(offset, rel, rows):
        other, odd = rel // 2, rel % 2
        row = near_column(offset, late, half)
        mirrored = near_column(other, late, half) + kept * odd
        fresh = (other == late) & (odd == 1)
        place = jnp.where(fresh, 0, jnp.where(offset == late, mirrored, 2 * kept + row))
        return jnp.where(fresh, tiles_ref[jnp.where(fresh, row, 0), rows, :], held_ref[place, rows, :])

    place_tiles(True, tile_of, out_refs)


def far_rounds(chip_count):
    wanted = []
    for chip in range(chip_count // 4, 3 * chip_count // 4):
        for offset in range(1, chip_count):
            kinds = [[tile_kind(chip, core, offset, k, 2 * chip_count)[1] for k in range(chip_count + 1)] for core in (0, 1)]
            count = max(sum(kind) for kind in kinds)
            if count:
                wanted.append((-count, chip, chip ^ offset))
    rounds = []
    for count, source, target in sorted(wanted):
        for pairs, _ in rounds:
            if source not in pairs and target not in pairs.values():
                pairs[source] = target
                break
        else:
            rounds.append(({source: target}, -count))
    return rounds


def joined_near_kernel(space_count, mean_ref, *refs):
    firsts, out_refs = refs[:space_count], refs[space_count:]
    me = lax.axis_index("snap")
    _, part_rows, width = firsts[0].shape
    band = out_refs[0].shape[1] // width
    chip_count = len(out_refs) + 1
    near_refs = dict(zip([offset for offset in range(chip_count) if offset != chip_count // 2], out_refs))
    slot = 0
    for offset, out_ref in near_refs.items():
        for k in range(band):
            near = tile_kind(me // 2, me % 2, offset, k, lax.axis_size("snap"))[0]
            lanes = slice(k * width, (k + 1) * width)

            @pl.when(jnp.logical_not(near))
            def _(out_ref=out_ref, lanes=lanes):
                out_ref[0:part_rows, lanes] = jnp.zeros((part_rows, width), jnp.float32)

            @pl.when(near)
            def _(out_ref=out_ref, lanes=lanes, slot=slot):
                out_ref[0:part_rows, lanes] = functools.reduce(jnp.add, [ref[slot] for ref in firsts])

            slot = slot + jnp.where(near, 1, 0)
        put_means(mean_ref, out_ref, part_rows)


def put_means(mean_ref, out_ref, first_row):
    across = out_ref.shape[1] // LANES
    for n in range(mean_ref.shape[0]):
        lanes = slice((n % across) * LANES, (n % across + 1) * LANES)
        out_ref[first_row + n // across : first_row + n // across + 1, lanes] = mean_ref[n : n + 1, :]


def joined_far_kernel(rounds, space_count, *refs):
    seconds, out_refs = refs[:space_count], refs[space_count:]
    me = lax.axis_index("snap")
    chip = me // 2
    _, _, width = seconds[0].shape
    chip_count = lax.axis_size("snap") // 2
    band = chip_count + 1
    slot = 0
    for offset in range(chip_count):
        here = [(0, chip_count)] if offset == 0 else []
        here += [(n + 1, source) for n, (pairs, _) in enumerate(rounds) for source in pairs if pairs[source] == source ^ offset]
        place = 0
        for k in range(band):
            far = tile_kind(chip, me % 2, offset, k, 2 * chip_count)[1]
            for n, source in here:
                mine = far if source == chip_count else jnp.logical_and(far, chip == source)

                @pl.when(mine)
                def _(n=n, slot=slot, place=place):
                    total = functools.reduce(jnp.add, [ref[slot] for ref in seconds])
                    lanes = pl.ds(pl.multiple_of(place * width, width), width)
                    out_refs[n][:, lanes] = total

            slot = slot + jnp.where(far, 1, 0)
            place = place + jnp.where(far, 1, 0)


def collected_kernel(first_chip, rounds, scale, *refs):
    me = lax.axis_index("snap")
    chip, core = me // 2, me % 2
    chip_count = lax.axis_size("snap") // 2
    hub_chips = chip_count // 2
    late = chip_count // 2
    nears, fars, (gram_ref, mean_ref) = refs[: chip_count - 1], refs[chip_count - 1 : -2], refs[-2:]
    nears = dict(zip([offset for offset in range(chip_count) if offset != late], nears))
    part_rows, columns = gram_ref.shape
    is_hub = (chip >= first_chip) & (chip < first_chip + hub_chips)
    total = jnp.zeros((part_rows, columns), jnp.float32)
    for offset, ref in nears.items():
        hub = (chip ^ offset) - first_chip
        held = True if offset < 2 else (hub >= 0) & (hub < hub_chips)
        total = total + jnp.where(held, ref[0:part_rows, :], 0.0)
    gram_ref[...] = total * scale
    for n, ref in enumerate(fars):
        source = jnp.where(is_hub, chip, -1)
        if n:
            source = -1
            for a, b in rounds[n - 1][0].items():
                source = jnp.where(chip == b, a, source)
        place = 0
        for k in range(columns // LANES):
            far = jnp.logical_and(source >= 0, tile_kind(source, core, source ^ chip, k, 2 * chip_count)[1])
            lanes = slice(k * LANES, (k + 1) * LANES)

            @pl.when(far)
            def _(ref=ref, lanes=lanes, place=place):
                sent = ref[:, pl.ds(pl.multiple_of(place * LANES, LANES), LANES)]
                gram_ref[:, lanes] = gram_ref[:, lanes] + sent * scale

            place = place + jnp.where(far, 1, 0)
    mean_rows = mean_ref.shape[0] // hub_chips
    across = columns // LANES
    for offset, ref in nears.items():
        hub = (chip ^ offset) - first_chip
        if offset == 0:
            hub = jnp.where(is_hub, hub, (chip ^ late) - first_chip)

        @pl.when((hub >= 0) & (hub < hub_chips))
        def _(ref=ref, hub=hub):
            for n in range(mean_rows):
                row, lanes = part_rows + n // across, slice((n % across) * LANES, (n % across + 1) * LANES)
                mean_ref[pl.ds(hub * mean_rows + n, 1), :] = ref[row : row + 1, lanes]


def per_device(snapshots):
    snap_count = lax.axis_size("snap")
    space_count = lax.axis_size("space")
    row_count, width = snapshots.shape
    chip_count = snap_count // 2
    first_chip, hub_chips = chip_count // 4, chip_count // 2
    hubs = list(range(2 * first_chip, 2 * (first_chip + hub_chips)))
    rows = row_count // hub_chips
    band = chip_count + 1
    part_rows = width // space_count
    late = chip_count // 2
    early = [offset for offset in range(chip_count) if offset not in (late, late ^ 1)] + [late ^ 1]
    near = 2 * len(early)
    vmem = pl.BlockSpec(memory_space=pltpu.VMEM)

    def shaped(dtype, *shape):
        return jax.ShapeDtypeStruct(shape, dtype)

    def kernel(body, operands, out_shapes, scratch=(), flops=1000, raw=False):
        sizes = [int(np.prod(s.shape)) * jnp.dtype(s.dtype).itemsize for s in (*operands, *out_shapes)]
        sizes += [int(np.prod(s.shape)) * jnp.dtype(s.dtype).itemsize for s in scratch if hasattr(s, "shape") and s.memory_space == pltpu.VMEM]
        return pl.pallas_call(
            body,
            out_shape=list(out_shapes),
            in_specs=[pl.BlockSpec(memory_space=pltpu.HBM) if raw else vmem] * len(operands),
            out_specs=[vmem] * len(out_shapes),
            scratch_shapes=list(scratch),
            cost_estimate=pl.CostEstimate(flops=flops, bytes_accessed=0, transcendentals=0),
            compiler_params=pltpu.CompilerParams(vmem_limit_bytes=sum(sizes) + (6 << 20)),
        )(*operands)

    def hub_of(device):
        chip = device // 2
        is_hub = (chip >= first_chip) & (chip < first_chip + hub_chips)
        return (jnp.where(is_hub, chip, chip ^ late) - first_chip) * rows

    def to_hubs(x, offset, name):
        pairs = [(h ^ (2 * offset), h) for h in hubs]
        if name == "sums" or offset == 1:
            pairs = [(i ^ (2 * offset), i) for i in range(snap_count)]
        elif offset != late:
            pairs = completed(pairs, snap_count)
        return lax.ppermute(x, "snap", pairs)

    def to_other_core(x):
        return lax.ppermute(x, "snap", [(i, i ^ 1) for i in range(snap_count)])

    piece = shaped(snapshots.dtype, rows, width)
    sums = shaped(jnp.float32, rows // LANES, LANES)
    offsets = early + [late]
    pieces = kernel(
        functools.partial(split_kernel, hub_of, offsets),
        [pltpu.with_memory_space_constraint(snapshots, pltpu.HBM)],
        [piece] * chip_count,
        [pltpu.SemaphoreType.DMA((chip_count,))],
        raw=True,
    )
    summed = [late] + early[2:]
    by_offset = dict(zip(offsets, pieces))
    (far_sums,) = kernel(
        sums_kernel,
        [by_offset[offset] for offset in summed],
        [shaped(jnp.float32, len(summed) * (rows // LANES), LANES)],
    )
    blocks = {0: pieces[0]}
    for offset, x in zip(offsets[1:], pieces[1:]):
        blocks[offset] = to_hubs(x, offset, "bulk")
    chip_sums = kernel(chip_sums_kernel, [far_sums, to_other_core(far_sums)], [sums] * len(summed))
    came = {offset: to_hubs(x, offset, "sums") for offset, x in zip(summed, chip_sums)}
    passed = {offset: to_other_core(blocks[offset]) for offset in offsets}

    first_slots, second_slots = slot_count(snap_count, False), slot_count(snap_count, True)
    half, kept = len(early), len(early) - 1
    turned, mean_rows, spread, *first = kernel(
        functools.partial(early_kernel, width * snap_count, near),
        [came[offset] for offset in summed] + [blocks[offset] for offset in early] + [passed[offset] for offset in early],
        [shaped(jnp.bfloat16, (near - 1) * width, rows), sums, shaped(jnp.float32, rows, LANES)]
        + [shaped(jnp.float32, first_slots, part_rows, width)] * space_count,
        [pltpu.VMEM((rows, near * width), jnp.bfloat16), pltpu.VMEM((half * width, near * width), jnp.float32)],
        flops=near * near * width * width * rows,
    )
    flops = 2 * snap_count * width * width * rows
    (held,) = kernel(
        functools.partial(far_same_kernel, half),
        [spread, blocks[late], turned],
        [shaped(jnp.float32, 3 * kept, width, width)],
        [pltpu.VMEM((rows, width), jnp.bfloat16)],
        flops=flops,
    )
    second = kernel(
        functools.partial(far_other_kernel, half),
        [spread, passed[late], turned, held],
        [shaped(jnp.float32, second_slots, part_rows, width)] * space_count,
        [pltpu.VMEM((rows, width), jnp.bfloat16), pltpu.VMEM((kept, width, width), jnp.float32)],
        flops=flops,
    )

    def over_space(parts):
        got = [parts[0]]
        for n in range(1, space_count):
            got.append(lax.ppermute(parts[n], "space", [(s, s ^ n) for s in range(space_count)]))
        return got

    mean_space = -(-(-(-(rows // LANES) // band)) // 8) * 8
    slab = shaped(jnp.float32, part_rows + mean_space, band * width)
    near_slabs = kernel(
        functools.partial(joined_near_kernel, space_count), [mean_rows, *over_space(first)], [slab] * len(early)
    )

    nears = [near_slabs[0]]
    for offset, x in zip(early[1:], near_slabs[1:]):
        sources = range(snap_count) if offset == 1 else hubs
        pairs = completed([(i, i ^ (2 * offset)) for i in sources], snap_count)
        nears.append(lax.ppermute(x, "snap", pairs))
    rounds = far_rounds(chip_count)
    far_slabs = kernel(
        functools.partial(joined_far_kernel, rounds, space_count),
        over_space(second),
        [shaped(jnp.float32, part_rows, count * width) for count in [band] + [count for _, count in rounds]],
    )
    fars = [far_slabs[0]]
    for n, (pairs, _) in enumerate(rounds):
        devices = [(2 * a + core, 2 * b + core) for a, b in pairs.items() for core in (0, 1)]
        fars.append(lax.ppermute(far_slabs[n + 1], "snap", completed(devices, snap_count)))
    gram_band, mean_field = kernel(
        functools.partial(collected_kernel, first_chip, rounds, 1.0 / (row_count * space_count)),
        nears + fars,
        [shaped(jnp.float32, part_rows, band * width), shaped(jnp.float32, row_count // LANES, LANES)],
    )
    return gram_band, mean_field.reshape(row_count)


def solution(mesh):
    return jax.shard_map(
        per_device,
        mesh=mesh,
        in_specs=(P("space", "snap"),),
        out_specs=(P(("snap", "space"), None), P("space")),
        check_vma=False,
    )
```

time: 79.3 us -> 71 us (0.90)
  the two profiles are of different devices: /device:TPU:12 before, /device:TPU:0 now
where the time goes in v7:
time: 71 us; the launch traced here: 70.8 us
  waiting for transfers between devices  31.8 us (45%)
  starting transfers between devices  27.8 us (39%)
  Pallas kernels  10.5 us (15%)
  between operations  0.77 us (1%)
    ppermute x5, waiting for transfers between devices, to_hubs(): return lax.ppermute(x, 'snap', pairs)  25.4 us
    ppermute x5, starting transfers between devices, to_hubs(): return lax.ppermute(x, 'snap', pairs)  13.2 us
    pallas_call x9, Pallas kernels, kernel(): pl.pallas_call(body, out_shape=list(out_shapes), in_specs=[pl.BlockSpec(m...  10.5 us
    ppermute x6, starting transfers between devices, over_space(): lax.ppermute(parts[n], 'space', [(s, s ^ n) for s in range(space_count)])  8.97 us
    ppermute x2, starting transfers between devices, per_device(): lax.ppermute(far_slabs[n + 1], 'snap', completed(devices, snap_count))  3.8 us
    ppermute x2, waiting for transfers between devices, per_device(): lax.ppermute(far_slabs[n + 1], 'snap', completed(devices, snap_count))  3.23 us
    ppermute x6, waiting for transfers between devices, over_space(): lax.ppermute(parts[n], 'space', [(s, s ^ n) for s in range(space_count)])  2.08 us
  transfers between devices with their start and end apart: 20, of which 8 were waited for; matrix products, arithmetic and copies ran while one was open for 0% of the time, Pallas kernels for 11%

profile of v7, /device:TPU:0, one launch (start us, length us, event | category | flops | bytes accessed | tf_op | source)
XLA Modules:
  0.0 70.8 jit_solution(1193450013023703193)
XLA Ops:
  0.6 1.6 %shard_map.30 = (bf16[2048,128]{1,0:T(8,128)(2,1)S(1)}, bf16[2048,128]{1,0:T(8,128)(2,1)S(1)}, bf16[2048,128]{1,0:T(8,128)(2,1)S(1)}, bf16[2048,128]{1,0:T(8,128)(2,1)S(1)}) custom-call(bf16[4096,128]{1,0:T(8,128)(2,1)} %rows_ref.1), custom_call_target="tpu_custom_call" | custom-call | flops 1000 | tf_op jit(solution)/shard_map/pallas_call | solution.py:354
  2.2 0.7 collective-permute-start.4
  2.9 5.9 %collective-permute-start.3 = (bf16[2048,128]{1,0:T(8,128)(2,1)S(1)}, bf16[2048,128]{1,0:T(8,128)(2,1)S(1)}, u32[]{:S(2)}, u32[]{:S(2)}) collective-permute-start(bf16[2048,128]{1,0:T(8,128)(2,1)S(1)} %get-tuple-element.32), channel_id=1, source_target_pairs={{8,0},{12,4},{0,8},{4,12},{24,16},{28,20},{16,24},{20,28},{9,1},{1... | collective-permute-start | bytes 1572872 | tf_op jit(solution)/shard_map/ppermute | solution.py:375
  8.8 1.8 %collective-permute-start.13 = (bf16[2048,128]{1,0:T(8,128)(2,1)S(1)}, bf16[2048,128]{1,0:T(8,128)(2,1)S(1)}, u32[]{:S(2)}, u32[]{:S(2)}) collective-permute-start(bf16[2048,128]{1,0:T(8,128)(2,1)S(1)} %get-tuple-element.27.refs_0_), channel_id=1, source_target_pairs={{24,8},{28,12},{0,16},{4,20},{25,9},{29,13},{1,17},{5,21},{26,10},... | collective-permute-start | bytes 1572872 | tf_op jit(solution)/shard_map/ppermute | solution.py:375
  10.7 0.1 collective-permute-start.5
  10.8 0.5 collective-permute-start.7
  11.2 9.9 %collective-permute-done.3.refs_2_ = bf16[2048,128]{1,0:T(8,128)(2,1)S(1)} collective-permute-done((bf16[2048,128]{1,0:T(8,128)(2,1)S(1)}, bf16[2048,128]{1,0:T(8,128)(2,1)S(1)}, u32[]{:S(2)}, u32[]{:S(2)}) %collective-permute-start.3) | collective-permute-done | bytes 524320 | tf_op jit(solution)/shard_map/ppermute | solution.py:375
  21.1 9.8 %collective-permute-done.13.same_ref = bf16[2048,128]{1,0:T(8,128)(2,1)S(1)} collective-permute-done((bf16[2048,128]{1,0:T(8,128)(2,1)S(1)}, bf16[2048,128]{1,0:T(8,128)(2,1)S(1)}, u32[]{:S(2)}, u32[]{:S(2)}) %collective-permute-start.13) | collective-permute-done | bytes 524320 | tf_op jit(solution)/shard_map/ppermute | solution.py:375
  31.0 0.3 shard_map.31.own_ref
  31.3 0.6 collective-permute-start
  31.9 1.0 %collective-permute-done.mate_ref = f32[32,128]{1,0:T(8,128)S(1)} collective-permute-done((f32[32,128]{1,0:T(8,128)S(1)}, f32[32,128]{1,0:T(8,128)S(1)}, u32[]{:S(2)}, u32[]{:S(2)}) %collective-permute-start) | collective-permute-done | bytes 16416 | tf_op jit(solution)/shard_map/ppermute | solution.py:378
  32.9 3.4 %collective-permute-start.1 = (f32[16,128]{1,0:T(8,128)S(1)}, f32[16,128]{1,0:T(8,128)S(1)}, u32[]{:S(2)}, u32[]{:S(2)}) collective-permute-start(f32[16,128]{1,0:T(8,128)S(1)} %get-tuple-element.29), channel_id=1, source_target_pairs={{16,0},{20,4},{24,8},{28,12},{0,16},{4,20},{8,24},{12,28},{17,1},{... | collective-permute-start | bytes 24584 | tf_op jit(solution)/shard_map/ppermute | solution.py:375
  36.3 1.6 %collective-permute-done.1.late_sums_ref = f32[16,128]{1,0:T(8,128)S(1)} collective-permute-done((f32[16,128]{1,0:T(8,128)S(1)}, f32[16,128]{1,0:T(8,128)S(1)}, u32[]{:S(2)}, u32[]{:S(2)}) %collective-permute-start.1) | collective-permute-done | bytes 8224 | tf_op jit(solution)/shard_map/ppermute | solution.py:375
  37.9 1.3 %collective-permute-start.2 = (f32[16,128]{1,0:T(8,128)S(1)}, f32[16,128]{1,0:T(8,128)S(1)}, u32[]{:S(2)}, u32[]{:S(2)}) collective-permute-start(f32[16,128]{1,0:T(8,128)S(1)} %get-tuple-element.30), channel_id=1, source_target_pairs={{24,0},{28,4},{16,8},{20,12},{8,16},{12,20},{0,24},{4,28},{25,1},{... | collective-permute-start | bytes 24584 | tf_op jit(solution)/shard_map/ppermute | solution.py:375
  39.3 4.1 %collective-permute-done.2.refs_0_ = f32[16,128]{1,0:T(8,128)S(1)} collective-permute-done((f32[16,128]{1,0:T(8,128)S(1)}, f32[16,128]{1,0:T(8,128)S(1)}, u32[]{:S(2)}, u32[]{:S(2)}) %collective-permute-start.2) | collective-permute-done | bytes 8224 | tf_op jit(solution)/shard_map/ppermute | solution.py:375
  43.4 5.0 %shard_map.33 = (bf16[640,2048]{1,0:T(8,128)(2,1)S(1)}, f32[16,128]{1,0:T(8,128)S(1)}, f32[2048,128]{1,0:T(8,128)S(1)}, f32[12,32,128]{2,1,0:T(8,128)S(1)}, f32[...) custom-call(f32[16,128]{1,0:T(8,128)S(1)} %collective-permute-done.1.late_sums_ref, ...), custom_call_target="tpu_custom_call" | custom-call | flops 1207959552 | tf_op jit(solution)/shard_map/pallas_call | solution.py:354
  48.4 2.5 %collective-permute-start.10 = (f32[12,32,128]{2,1,0:T(8,128)S(1)}, f32[12,32,128]{2,1,0:T(8,128)S(1)}, u32[]{:S(2)}, u32[]{:S(2)}) collective-permute-start(f32[12,32,128]{2,1,0:T(8,128)S(1)} %get-tuple-element.37), channel_id=1, source_target_pairs={{0,3},{1,2},{2,1},{3,0},{4,7},{5,6},{6,5},{7,4},{8,11},{9,10},{10,... | collective-permute-start | bytes 589832 | tf_op jit(solution)/shard_map/ppermute | solution.py:433
  50.9 0.5 collective-permute-start.8
  51.5 0.5 collective-permute-start.9
  52.0 0.9 %shard_map.35.held_ref = f32[6,128,128]{2,1,0:T(8,128)S(1)} custom-call(f32[2048,128]{1,0:T(8,128)S(1)} %get-tuple-element.41.spread_ref, bf16[2048,128]{1,0:T(8,128)(2,1)S(1)} %collective-permute-done.13.same_ref, bf16[640,2048]{1,0:T(8,128)(2,1)S(1)} %get-tuple-element.42.turned_ref), custom_call_target="tpu_custom_call" | custom-call | flops 536870912 | tf_op jit(solution)/shard_map/pallas_call | solution.py:354
  52.9 1.3 %shard_map.36 = (f32[6,32,128]{2,1,0:T(8,128)S(1)}, f32[6,32,128]{2,1,0:T(8,128)S(1)}, f32[6,32,128]{2,1,0:T(8,128)S(1)}, f32[6,32,128]{2,1,0:T(8,128)S(1)}) custom-call(f32[2048,128]{1,0:T(8,128)S(1)} %get-tuple-element.41.spread_ref, bf16[2048,128]{1,0:T(8,128)(2,1)S(1)} %collective-permute-done.14.other_ref, ...), custom_call_target="tpu_custom_call" | custom-call | flops 536870912 | tf_op jit(solution)/shard_map/pallas_call | solution.py:354
  54.2 1.6 %collective-permute-start.15 = (f32[6,32,128]{2,1,0:T(8,128)S(1)}, f32[6,32,128]{2,1,0:T(8,128)S(1)}, u32[]{:S(2)}, u32[]{:S(2)}) collective-permute-start(f32[6,32,128]{2,1,0:T(8,128)S(1)} %get-tuple-element.44), channel_id=1, source_target_pairs={{0,1},{1,0},{2,3},{3,2},{4,5},{5,4},{6,7},{7,6},{8,9},{9,8},{10,11... | collective-permute-start | bytes 294920 | tf_op jit(solution)/shard_map/ppermute | solution.py:433
  55.7 1.5 %collective-permute-start.16 = (f32[6,32,128]{2,1,0:T(8,128)S(1)}, f32[6,32,128]{2,1,0:T(8,128)S(1)}, u32[]{:S(2)}, u32[]{:S(2)}) collective-permute-start(f32[6,32,128]{2,1,0:T(8,128)S(1)} %get-tuple-element.45), channel_id=1, source_target_pairs={{0,2},{1,3},{2,0},{3,1},{4,6},{5,7},{6,4},{7,5},{8,10},{9,11},{10,... | collective-permute-start | bytes 294920 | tf_op jit(solution)/shard_map/ppermute | solution.py:433
  57.3 2.3 %collective-permute-start.17 = (f32[6,32,128]{2,1,0:T(8,128)S(1)}, f32[6,32,128]{2,1,0:T(8,128)S(1)}, u32[]{:S(2)}, u32[]{:S(2)}) collective-permute-start(f32[6,32,128]{2,1,0:T(8,128)S(1)} %get-tuple-element.46), channel_id=1, source_target_pairs={{0,3},{1,2},{2,1},{3,0},{4,7},{5,6},{6,5},{7,4},{8,11},{9,10},{10,... | collective-permute-start | bytes 294920 | tf_op jit(solution)/shard_map/ppermute | solution.py:433
  59.6 1.1 %collective-permute-done.8.refs_1_ = f32[12,32,128]{2,1,0:T(8,128)S(1)} collective-permute-done((f32[12,32,128]{2,1,0:T(8,128)S(1)}, f32[12,32,128]{2,1,0:T(8,128)S(1)}, u32[]{:S(2)}, u32[]{:S(2)}) %collective-permute-start.8) | collective-permute-done | bytes 196640 | tf_op jit(solution)/shard_map/ppermute | solution.py:433
  60.7 0.3 shard_map.34
  61.1 0.7 collective-permute-start.12
  61.8 1.0 %collective-permute-done.17.refs_3_ = f32[6,32,128]{2,1,0:T(8,128)S(1)} collective-permute-done((f32[6,32,128]{2,1,0:T(8,128)S(1)}, f32[6,32,128]{2,1,0:T(8,128)S(1)}, u32[]{:S(2)}, u32[]{:S(2)}) %collective-permute-start.17) | collective-permute-done | bytes 98336 | tf_op jit(solution)/shard_map/ppermute | solution.py:433
  62.8 3.1 %collective-permute-start.18 = (f32[32,512]{1,0:T(8,128)S(1)}, f32[32,512]{1,0:T(8,128)S(1)}, u32[]{:S(2)}, u32[]{:S(2)}) collective-permute-start(f32[32,512]{1,0:T(8,128)S(1)} %get-tuple-element.48), channel_id=1, source_target_pairs={{8,24},{12,28},{16,0},{20,4},{0,8},{4,12},{24,16},{28,20},{9,25},{... | collective-permute-start | bytes 196616 | tf_op jit(solution)/shard_map/ppermute | solution.py:456
  65.9 0.7 collective-permute-start.19
  66.6 3.2 %collective-permute-done.18.refs_4_ = f32[32,512]{1,0:T(8,128)S(1)} collective-permute-done((f32[32,512]{1,0:T(8,128)S(1)}, f32[32,512]{1,0:T(8,128)S(1)}, u32[]{:S(2)}, u32[]{:S(2)}) %collective-permute-start.18) | collective-permute-done | bytes 65568 | tf_op jit(solution)/shard_map/ppermute | solution.py:456
  69.8 1.0 %shard_map.38 = (f32[32,640]{1,0:T(8,128)}, f32[32,128]{1,0:T(8,128)}) custom-call(f32[40,640]{1,0:T(8,128)S(1)} %get-tuple-element.38.refs_0_, f32[40,640]{1,0:T(8,128)S(1)} %collective-permute-done.11.refs_1_, f32[40,640]{1,0:T(8,128)S(1)} %collective-permute-done.12.refs_2_, f32[32,640]{1,0:T(8,128)S(1)} %get-tuple-element.47.refs_3_, ...), custom_call_target="tpu_custom_call" | custom-call | flops 1000 | tf_op jit(solution)/shard_map/pallas_call | solution.py:354
  (17 shorter events, 0.1 us)
Async XLA Ops:
  2.2 8.5 %collective-permute-start.4 = (bf16[2048,128]{1,0:T(8,128)(2,1)S(1)}, bf16[2048,128]{1,0:T(8,128)(2,1)S(1)}, u32[]{:S(2)}, u32[]{:S(2)}) collective-permute-start(bf16[2048,128]{1,0:T(8,128)(2,1)S(1)} %get-tuple-element.28.refs_1_), channel_id=1, source_target_pairs={{16,8},{20,12},{8,16},{12,20},{0,0},{4,4},{24,24},{28,28},{17,9},{... | collective-permute-start | bytes 1572872 | tf_op jit(solution)/shard_map/ppermute | solution.py:375
  2.9 18.2 %collective-permute-start.3 = (bf16[2048,128]{1,0:T(8,128)(2,1)S(1)}, bf16[2048,128]{1,0:T(8,128)(2,1)S(1)}, u32[]{:S(2)}, u32[]{:S(2)}) collective-permute-start(bf16[2048,128]{1,0:T(8,128)(2,1)S(1)} %get-tuple-element.32), channel_id=1, source_target_pairs={{8,0},{12,4},{0,8},{4,12},{24,16},{28,20},{16,24},{20,28},{9,1},{1... | collective-permute-start | bytes 1572872 | tf_op jit(solution)/shard_map/ppermute | solution.py:375
  8.8 22.1 %collective-permute-start.13 = (bf16[2048,128]{1,0:T(8,128)(2,1)S(1)}, bf16[2048,128]{1,0:T(8,128)(2,1)S(1)}, u32[]{:S(2)}, u32[]{:S(2)}) collective-permute-start(bf16[2048,128]{1,0:T(8,128)(2,1)S(1)} %get-tuple-element.27.refs_0_), channel_id=1, source_target_pairs={{24,8},{28,12},{0,16},{4,20},{25,9},{29,13},{1,17},{5,21},{26,10},... | collective-permute-start | bytes 1572872 | tf_op jit(solution)/shard_map/ppermute | solution.py:375
  10.7 32.7 %collective-permute-start.5 = (bf16[2048,128]{1,0:T(8,128)(2,1)S(1)}, bf16[2048,128]{1,0:T(8,128)(2,1)S(1)}, u32[]{:S(2)}, u32[]{:S(2)}) collective-permute-start(bf16[2048,128]{1,0:T(8,128)(2,1)S(1)} %get-tuple-element.31.refs_1_), channel_id=1, source_target_pairs={{0,4},{4,0},{8,12},{12,8},{16,20},{20,16},{24,28},{28,24},{1,5},{5... | collective-permute-start | bytes 1572872 | tf_op jit(solution)/shard_map/ppermute | solution.py:378
  10.8 32.6 %collective-permute-start.7 = (bf16[2048,128]{1,0:T(8,128)(2,1)S(1)}, bf16[2048,128]{1,0:T(8,128)(2,1)S(1)}, u32[]{:S(2)}, u32[]{:S(2)}) collective-permute-start(bf16[2048,128]{1,0:T(8,128)(2,1)S(1)} %collective-permute-done.4.refs_3_), channel_id=1, source_target_pairs={{0,4},{4,0},{8,12},{12,8},{16,20},{20,16},{24,28},{28,24},{1,5},{5... | collective-permute-start | bytes 1572872 | tf_op jit(solution)/shard_map/ppermute | solution.py:378
  21.1 22.2 %collective-permute-start.6 = (bf16[2048,128]{1,0:T(8,128)(2,1)S(1)}, bf16[2048,128]{1,0:T(8,128)(2,1)S(1)}, u32[]{:S(2)}, u32[]{:S(2)}) collective-permute-start(bf16[2048,128]{1,0:T(8,128)(2,1)S(1)} %collective-permute-done.3.refs_2_), channel_id=1, source_target_pairs={{0,4},{4,0},{8,12},{12,8},{16,20},{20,16},{24,28},{28,24},{1,5},{5... | collective-permute-start | bytes 1572872 | tf_op jit(solution)/shard_map/ppermute | solution.py:378
  31.0 21.9 %collective-permute-start.14 = (bf16[2048,128]{1,0:T(8,128)(2,1)S(1)}, bf16[2048,128]{1,0:T(8,128)(2,1)S(1)}, u32[]{:S(2)}, u32[]{:S(2)}) collective-permute-start(bf16[2048,128]{1,0:T(8,128)(2,1)S(1)} %collective-permute-done.13.same_ref), channel_id=1, source_target_pairs={{0,4},{4,0},{8,12},{12,8},{16,20},{20,16},{24,28},{28,24},{1,5},{5... | collective-permute-start | bytes 1572872 | tf_op jit(solution)/shard_map/ppermute | solution.py:378
  31.3 1.6 %collective-permute-start = (f32[32,128]{1,0:T(8,128)S(1)}, f32[32,128]{1,0:T(8,128)S(1)}, u32[]{:S(2)}, u32[]{:S(2)}) collective-permute-start(f32[32,128]{1,0:T(8,128)S(1)} %shard_map.31.own_ref), channel_id=1, source_target_pairs={{0,4},{4,0},{8,12},{12,8},{16,20},{20,16},{24,28},{28,24},{1,5},{5... | collective-permute-start | bytes 49160 | tf_op jit(solution)/shard_map/ppermute | solution.py:378
  32.9 5.0 %collective-permute-start.1 = (f32[16,128]{1,0:T(8,128)S(1)}, f32[16,128]{1,0:T(8,128)S(1)}, u32[]{:S(2)}, u32[]{:S(2)}) collective-permute-start(f32[16,128]{1,0:T(8,128)S(1)} %get-tuple-element.29), channel_id=1, source_target_pairs={{16,0},{20,4},{24,8},{28,12},{0,16},{4,20},{8,24},{12,28},{17,1},{... | collective-permute-start | bytes 24584 | tf_op jit(solution)/shard_map/ppermute | solution.py:375
  37.9 5.4 %collective-permute-start.2 = (f32[16,128]{1,0:T(8,128)S(1)}, f32[16,128]{1,0:T(8,128)S(1)}, u32[]{:S(2)}, u32[]{:S(2)}) collective-permute-start(f32[16,128]{1,0:T(8,128)S(1)} %get-tuple-element.30), channel_id=1, source_target_pairs={{24,0},{28,4},{16,8},{20,12},{8,16},{12,20},{0,24},{4,28},{25,1},{... | collective-permute-start | bytes 24584 | tf_op jit(solution)/shard_map/ppermute | solution.py:375
  48.4 8.8 %collective-permute-start.10 = (f32[12,32,128]{2,1,0:T(8,128)S(1)}, f32[12,32,128]{2,1,0:T(8,128)S(1)}, u32[]{:S(2)}, u32[]{:S(2)}) collective-permute-start(f32[12,32,128]{2,1,0:T(8,128)S(1)} %get-tuple-element.37), channel_id=1, source_target_pairs={{0,3},{1,2},{2,1},{3,0},{4,7},{5,6},{6,5},{7,4},{8,11},{9,10},{10,... | collective-permute-start | bytes 589832 | tf_op jit(solution)/shard_map/ppermute | solution.py:433
  50.9 9.8 %collective-permute-start.8 = (f32[12,32,128]{2,1,0:T(8,128)S(1)}, f32[12,32,128]{2,1,0:T(8,128)S(1)}, u32[]{:S(2)}, u32[]{:S(2)}) collective-permute-start(f32[12,32,128]{2,1,0:T(8,128)S(1)} %get-tuple-element.35), channel_id=1, source_target_pairs={{0,1},{1,0},{2,3},{3,2},{4,5},{5,4},{6,7},{7,6},{8,9},{9,8},{10,11... | collective-permute-start | bytes 589832 | tf_op jit(solution)/shard_map/ppermute | solution.py:433
  51.5 9.2 %collective-permute-start.9 = (f32[12,32,128]{2,1,0:T(8,128)S(1)}, f32[12,32,128]{2,1,0:T(8,128)S(1)}, u32[]{:S(2)}, u32[]{:S(2)}) collective-permute-start(f32[12,32,128]{2,1,0:T(8,128)S(1)} %get-tuple-element.36), channel_id=1, source_target_pairs={{0,2},{1,3},{2,0},{3,1},{4,6},{5,7},{6,4},{7,5},{8,10},{9,11},{10,... | collective-permute-start | bytes 589832 | tf_op jit(solution)/shard_map/ppermute | solution.py:433
  54.2 7.6 %collective-permute-start.15 = (f32[6,32,128]{2,1,0:T(8,128)S(1)}, f32[6,32,128]{2,1,0:T(8,128)S(1)}, u32[]{:S(2)}, u32[]{:S(2)}) collective-permute-start(f32[6,32,128]{2,1,0:T(8,128)S(1)} %get-tuple-element.44), channel_id=1, source_target_pairs={{0,1},{1,0},{2,3},{3,2},{4,5},{5,4},{6,7},{7,6},{8,9},{9,8},{10,11... | collective-permute-start | bytes 294920 | tf_op jit(solution)/shard_map/ppermute | solution.py:433
  55.7 6.1 %collective-permute-start.16 = (f32[6,32,128]{2,1,0:T(8,128)S(1)}, f32[6,32,128]{2,1,0:T(8,128)S(1)}, u32[]{:S(2)}, u32[]{:S(2)}) collective-permute-start(f32[6,32,128]{2,1,0:T(8,128)S(1)} %get-tuple-element.45), channel_id=1, source_target_pairs={{0,2},{1,3},{2,0},{3,1},{4,6},{5,7},{6,4},{7,5},{8,10},{9,11},{10,... | collective-permute-start | bytes 294920 | tf_op jit(solution)/shard_map/ppermute | solution.py:433
  57.3 5.5 %collective-permute-start.17 = (f32[6,32,128]{2,1,0:T(8,128)S(1)}, f32[6,32,128]{2,1,0:T(8,128)S(1)}, u32[]{:S(2)}, u32[]{:S(2)}) collective-permute-start(f32[6,32,128]{2,1,0:T(8,128)S(1)} %get-tuple-element.46), channel_id=1, source_target_pairs={{0,3},{1,2},{2,1},{3,0},{4,7},{5,6},{6,5},{7,4},{8,11},{9,10},{10,... | collective-permute-start | bytes 294920 | tf_op jit(solution)/shard_map/ppermute | solution.py:433
  61.0 8.8 %collective-permute-start.11 = (f32[40,640]{1,0:T(8,128)S(1)}, f32[40,640]{1,0:T(8,128)S(1)}, u32[]{:S(2)}, u32[]{:S(2)}) collective-permute-start(f32[40,640]{1,0:T(8,128)S(1)} %get-tuple-element.39), channel_id=1, source_target_pairs={{0,8},{4,12},{8,0},{12,4},{16,24},{20,28},{24,16},{28,20},{1,9},{5... | collective-permute-start | bytes 307208 | tf_op jit(solution)/shard_map/ppermute | solution.py:446
  61.1 8.7 %collective-permute-start.12 = (f32[40,640]{1,0:T(8,128)S(1)}, f32[40,640]{1,0:T(8,128)S(1)}, u32[]{:S(2)}, u32[]{:S(2)}) collective-permute-start(f32[40,640]{1,0:T(8,128)S(1)} %get-tuple-element.40), channel_id=1, source_target_pairs={{8,16},{12,20},{16,8},{20,12},{0,0},{4,4},{24,24},{28,28},{9,17},{... | collective-permute-start | bytes 307208 | tf_op jit(solution)/shard_map/ppermute | solution.py:446
  62.8 7.0 %collective-permute-start.18 = (f32[32,512]{1,0:T(8,128)S(1)}, f32[32,512]{1,0:T(8,128)S(1)}, u32[]{:S(2)}, u32[]{:S(2)}) collective-permute-start(f32[32,512]{1,0:T(8,128)S(1)} %get-tuple-element.48), channel_id=1, source_target_pairs={{8,24},{12,28},{16,0},{20,4},{0,8},{4,12},{24,16},{28,20},{9,25},{... | collective-permute-start | bytes 196616 | tf_op jit(solution)/shard_map/ppermute | solution.py:456
  65.9 0.7 collective-permute-start.19

commit v8 on v7

--- a/solution.py
+++ b/solution.py
@@ -11,6 +11,8 @@
 
 
 LANES = 128
+CHUNKS = 4
+UNROLLED = 32
 
 
 def completed(pairs, count):
@@ -39,6 +41,11 @@
     return jnp.where(offset == late ^ 1, count - 1, offset - jnp.where(offset > late, 2, 0))
 
 
+def other_column(offset, late, count):
+    column = near_column(offset, late, count)
+    return jnp.where(offset == 1, count - 1, column - jnp.where(column > 1, 1, 0))
+
+
 def place_tiles(wanted_far, tile_of, out_refs):
     me, space = lax.axis_index("snap"), lax.axis_index("space")
     snap_count = lax.axis_size("snap")
@@ -59,7 +66,12 @@
 
         return slot + jnp.where(wanted, 1, 0)
 
-    lax.fori_loop(0, chip_count * band, one, 0)
+    if chip_count * band > UNROLLED:
+        lax.fori_loop(0, chip_count * band, one, 0)
+        return
+    slot = 0
+    for pair in range(chip_count * band):
+        slot = one(pair, slot)
 
 
 def slot_count(snap_count, wanted_far):
@@ -78,23 +90,16 @@
 
 
 def over_tiles(count, one_tile):
-    group = math.gcd(count, 4)
-
-    def some(step, carry):
-        for n in range(group):
-            one_tile(step * group + n)
-        return carry
-
-    lax.fori_loop(0, count // group, some, 0)
-
-
-def split_kernel(hub_of, offsets, rows_ref, *refs):
-    pieces, sems = refs[:-1], refs[-1]
+    for tile in range(count):
+        one_tile(tile)
+
+
+def split_kernel(hub_of, rows_ref, own_ref, next_ref, sems):
     me = lax.axis_index("snap")
     copies = []
-    for n, offset in enumerate(offsets):
-        first = pl.multiple_of(hub_of(me ^ (2 * offset)), pieces[0].shape[0])
-        copies.append(pltpu.make_async_copy(rows_ref.at[pl.ds(first, pieces[0].shape[0]), :], pieces[n], sems.at[n]))
+    for n, (device, piece_ref) in enumerate(((me, own_ref), (me ^ 2, next_ref))):
+        first = pl.multiple_of(hub_of(device), piece_ref.shape[0])
+        copies.append(pltpu.make_async_copy(rows_ref.at[pl.ds(first, piece_ref.shape[0]), :], piece_ref, sems.at[n]))
     for copy in copies:
         copy.start()
     for copy in copies:
@@ -118,65 +123,78 @@
         out_ref[...] = own_ref[rows, :] + mate_ref[rows, :]
 
 
-def early_kernel(total_columns, near, late_sums_ref, *refs):
-    half = near // 2
-    rest_sums, blocks = refs[: half - 2], refs[half - 2 : half - 2 + near]
-    turned_ref, mean_ref, spread_ref, *out_refs = refs[half - 2 + near : -2]
-    fluct_ref, tiles_ref = refs[-2:]
+def near_kernel(total_columns, half, chunks, *refs):
+    sums_refs, blocks = refs[: half + 1], refs[half + 1 : 3 * half]
+    turned_ref, mean_ref, spread_ref, tiles_ref, fluct_ref = refs[3 * half :]
     rows, width = blocks[0].shape
+    step = rows // chunks
+    for chunk in range(chunks):
+        for tile in range(chunk * step // LANES, (chunk + 1) * step // LANES):
+            target = slice(tile * LANES, (tile + 1) * LANES)
+            total = functools.reduce(jnp.add, [ref[tile : tile + 1, :] for ref in sums_refs])
+            row = total * (1.0 / total_columns)
+            mean_ref[tile : tile + 1, :] = row
+            mean = as_column(row)
+            spread_ref[target, :] = mean
+            for n, ref in enumerate(blocks):
+                value = (ref[target, :].astype(jnp.float32) - mean).astype(jnp.bfloat16)
+                fluct_ref[target, n * width : (n + 1) * width] = value
+                if n < len(blocks) - 1:
+                    turned_ref[n * width : (n + 1) * width, target] = jnp.transpose(value)
+        across = slice(chunk * step, (chunk + 1) * step)
+        left = turned_ref[0 : half * width, across]
+        for first in range(0, len(blocks) * width, 2 * width):
+            columns = slice(first, min(first + 2 * width, len(blocks) * width))
+            part = product(left, fluct_ref[across, columns])
+            tiles_ref[:, columns] = part if chunk == 0 else tiles_ref[:, columns] + part
+
+
+def near_last_kernel(half, spread_ref, last_ref, turned_ref, held_ref, last_turned_ref, *refs):
+    out_refs, (fluct_ref, tiles_ref) = refs[:-2], refs[-2:]
+    rows, width = last_ref.shape
     late = lax.axis_size("snap") // 4
-    chip = lax.axis_index("snap") // 2
-    is_hub = (chip >= late // 2) & (chip < late // 2 + late)
 
     def one_tile(tile):
-        target = pl.ds(pl.multiple_of(tile * LANES, LANES), LANES)
-        held = [ref[target, :].astype(jnp.float32) for ref in blocks]
-        always = functools.reduce(jnp.add, [held[n] for n in range(near) if n % half < 2])
-        at_hubs = functools.reduce(jnp.add, [held[n] for n in range(near) if n % half >= 2])
-        near_sum = jnp.sum(jnp.transpose(always + jnp.where(is_hub, at_hubs, 0.0)), axis=0, keepdims=True)
-        rest = functools.reduce(jnp.add, [ref[pl.ds(tile, 1), :] for ref in rest_sums])
-        far_sum = late_sums_ref[pl.ds(tile, 1), :] + jnp.where(is_hub, 0.0, rest)
-        row = (near_sum + far_sum) * (1.0 / total_columns)
-        mean_ref[pl.ds(tile, 1), :] = row
-        mean = as_column(row)
-        spread_ref[target, :] = mean
-        for n in range(near):
-            value = (held[n] - mean).astype(jnp.bfloat16)
-            fluct_ref[target, n * width : (n + 1) * width] = value
-            if n < near - 1:
-                turned_ref[n * width : (n + 1) * width, target] = jnp.transpose(value)
+        target = slice(tile * LANES, (tile + 1) * LANES)
+        value = (last_ref[target, :].astype(jnp.float32) - spread_ref[target, :]).astype(jnp.bfloat16)
+        fluct_ref[target, :] = value
+        last_turned_ref[:, target] = jnp.transpose(value)
 
     over_tiles(rows // LANES, one_tile)
-    for first in range(0, near * width, 2 * width):
-        columns = slice(first, min(first + 2 * width, near * width))
-        tiles_ref[:, columns] = product(turned_ref[0 : half * width, :], fluct_ref[:, columns])
+    tiles_ref[...] = product(turned_ref[0 : half * width, :], fluct_ref[...])
 
     def tile_of(offset, rel, rows):
         row = near_column(offset, late, half)
-        column = near_column(rel // 2, late, half) + half * (rel % 2)
+        other = rel // 2
+        odd = rel % 2 == 1
+        column = jnp.where(odd, half + other_column(other, late, half), near_column(other, late, half))
+        last = column == 2 * half - 1
         rows = pl.ds(pl.multiple_of(row * width + rows.start, rows.size), rows.size)
-        return tiles_ref[rows, pl.ds(pl.multiple_of(column * width, width), width)]
+        lanes = pl.ds(pl.multiple_of(jnp.where(last, 0, column) * width, width), width)
+        return jnp.where(last, tiles_ref[rows, :], held_ref[rows, lanes])
 
     place_tiles(False, tile_of, out_refs)
 
 
-def far_same_kernel(half, spread_ref, same_ref, turned_ref, tiles_ref, fluct_ref):
+def far_same_kernel(half, spread_ref, same_ref, turned_ref, last_turned_ref, tiles_ref, fluct_ref):
     rows, width = same_ref.shape
 
     def one_tile(tile):
-        target = pl.ds(pl.multiple_of(tile * LANES, LANES), LANES)
+        target = slice(tile * LANES, (tile + 1) * LANES)
         fluct_ref[target, :] = (same_ref[target, :].astype(jnp.float32) - spread_ref[target, :]).astype(jnp.bfloat16)
 
     over_tiles(rows // LANES, one_tile)
     kept = half - 1
-    for odd in (0, 1):
-        first = odd * half * width
-        column = product(turned_ref[first : first + kept * width, :], fluct_ref[...])
-        for n in range(kept):
-            tile = column[n * width : (n + 1) * width, :]
-            tiles_ref[odd * kept + n] = jnp.transpose(tile)
-            if not odd:
-                tiles_ref[2 * kept + n] = tile
+    own = product(turned_ref[0 : kept * width, :], fluct_ref[...])
+    other = product(turned_ref[half * width : (half + kept - 1) * width, :], fluct_ref[...])
+    last = product(last_turned_ref[...], fluct_ref[...])
+    for n in range(kept):
+        tile = own[n * width : (n + 1) * width, :]
+        tiles_ref[n] = jnp.transpose(tile)
+        tiles_ref[2 * kept + n] = tile
+    for n in range(kept - 1):
+        tiles_ref[kept + n] = jnp.transpose(other[n * width : (n + 1) * width, :])
+    tiles_ref[2 * kept - 1] = jnp.transpose(last)
 
 
 def far_other_kernel(half, spread_ref, other_ref, turned_ref, held_ref, *refs):
@@ -184,7 +202,7 @@
     rows, width = other_ref.shape
 
     def one_tile(tile):
-        target = pl.ds(pl.multiple_of(tile * LANES, LANES), LANES)
+        target = slice(tile * LANES, (tile + 1) * LANES)
         fluct_ref[target, :] = (other_ref[target, :].astype(jnp.float32) - spread_ref[target, :]).astype(jnp.bfloat16)
 
     over_tiles(rows // LANES, one_tile)
@@ -197,7 +215,9 @@
     def tile_of(offset, rel, rows):
         other, odd = rel // 2, rel % 2
         row = near_column(offset, late, half)
-        mirrored = near_column(other, late, half) + kept * odd
+        beyond = other_column(other, late, half)
+        beyond = kept + jnp.where(other == 1, kept - 1, beyond)
+        mirrored = jnp.where(odd == 1, beyond, near_column(other, late, half))
         fresh = (other == late) & (odd == 1)
         place = jnp.where(fresh, 0, jnp.where(offset == late, mirrored, 2 * kept + row))
         return jnp.where(fresh, tiles_ref[jnp.where(fresh, row, 0), rows, :], held_ref[place, rows, :])
@@ -380,41 +400,51 @@
     piece = shaped(snapshots.dtype, rows, width)
     sums = shaped(jnp.float32, rows // LANES, LANES)
     offsets = early + [late]
-    pieces = kernel(
-        functools.partial(split_kernel, hub_of, offsets),
+    own_piece, next_piece = kernel(
+        functools.partial(split_kernel, hub_of),
         [pltpu.with_memory_space_constraint(snapshots, pltpu.HBM)],
-        [piece] * chip_count,
-        [pltpu.SemaphoreType.DMA((chip_count,))],
+        [piece] * 2,
+        [pltpu.SemaphoreType.DMA((2,))],
         raw=True,
     )
-    summed = [late] + early[2:]
-    by_offset = dict(zip(offsets, pieces))
-    (far_sums,) = kernel(
-        sums_kernel,
-        [by_offset[offset] for offset in summed],
-        [shaped(jnp.float32, len(summed) * (rows // LANES), LANES)],
-    )
-    blocks = {0: pieces[0]}
-    for offset, x in zip(offsets[1:], pieces[1:]):
-        blocks[offset] = to_hubs(x, offset, "bulk")
-    chip_sums = kernel(chip_sums_kernel, [far_sums, to_other_core(far_sums)], [sums] * len(summed))
-    came = {offset: to_hubs(x, offset, "sums") for offset, x in zip(summed, chip_sums)}
+    pieces = {}
+    for offset in offsets:
+        if offset in (0, 1, late, late ^ 1):
+            pieces[offset] = own_piece if offset in (0, late) else next_piece
+        elif offset ^ late in pieces:
+            pieces[offset] = pieces[offset ^ late]
+        else:
+            pieces[offset] = lax.dynamic_slice_in_dim(snapshots, hub_of(lax.axis_index("snap") ^ (2 * offset)), rows, 0)
+    blocks = {0: own_piece} | {offset: to_hubs(pieces[offset], offset, "bulk") for offset in offsets[1:]}
+
+    distinct = list({id(x): x for x in pieces.values()}.values())
+    place = {offset: [x is pieces[offset] for x in distinct].index(True) for offset in offsets}
+    (row_sums,) = kernel(sums_kernel, distinct, [shaped(jnp.float32, len(distinct) * (rows // LANES), LANES)])
+    chip_sums = kernel(chip_sums_kernel, [row_sums, to_other_core(row_sums)], [sums] * len(distinct))
+    came = [chip_sums[place[0]]] + [to_hubs(chip_sums[place[offset]], offset, "sums") for offset in offsets[1:]]
     passed = {offset: to_other_core(blocks[offset]) for offset in offsets}
 
     first_slots, second_slots = slot_count(snap_count, False), slot_count(snap_count, True)
     half, kept = len(early), len(early) - 1
-    turned, mean_rows, spread, *first = kernel(
-        functools.partial(early_kernel, width * snap_count, near),
-        [came[offset] for offset in summed] + [blocks[offset] for offset in early] + [passed[offset] for offset in early],
-        [shaped(jnp.bfloat16, (near - 1) * width, rows), sums, shaped(jnp.float32, rows, LANES)]
-        + [shaped(jnp.float32, first_slots, part_rows, width)] * space_count,
-        [pltpu.VMEM((rows, near * width), jnp.bfloat16), pltpu.VMEM((half * width, near * width), jnp.float32)],
+    products = shaped(jnp.float32, half * width, (near - 1) * width)
+    turned, mean_rows, spread, near_held = kernel(
+        functools.partial(near_kernel, width * snap_count, half, math.gcd(rows // LANES, CHUNKS)),
+        came + [blocks[offset] for offset in early] + [passed[offset] for offset in early if offset != 1],
+        [shaped(jnp.bfloat16, (near - 2) * width, rows), sums, shaped(jnp.float32, rows, LANES), products],
+        [pltpu.VMEM((rows, (near - 1) * width), jnp.bfloat16)],
         flops=near * near * width * width * rows,
+    )
+    last_turned, *first = kernel(
+        functools.partial(near_last_kernel, half),
+        [spread, passed[1], turned, near_held],
+        [shaped(jnp.bfloat16, width, rows)] + [shaped(jnp.float32, first_slots, part_rows, width)] * space_count,
+        [pltpu.VMEM((rows, width), jnp.bfloat16), pltpu.VMEM((half * width, width), jnp.float32)],
+        flops=2 * half * width * width * rows,
     )
     flops = 2 * snap_count * width * width * rows
     (held,) = kernel(
         functools.partial(far_same_kernel, half),
-        [spread, blocks[late], turned],
+        [spread, blocks[late], turned, last_turned],
         [shaped(jnp.float32, 3 * kept, width, width)],
         [pltpu.VMEM((rows, width), jnp.bfloat16)],
         flops=flops,

time: 71 us -> 72.4 us (1.020)
  starting transfers between devices: 27.8 us -> 31.9 us
  Pallas kernels: 10.5 us -> 7.31 us
    pallas_call x9 -> x10, Pallas kernels: 10.5 us -> 7.31 us  [kernel(): pl.pallas_call(body, out_shape=list(out_shapes), in_specs=[pl.BlockSpec(m...]
    ppermute x5 -> x6, waiting for transfers between devices: 25.4 us -> 27.6 us  [to_hubs(): return lax.ppermute(x, 'snap', pairs)]
    ppermute x6, starting transfers between devices: 8.97 us -> 10.5 us  [over_space(): lax.ppermute(parts[n], 'space', [(s, s ^ n) for s in range(space_count)])]
    ppermute x5 -> x6, starting transfers between devices: 13.2 us -> 14.5 us  [to_hubs(): return lax.ppermute(x, 'snap', pairs)]
    ppermute x2, waiting for transfers between devices: 3.23 us -> 2.1 us  [per_device(): lax.ppermute(far_slabs[n + 1], 'snap', completed(devices, snap_count))]
  transfers between devices with their start and end apart: 20 -> 21, of which waited for: 8 -> 9; matrix products, arithmetic and copies ran while one was open for 0% -> 0% of each run, Pallas kernels for 11% -> 7%
where the time goes in v8:
time: 72.4 us; the launch traced here: 72.2 us
  waiting for transfers between devices  32.2 us (44%)
  starting transfers between devices  31.9 us (44%)
  Pallas kernels  7.31 us (10%)
  between operations  0.77 us (1%)
    ppermute x6, waiting for transfers between devices, to_hubs(): return lax.ppermute(x, 'snap', pairs)  27.6 us
    ppermute x6, starting transfers between devices, to_hubs(): return lax.ppermute(x, 'snap', pairs)  14.5 us
    ppermute x6, starting transfers between devices, over_space(): lax.ppermute(parts[n], 'space', [(s, s ^ n) for s in range(space_count)])  10.5 us
    pallas_call x10, Pallas kernels, kernel(): pl.pallas_call(body, out_shape=list(out_shapes), in_specs=[pl.BlockSpec(m...  7.31 us
    ppermute x2, starting transfers between devices, per_device(): lax.ppermute(far_slabs[n + 1], 'snap', completed(devices, snap_count))  4.4 us
    ppermute x2, waiting for transfers between devices, per_device(): lax.ppermute(far_slabs[n + 1], 'snap', completed(devices, snap_count))  2.1 us
    ppermute x6, waiting for transfers between devices, over_space(): lax.ppermute(parts[n], 'space', [(s, s ^ n) for s in range(space_count)])  1.46 us
  transfers between devices with their start and end apart: 21, of which 9 were waited for; matrix products, arithmetic and copies ran while one was open for 0% of the time, Pallas kernels for 7%

profile of v8, /device:TPU:0, one launch (start us, length us, event | category | flops | bytes accessed | tf_op | source)
XLA Modules:
  0.0 72.2 jit_solution(3003598283803103046)
XLA Ops:
  0.6 1.2 %shard_map.30 = (bf16[2048,128]{1,0:T(8,128)(2,1)S(1)}, bf16[2048,128]{1,0:T(8,128)(2,1)S(1)}) custom-call(bf16[4096,128]{1,0:T(8,128)(2,1)} %rows_ref.1), custom_call_target="tpu_custom_call" | custom-call | flops 1000 | tf_op jit(solution)/shard_map/pallas_call | solution.py:374
  1.9 0.7 collective-permute-start.5
  2.6 5.9 %collective-permute-start.4 = (bf16[2048,128]{1,0:T(8,128)(2,1)S(1)}, bf16[2048,128]{1,0:T(8,128)(2,1)S(1)}, u32[]{:S(2)}, u32[]{:S(2)}) collective-permute-start(bf16[2048,128]{1,0:T(8,128)(2,1)S(1)} %get-tuple-element.28.refs_1_), channel_id=1, source_target_pairs={{8,0},{12,4},{0,8},{4,12},{24,16},{28,20},{16,24},{20,28},{9,1},{1... | collective-permute-start | bytes 1572872 | tf_op jit(solution)/shard_map/ppermute | solution.py:395
  8.5 1.8 %collective-permute-start.14 = (bf16[2048,128]{1,0:T(8,128)(2,1)S(1)}, bf16[2048,128]{1,0:T(8,128)(2,1)S(1)}, u32[]{:S(2)}, u32[]{:S(2)}) collective-permute-start(bf16[2048,128]{1,0:T(8,128)(2,1)S(1)} %get-tuple-element.27.refs_0_.refs_4_), channel_id=1, source_target_pairs={{24,8},{28,12},{0,16},{4,20},{25,9},{29,13},{1,17},{5,21},{26,10},... | collective-permute-start | bytes 1572872 | tf_op jit(solution)/shard_map/ppermute | solution.py:395
  10.9 9.9 %collective-permute-done.4.refs_5_ = bf16[2048,128]{1,0:T(8,128)(2,1)S(1)} collective-permute-done((bf16[2048,128]{1,0:T(8,128)(2,1)S(1)}, bf16[2048,128]{1,0:T(8,128)(2,1)S(1)}, u32[]{:S(2)}, u32[]{:S(2)}) %collective-permute-start.4) | collective-permute-done | bytes 524320 | tf_op jit(solution)/shard_map/ppermute | solution.py:395
  20.8 9.8 %collective-permute-done.14.same_ref = bf16[2048,128]{1,0:T(8,128)(2,1)S(1)} collective-permute-done((bf16[2048,128]{1,0:T(8,128)(2,1)S(1)}, bf16[2048,128]{1,0:T(8,128)(2,1)S(1)}, u32[]{:S(2)}, u32[]{:S(2)}) %collective-permute-start.14) | collective-permute-done | bytes 524320 | tf_op jit(solution)/shard_map/ppermute | solution.py:395
  31.0 0.6 collective-permute-start
  31.5 1.0 %collective-permute-done.mate_ref = f32[32,128]{1,0:T(8,128)S(1)} collective-permute-done((f32[32,128]{1,0:T(8,128)S(1)}, f32[32,128]{1,0:T(8,128)S(1)}, u32[]{:S(2)}, u32[]{:S(2)}) %collective-permute-start) | collective-permute-done | bytes 16416 | tf_op jit(solution)/shard_map/ppermute | solution.py:398
  32.6 2.4 %collective-permute-start.1 = (f32[16,128]{1,0:T(8,128)S(1)}, f32[16,128]{1,0:T(8,128)S(1)}, u32[]{:S(2)}, u32[]{:S(2)}) collective-permute-start(f32[16,128]{1,0:T(8,128)S(1)} %get-tuple-element.30), channel_id=1, source_target_pairs={{8,0},{12,4},{0,8},{4,12},{24,16},{28,20},{16,24},{20,28},{9,1},{1... | collective-permute-start | bytes 24584 | tf_op jit(solution)/shard_map/ppermute | solution.py:395
  34.9 1.6 %collective-permute-done.1.refs_1_ = f32[16,128]{1,0:T(8,128)S(1)} collective-permute-done((f32[16,128]{1,0:T(8,128)S(1)}, f32[16,128]{1,0:T(8,128)S(1)}, u32[]{:S(2)}, u32[]{:S(2)}) %collective-permute-start.1) | collective-permute-done | bytes 8224 | tf_op jit(solution)/shard_map/ppermute | solution.py:395
  36.6 2.5 %collective-permute-start.2 = (f32[16,128]{1,0:T(8,128)S(1)}, f32[16,128]{1,0:T(8,128)S(1)}, u32[]{:S(2)}, u32[]{:S(2)}) collective-permute-start(f32[16,128]{1,0:T(8,128)S(1)} %get-tuple-element.30), channel_id=1, source_target_pairs={{24,0},{28,4},{16,8},{20,12},{8,16},{12,20},{0,24},{4,28},{25,1},{... | collective-permute-start | bytes 24584 | tf_op jit(solution)/shard_map/ppermute | solution.py:395
  39.0 3.0 %collective-permute-done.2.refs_2_ = f32[16,128]{1,0:T(8,128)S(1)} collective-permute-done((f32[16,128]{1,0:T(8,128)S(1)}, f32[16,128]{1,0:T(8,128)S(1)}, u32[]{:S(2)}, u32[]{:S(2)}) %collective-permute-start.2) | collective-permute-done | bytes 8224 | tf_op jit(solution)/shard_map/ppermute | solution.py:395
  42.0 1.2 %collective-permute-start.3 = (f32[16,128]{1,0:T(8,128)S(1)}, f32[16,128]{1,0:T(8,128)S(1)}, u32[]{:S(2)}, u32[]{:S(2)}) collective-permute-start(f32[16,128]{1,0:T(8,128)S(1)} %get-tuple-element.29.refs_0_), channel_id=1, source_target_pairs={{16,0},{20,4},{24,8},{28,12},{0,16},{4,20},{8,24},{12,28},{17,1},{... | collective-permute-start | bytes 24584 | tf_op jit(solution)/shard_map/ppermute | solution.py:395
  43.2 3.3 %collective-permute-done.3.refs_3_ = f32[16,128]{1,0:T(8,128)S(1)} collective-permute-done((f32[16,128]{1,0:T(8,128)S(1)}, f32[16,128]{1,0:T(8,128)S(1)}, u32[]{:S(2)}, u32[]{:S(2)}) %collective-permute-start.3) | collective-permute-done | bytes 8224 | tf_op jit(solution)/shard_map/ppermute | solution.py:395
  46.6 1.9 %shard_map.33 = (bf16[512,2048]{1,0:T(8,128)(2,1)S(1)}, f32[16,128]{1,0:T(8,128)S(1)}, f32[2048,128]{1,0:T(8,128)S(1)}, f32[384,640]{1,0:T(8,128)S(1)}) custom-call(f32[16,128]{1,0:T(8,128)S(1)} %get-tuple-element.29.refs_0_, f32[16,128]{1,0:T(8,128)S(1)} %collective-permute-done.1.refs_1_, f32[16,128]{1,0:T(8,128)S(1)} %collective-permute-done.2.refs_2_, ...), custom_call_target="tpu_custom_call" | custom-call | flops 1207959552 | tf_op jit(solution)/shard_map/pallas_call | solution.py:374
  48.5 0.9 %shard_map.34 = (bf16[128,2048]{1,0:T(8,128)(2,1)S(1)}, f32[12,32,128]{2,1,0:T(8,128)S(1)}, f32[12,32,128]{2,1,0:T(8,128)S(1)}, f32[12,32,128]{2,1,0:T(8,128)S(1)}, f32[12,32,128]{2,1,0:T(8,128)S(1)}) custom-call(f32[2048,128]{1,0:T(8,128)S(1)} %get-tuple-element.32.spread_ref, bf16[2048,128]{1,0:T(8,128)(2,1)S(1)} %collective-permute-done.8.last_ref, ...), custom_call_target="tpu_custom_call" | custom-call | flops 201326592 | tf_op jit(solution)/shard_map/pallas_call | solution.py:374
  49.5 1.6 %collective-permute-start.10 = (f32[12,32,128]{2,1,0:T(8,128)S(1)}, f32[12,32,128]{2,1,0:T(8,128)S(1)}, u32[]{:S(2)}, u32[]{:S(2)}) collective-permute-start(f32[12,32,128]{2,1,0:T(8,128)S(1)} %get-tuple-element.37), channel_id=1, source_target_pairs={{0,2},{1,3},{2,0},{3,1},{4,6},{5,7},{6,4},{7,5},{8,10},{9,11},{10,... | collective-permute-start | bytes 589832 | tf_op jit(solution)/shard_map/ppermute | solution.py:463
  51.0 1.4 %collective-permute-start.11 = (f32[12,32,128]{2,1,0:T(8,128)S(1)}, f32[12,32,128]{2,1,0:T(8,128)S(1)}, u32[]{:S(2)}, u32[]{:S(2)}) collective-permute-start(f32[12,32,128]{2,1,0:T(8,128)S(1)} %get-tuple-element.38), channel_id=1, source_target_pairs={{0,3},{1,2},{2,1},{3,0},{4,7},{5,6},{6,5},{7,4},{8,11},{9,10},{10,... | collective-permute-start | bytes 589832 | tf_op jit(solution)/shard_map/ppermute | solution.py:463
  52.5 0.5 collective-permute-start.9
  53.0 0.8 %shard_map.36.held_ref = f32[6,128,128]{2,1,0:T(8,128)S(1)} custom-call(f32[2048,128]{1,0:T(8,128)S(1)} %get-tuple-element.32.spread_ref, bf16[2048,128]{1,0:T(8,128)(2,1)S(1)} %collective-permute-done.14.same_ref, bf16[512,2048]{1,0:T(8,128)(2,1)S(1)} %get-tuple-element.33.turned_ref, bf16[128,2048]{1,0:T(8,128)(2,1)S(1)} %get-tuple-element.42.last_turned_ref), custom_call_target="tpu_custom_call" | custom-call | flops 536870912 | tf_op jit(solution)/shard_map/pallas_call | solution.py:374
  53.8 0.7 %shard_map.37 = (f32[6,32,128]{2,1,0:T(8,128)S(1)}, f32[6,32,128]{2,1,0:T(8,128)S(1)}, f32[6,32,128]{2,1,0:T(8,128)S(1)}, f32[6,32,128]{2,1,0:T(8,128)S(1)}) custom-call(f32[2048,128]{1,0:T(8,128)S(1)} %get-tuple-element.32.spread_ref, bf16[2048,128]{1,0:T(8,128)(2,1)S(1)} %collective-permute-done.15.other_ref, ...), custom_call_target="tpu_custom_call" | custom-call | flops 536870912 | tf_op jit(solution)/shard_map/pallas_call | solution.py:374
  54.6 1.6 %collective-permute-start.16 = (f32[6,32,128]{2,1,0:T(8,128)S(1)}, f32[6,32,128]{2,1,0:T(8,128)S(1)}, u32[]{:S(2)}, u32[]{:S(2)}) collective-permute-start(f32[6,32,128]{2,1,0:T(8,128)S(1)} %get-tuple-element.44), channel_id=1, source_target_pairs={{0,1},{1,0},{2,3},{3,2},{4,5},{5,4},{6,7},{7,6},{8,9},{9,8},{10,11... | collective-permute-start | bytes 294920 | tf_op jit(solution)/shard_map/ppermute | solution.py:463
  56.1 1.5 %collective-permute-start.17 = (f32[6,32,128]{2,1,0:T(8,128)S(1)}, f32[6,32,128]{2,1,0:T(8,128)S(1)}, u32[]{:S(2)}, u32[]{:S(2)}) collective-permute-start(f32[6,32,128]{2,1,0:T(8,128)S(1)} %get-tuple-element.45), channel_id=1, source_target_pairs={{0,2},{1,3},{2,0},{3,1},{4,6},{5,7},{6,4},{7,5},{8,10},{9,11},{10,... | collective-permute-start | bytes 294920 | tf_op jit(solution)/shard_map/ppermute | solution.py:463
  57.6 0.5 collective-permute-done.10.refs_2_
  58.2 3.9 %collective-permute-start.18 = (f32[6,32,128]{2,1,0:T(8,128)S(1)}, f32[6,32,128]{2,1,0:T(8,128)S(1)}, u32[]{:S(2)}, u32[]{:S(2)}) collective-permute-start(f32[6,32,128]{2,1,0:T(8,128)S(1)} %get-tuple-element.46), channel_id=1, source_target_pairs={{0,3},{1,2},{2,1},{3,0},{4,7},{5,6},{6,5},{7,4},{8,11},{9,10},{10,... | collective-permute-start | bytes 294920 | tf_op jit(solution)/shard_map/ppermute | solution.py:463
  62.4 0.6 collective-permute-start.12
  63.1 0.7 collective-permute-start.13
  63.7 0.9 %collective-permute-done.18.refs_3_ = f32[6,32,128]{2,1,0:T(8,128)S(1)} collective-permute-done((f32[6,32,128]{2,1,0:T(8,128)S(1)}, f32[6,32,128]{2,1,0:T(8,128)S(1)}, u32[]{:S(2)}, u32[]{:S(2)}) %collective-permute-start.18) | collective-permute-done | bytes 98336 | tf_op jit(solution)/shard_map/ppermute | solution.py:463
  64.7 3.8 %collective-permute-start.19 = (f32[32,512]{1,0:T(8,128)S(1)}, f32[32,512]{1,0:T(8,128)S(1)}, u32[]{:S(2)}, u32[]{:S(2)}) collective-permute-start(f32[32,512]{1,0:T(8,128)S(1)} %get-tuple-element.48), channel_id=1, source_target_pairs={{8,24},{12,28},{16,0},{20,4},{0,8},{4,12},{24,16},{28,20},{9,25},{... | collective-permute-start | bytes 196616 | tf_op jit(solution)/shard_map/ppermute | solution.py:486
  68.4 0.7 collective-permute-start.20
  69.1 2.1 %collective-permute-done.19.refs_4_ = f32[32,512]{1,0:T(8,128)S(1)} collective-permute-done((f32[32,512]{1,0:T(8,128)S(1)}, f32[32,512]{1,0:T(8,128)S(1)}, u32[]{:S(2)}, u32[]{:S(2)}) %collective-permute-start.19) | collective-permute-done | bytes 65568 | tf_op jit(solution)/shard_map/ppermute | solution.py:486
  71.2 1.0 %shard_map.39 = (f32[32,640]{1,0:T(8,128)}, f32[32,128]{1,0:T(8,128)}) custom-call(f32[40,640]{1,0:T(8,128)S(1)} %get-tuple-element.39.refs_0_, f32[40,640]{1,0:T(8,128)S(1)} %collective-permute-done.12.refs_1_, f32[40,640]{1,0:T(8,128)S(1)} %collective-permute-done.13.refs_2_, f32[32,640]{1,0:T(8,128)S(1)} %get-tuple-element.47.refs_3_, ...), custom_call_target="tpu_custom_call" | custom-call | flops 1000 | tf_op jit(solution)/shard_map/pallas_call | solution.py:374
  (20 shorter events, 1.3 us)
Async XLA Ops:
  1.9 8.5 %collective-permute-start.5 = (bf16[2048,128]{1,0:T(8,128)(2,1)S(1)}, bf16[2048,128]{1,0:T(8,128)(2,1)S(1)}, u32[]{:S(2)}, u32[]{:S(2)}) collective-permute-start(bf16[2048,128]{1,0:T(8,128)(2,1)S(1)} %get-tuple-element.28.refs_1_), channel_id=1, source_target_pairs={{16,8},{20,12},{8,16},{12,20},{0,0},{4,4},{24,24},{28,28},{17,9},{... | collective-permute-start | bytes 1572872 | tf_op jit(solution)/shard_map/ppermute | solution.py:395
  2.6 18.2 %collective-permute-start.4 = (bf16[2048,128]{1,0:T(8,128)(2,1)S(1)}, bf16[2048,128]{1,0:T(8,128)(2,1)S(1)}, u32[]{:S(2)}, u32[]{:S(2)}) collective-permute-start(bf16[2048,128]{1,0:T(8,128)(2,1)S(1)} %get-tuple-element.28.refs_1_), channel_id=1, source_target_pairs={{8,0},{12,4},{0,8},{4,12},{24,16},{28,20},{16,24},{20,28},{9,1},{1... | collective-permute-start | bytes 1572872 | tf_op jit(solution)/shard_map/ppermute | solution.py:395
  8.5 22.1 %collective-permute-start.14 = (bf16[2048,128]{1,0:T(8,128)(2,1)S(1)}, bf16[2048,128]{1,0:T(8,128)(2,1)S(1)}, u32[]{:S(2)}, u32[]{:S(2)}) collective-permute-start(bf16[2048,128]{1,0:T(8,128)(2,1)S(1)} %get-tuple-element.27.refs_0_.refs_4_), channel_id=1, source_target_pairs={{24,8},{28,12},{0,16},{4,20},{25,9},{29,13},{1,17},{5,21},{26,10},... | collective-permute-start | bytes 1572872 | tf_op jit(solution)/shard_map/ppermute | solution.py:395
  10.3 36.2 %collective-permute-start.6 = (bf16[2048,128]{1,0:T(8,128)(2,1)S(1)}, bf16[2048,128]{1,0:T(8,128)(2,1)S(1)}, u32[]{:S(2)}, u32[]{:S(2)}) collective-permute-start(bf16[2048,128]{1,0:T(8,128)(2,1)S(1)} %get-tuple-element.27.refs_0_.refs_4_), channel_id=1, source_target_pairs={{0,4},{4,0},{8,12},{12,8},{16,20},{20,16},{24,28},{28,24},{1,5},{5... | collective-permute-start | bytes 1572872 | tf_op jit(solution)/shard_map/ppermute | solution.py:398
  10.4 36.1 %collective-permute-start.7 = (bf16[2048,128]{1,0:T(8,128)(2,1)S(1)}, bf16[2048,128]{1,0:T(8,128)(2,1)S(1)}, u32[]{:S(2)}, u32[]{:S(2)}) collective-permute-start(bf16[2048,128]{1,0:T(8,128)(2,1)S(1)} %collective-permute-done.5.refs_6_), channel_id=1, source_target_pairs={{0,4},{4,0},{8,12},{12,8},{16,20},{20,16},{24,28},{28,24},{1,5},{5... | collective-permute-start | bytes 1572872 | tf_op jit(solution)/shard_map/ppermute | solution.py:398
  20.8 27.7 %collective-permute-start.8 = (bf16[2048,128]{1,0:T(8,128)(2,1)S(1)}, bf16[2048,128]{1,0:T(8,128)(2,1)S(1)}, u32[]{:S(2)}, u32[]{:S(2)}) collective-permute-start(bf16[2048,128]{1,0:T(8,128)(2,1)S(1)} %collective-permute-done.4.refs_5_), channel_id=1, source_target_pairs={{0,4},{4,0},{8,12},{12,8},{16,20},{20,16},{24,28},{28,24},{1,5},{5... | collective-permute-start | bytes 1572872 | tf_op jit(solution)/shard_map/ppermute | solution.py:398
  30.6 23.2 %collective-permute-start.15 = (bf16[2048,128]{1,0:T(8,128)(2,1)S(1)}, bf16[2048,128]{1,0:T(8,128)(2,1)S(1)}, u32[]{:S(2)}, u32[]{:S(2)}) collective-permute-start(bf16[2048,128]{1,0:T(8,128)(2,1)S(1)} %collective-permute-done.14.same_ref), channel_id=1, source_target_pairs={{0,4},{4,0},{8,12},{12,8},{16,20},{20,16},{24,28},{28,24},{1,5},{5... | collective-permute-start | bytes 1572872 | tf_op jit(solution)/shard_map/ppermute | solution.py:398
  31.0 1.6 %collective-permute-start = (f32[32,128]{1,0:T(8,128)S(1)}, f32[32,128]{1,0:T(8,128)S(1)}, u32[]{:S(2)}, u32[]{:S(2)}) collective-permute-start(f32[32,128]{1,0:T(8,128)S(1)} %shard_map.31.own_ref), channel_id=1, source_target_pairs={{0,4},{4,0},{8,12},{12,8},{16,20},{20,16},{24,28},{28,24},{1,5},{5... | collective-permute-start | bytes 49160 | tf_op jit(solution)/shard_map/ppermute | solution.py:398
  32.6 4.0 %collective-permute-start.1 = (f32[16,128]{1,0:T(8,128)S(1)}, f32[16,128]{1,0:T(8,128)S(1)}, u32[]{:S(2)}, u32[]{:S(2)}) collective-permute-start(f32[16,128]{1,0:T(8,128)S(1)} %get-tuple-element.30), channel_id=1, source_target_pairs={{8,0},{12,4},{0,8},{4,12},{24,16},{28,20},{16,24},{20,28},{9,1},{1... | collective-permute-start | bytes 24584 | tf_op jit(solution)/shard_map/ppermute | solution.py:395
  36.6 5.4 %collective-permute-start.2 = (f32[16,128]{1,0:T(8,128)S(1)}, f32[16,128]{1,0:T(8,128)S(1)}, u32[]{:S(2)}, u32[]{:S(2)}) collective-permute-start(f32[16,128]{1,0:T(8,128)S(1)} %get-tuple-element.30), channel_id=1, source_target_pairs={{24,0},{28,4},{16,8},{20,12},{8,16},{12,20},{0,24},{4,28},{25,1},{... | collective-permute-start | bytes 24584 | tf_op jit(solution)/shard_map/ppermute | solution.py:395
  42.0 4.5 %collective-permute-start.3 = (f32[16,128]{1,0:T(8,128)S(1)}, f32[16,128]{1,0:T(8,128)S(1)}, u32[]{:S(2)}, u32[]{:S(2)}) collective-permute-start(f32[16,128]{1,0:T(8,128)S(1)} %get-tuple-element.29.refs_0_), channel_id=1, source_target_pairs={{16,0},{20,4},{24,8},{28,12},{0,16},{4,20},{8,24},{12,28},{17,1},{... | collective-permute-start | bytes 24584 | tf_op jit(solution)/shard_map/ppermute | solution.py:395
  49.5 8.7 %collective-permute-start.10 = (f32[12,32,128]{2,1,0:T(8,128)S(1)}, f32[12,32,128]{2,1,0:T(8,128)S(1)}, u32[]{:S(2)}, u32[]{:S(2)}) collective-permute-start(f32[12,32,128]{2,1,0:T(8,128)S(1)} %get-tuple-element.37), channel_id=1, source_target_pairs={{0,2},{1,3},{2,0},{3,1},{4,6},{5,7},{6,4},{7,5},{8,10},{9,11},{10,... | collective-permute-start | bytes 589832 | tf_op jit(solution)/shard_map/ppermute | solution.py:463
  51.0 11.0 %collective-permute-start.11 = (f32[12,32,128]{2,1,0:T(8,128)S(1)}, f32[12,32,128]{2,1,0:T(8,128)S(1)}, u32[]{:S(2)}, u32[]{:S(2)}) collective-permute-start(f32[12,32,128]{2,1,0:T(8,128)S(1)} %get-tuple-element.38), channel_id=1, source_target_pairs={{0,3},{1,2},{2,1},{3,0},{4,7},{5,6},{6,5},{7,4},{8,11},{9,10},{10,... | collective-permute-start | bytes 589832 | tf_op jit(solution)/shard_map/ppermute | solution.py:463
  52.5 9.6 %collective-permute-start.9 = (f32[12,32,128]{2,1,0:T(8,128)S(1)}, f32[12,32,128]{2,1,0:T(8,128)S(1)}, u32[]{:S(2)}, u32[]{:S(2)}) collective-permute-start(f32[12,32,128]{2,1,0:T(8,128)S(1)} %get-tuple-element.36), channel_id=1, source_target_pairs={{0,1},{1,0},{2,3},{3,2},{4,5},{5,4},{6,7},{7,6},{8,9},{9,8},{10,11... | collective-permute-start | bytes 589832 | tf_op jit(solution)/shard_map/ppermute | solution.py:463
  54.6 9.2 %collective-permute-start.16 = (f32[6,32,128]{2,1,0:T(8,128)S(1)}, f32[6,32,128]{2,1,0:T(8,128)S(1)}, u32[]{:S(2)}, u32[]{:S(2)}) collective-permute-start(f32[6,32,128]{2,1,0:T(8,128)S(1)} %get-tuple-element.44), channel_id=1, source_target_pairs={{0,1},{1,0},{2,3},{3,2},{4,5},{5,4},{6,7},{7,6},{8,9},{9,8},{10,11... | collective-permute-start | bytes 294920 | tf_op jit(solution)/shard_map/ppermute | solution.py:463
  56.1 7.6 %collective-permute-start.17 = (f32[6,32,128]{2,1,0:T(8,128)S(1)}, f32[6,32,128]{2,1,0:T(8,128)S(1)}, u32[]{:S(2)}, u32[]{:S(2)}) collective-permute-start(f32[6,32,128]{2,1,0:T(8,128)S(1)} %get-tuple-element.45), channel_id=1, source_target_pairs={{0,2},{1,3},{2,0},{3,1},{4,6},{5,7},{6,4},{7,5},{8,10},{9,11},{10,... | collective-permute-start | bytes 294920 | tf_op jit(solution)/shard_map/ppermute | solution.py:463
  58.2 6.5 %collective-permute-start.18 = (f32[6,32,128]{2,1,0:T(8,128)S(1)}, f32[6,32,128]{2,1,0:T(8,128)S(1)}, u32[]{:S(2)}, u32[]{:S(2)}) collective-permute-start(f32[6,32,128]{2,1,0:T(8,128)S(1)} %get-tuple-element.46), channel_id=1, source_target_pairs={{0,3},{1,2},{2,1},{3,0},{4,7},{5,6},{6,5},{7,4},{8,11},{9,10},{10,... | collective-permute-start | bytes 294920 | tf_op jit(solution)/shard_map/ppermute | solution.py:463
  62.4 8.8 %collective-permute-start.12 = (f32[40,640]{1,0:T(8,128)S(1)}, f32[40,640]{1,0:T(8,128)S(1)}, u32[]{:S(2)}, u32[]{:S(2)}) collective-permute-start(f32[40,640]{1,0:T(8,128)S(1)} %get-tuple-element.40), channel_id=1, source_target_pairs={{0,8},{4,12},{8,0},{12,4},{16,24},{20,28},{24,16},{28,20},{1,9},{5... | collective-permute-start | bytes 307208 | tf_op jit(solution)/shard_map/ppermute | solution.py:476
  63.1 8.1 %collective-permute-start.13 = (f32[40,640]{1,0:T(8,128)S(1)}, f32[40,640]{1,0:T(8,128)S(1)}, u32[]{:S(2)}, u32[]{:S(2)}) collective-permute-start(f32[40,640]{1,0:T(8,128)S(1)} %get-tuple-element.41), channel_id=1, source_target_pairs={{8,16},{12,20},{16,8},{20,12},{0,0},{4,4},{24,24},{28,28},{9,17},{... | collective-permute-start | bytes 307208 | tf_op jit(solution)/shard_map/ppermute | solution.py:476
  64.7 6.5 %collective-permute-start.19 = (f32[32,512]{1,0:T(8,128)S(1)}, f32[32,512]{1,0:T(8,128)S(1)}, u32[]{:S(2)}, u32[]{:S(2)}) collective-permute-start(f32[32,512]{1,0:T(8,128)S(1)} %get-tuple-element.48), channel_id=1, source_target_pairs={{8,24},{12,28},{16,0},{20,4},{0,8},{4,12},{24,16},{28,20},{9,25},{... | collective-permute-start | bytes 196616 | tf_op jit(solution)/shard_map/ppermute | solution.py:486
  68.4 0.7 collective-permute-start.20
